TPU v7x, 256 devices: a whole 4x4x8 slice. The times are simulated.
256 devices in a mesh: gy: 16 (over z, core), gz: 16 (over y, x).
Axes of the slice: x: 4, y: 4, z: 8, core: 2. Of those that a mesh axis runs over, the one named last changes fastest.
Arguments:
- displacement: float32 [3, 128, 128, 256], P(None, 'gy', 'gz'), may hold values from -0.08 to 0.08
- load: float32 [3, 128, 128, 256], P(None, 'gy', 'gz'), may hold values from -6 to 6
- occupancy: int32 [128, 128, 256], P('gy', 'gz'), may hold values 0 or 1
- voxel_muscle_group: int32 [128, 128, 256], P('gy', 'gz'), may hold values from 0 to 31
- activation: float32 [32], replicated, may hold values from 0.2 to 2
Outputs:
- adjoint: float32 [3, 128, 128, 256], P(None, 'gy', 'gz')
- muscle_grad: float32 [32], replicated
All inputs are finite; a program needn't handle non-finite values. No bound on the sum of `occupancy` on one device may be relied on, other than what follows from the above.
Results may differ from a plain program's by a relative error of at most 0.0003.
Values sent between devices are 32-bit elements; how exact they have to be, the bound alone decides.
No kernel may reach another device: no remote copies, remote signals or barrier semaphores. Data moves between devices by JAX's collectives and lax.ppermute only.
A program may use at most 64 MiB of HBM per device.

v0:
```python
from functools import reduce
import math

import jax
import jax.numpy as jnp
from jax import lax
from jax.sharding import PartitionSpec as P

ITERS = 4


shear_modulus = 1.0
lame_first = 4.0
mass_scale = 0.05


def padded(block, sides, width):
    for axis, dim in sides:
        count = lax.axis_size(axis)
        forward = [(i, i + 1) for i in range(count - 1)]
        backward = [(target, source) for source, target in forward]
        low = lax.ppermute(
            lax.slice_in_dim(block, block.shape[dim] - width, None, axis=dim), axis, forward
        )
        high = lax.ppermute(lax.slice_in_dim(block, 0, width, axis=dim), axis, backward)
        block = jnp.concatenate([low, block, high], axis=dim)
    return block


def shifted(shard, axis, by):
    length = lax.axis_size(axis)
    pairs = [(i, i + by) for i in range(length) if 0 <= i + by < length]
    return lax.ppermute(shard, axis, pairs)


def accumulate_every(summand_terms):
    return reduce(lambda earlier_part, later_part: earlier_part + later_part, summand_terms)


def forward_x(values):
    return jnp.concatenate([values[..., 1:], jnp.zeros_like(values[..., :1])], axis=-1)


def backward_x(values):
    return jnp.concatenate([jnp.zeros_like(values[..., :1]), values[..., :-1]], axis=-1)


def element_gradient(extended):
    leading = forward_x(extended)
    paired = extended + leading
    slopes = leading - extended
    summed_z = paired[:, :, :-1] + paired[:, :, 1:]
    differ_z = paired[:, :, 1:] - paired[:, :, :-1]
    slopes_z = slopes[:, :, :-1] + slopes[:, :, 1:]
    grad_x = 0.25 * (slopes_z[:, :-1] + slopes_z[:, 1:])
    grad_y = 0.25 * (summed_z[:, 1:] - summed_z[:, :-1])
    grad_z = 0.25 * (differ_z[:, :-1] + differ_z[:, 1:])
    return [
        [grad_x[comp_idx], grad_y[comp_idx], grad_z[comp_idx]]
        for comp_idx in range(extended.shape[0])
    ]


def element_terms(state_ext):
    deform = element_gradient(state_ext[:3])
    deform = [
        [
            deform[row_index][col_idx] + (1.0 if row_index == col_idx else 0.0)
            for col_idx in range(3)
        ]
        for row_index in range(3)
    ]
    cofactor = [
        [
            deform[(row_index + 1) % 3][(col_idx + 1) % 3]
            * deform[(row_index + 2) % 3][(col_idx + 2) % 3]
            - deform[(row_index + 1) % 3][(col_idx + 2) % 3]
            * deform[(row_index + 2) % 3][(col_idx + 1) % 3]
            for col_idx in range(3)
        ]
        for row_index in range(3)
    ]
    volume_ratio = accumulate_every(
        [deform[0][col_idx] * cofactor[0][col_idx] for col_idx in range(3)]
    )
    inverse_t = [
        [cofactor[row_index][col_idx] / volume_ratio for col_idx in range(3)]
        for row_index in range(3)
    ]
    shear_term = shear_modulus - lame_first * jnp.log(volume_ratio)
    occupied = state_ext[3, :-1, :-1]
    muscle_act = state_ext[4, :-1, :-1]
    fiber = [deform[row_index][0] for row_index in range(3)]
    return (inverse_t, shear_term, occupied, muscle_act, fiber)


def stress_rate(grad_field, terms):
    inverse_t, shear_term, occupied, muscle_act, fiber = terms
    trace_term = accumulate_every(
        [
            inverse_t[row_index][col_idx] * grad_field[row_index][col_idx]
            for row_index in range(3)
            for col_idx in range(3)
        ]
    )
    mixed = [
        [
            accumulate_every(
                [
                    grad_field[inner_idx][mid_idx] * inverse_t[inner_idx][col_idx]
                    for inner_idx in range(3)
                ]
            )
            for col_idx in range(3)
        ]
        for mid_idx in range(3)
    ]
    rotated = [
        [
            accumulate_every(
                [inverse_t[row_index][mid_idx] * mixed[mid_idx][col_idx] for mid_idx in range(3)]
            )
            for col_idx in range(3)
        ]
        for row_index in range(3)
    ]
    scaled = 0.25 * occupied
    result = []
    for row_index in range(3):
        line = []
        for col_idx in range(3):
            value = (
                shear_modulus * grad_field[row_index][col_idx]
                + shear_term * rotated[row_index][col_idx]
                + lame_first * trace_term * inverse_t[row_index][col_idx]
            )
            if col_idx == 0:
                value = value + muscle_act * grad_field[row_index][0]
            line.append(scaled * value)
        result.append(line)
    return result


def node_forces(rate):
    forces = []
    for row_index in range(3):
        along_x = backward_x(rate[row_index][0]) - rate[row_index][0]
        across_y = rate[row_index][1] + backward_x(rate[row_index][1])
        across_z = rate[row_index][2] + backward_x(rate[row_index][2])
        combined = along_x[:, :-1] + along_x[:, 1:] + (across_z[:, :-1] - across_z[:, 1:])
        stacked_y = across_y[:, :-1] + across_y[:, 1:]
        forces.append(combined[:-1] + combined[1:] + (stacked_y[:-1] - stacked_y[1:]))
    return jnp.stack(forces)


def muscle_sums(extended, terms, muscle_ids, levels):
    grad_field = element_gradient(extended)
    fiber = terms[4]
    occupied = terms[2]
    work = (
        accumulate_every(
            [fiber[row_index][1:, 1:] * grad_field[row_index][0][1:, 1:] for row_index in range(3)]
        )
        * occupied[1:, 1:]
    )
    return jnp.sum(
        jnp.where(
            muscle_ids[None] == levels[:, None, None, None], work[None], jnp.zeros((), work.dtype)
        ),
        axis=(1, 2, 3),
    )


def squares(residual):
    return lax.psum(jnp.sum(residual * residual), ("gy", "gz"))


def per_device(displacement, load, occupancy, voxel_muscle_group, activation):
    rows_local, cols_local, depth = occupancy.shape
    muscles = activation.shape[0]
    levels = jnp.arange(muscles, dtype=jnp.int32)
    muscle_act = jnp.sum(
        jnp.where(
            voxel_muscle_group[None] == levels[:, None, None, None],
            activation[:, None, None, None],
            0.0,
        ),
        axis=0,
    )
    state = jnp.concatenate(
        [displacement, occupancy.astype(jnp.float32)[None], muscle_act[None]], axis=0
    )
    state_ext = padded(state, (("gy", 1), ("gz", 2)), 1)

    def current_terms():
        return element_terms(state_ext)

    solution = jnp.zeros_like(load)
    residual = load
    direction = load
    norm_now = squares(residual)
    for step in range(ITERS):
        extended = padded(direction, (("gy", 1), ("gz", 2)), 1)
        image = mass_scale * direction + node_forces(
            stress_rate(element_gradient(extended), current_terms())
        )
        alpha = norm_now / lax.psum(jnp.sum(direction * image), ("gy", "gz"))
        solution = solution + alpha * direction
        residual = residual - alpha * image
        norm_next = squares(residual)
        direction = residual + norm_next / norm_now * direction
        norm_now = norm_next
    upper_row = shifted(solution[:, :1], "gy", -1)
    with_rows = jnp.concatenate([solution, upper_row], axis=1)
    upper_col = shifted(with_rows[:, :, :1], "gz", -1)
    with_both = jnp.concatenate([with_rows, upper_col], axis=2)
    adjoint_extended = jnp.pad(with_both, ((0, 0), (1, 0), (1, 0), (0, 0)))
    local_sums = muscle_sums(adjoint_extended, current_terms(), voxel_muscle_group, levels)
    total = lax.psum(local_sums, ("gy", "gz"))
    cells = depth * rows_local * lax.axis_size("gy") * cols_local * lax.axis_size("gz")
    muscle_grad = -(1.0 / math.sqrt(cells / muscles)) * total
    return (solution, muscle_grad)


def solution(mesh):
    placed = (
        P(None, "gy", "gz", None),
        P(None, "gy", "gz", None),
        P("gy", "gz", None),
        P("gy", "gz", None),
        P(),
    )
    return jax.shard_map(
        per_device,
        mesh=mesh,
        in_specs=placed,
        out_specs=(P(None, "gy", "gz", None), P()),
        check_vma=False,
    )
```

profile of v0, /device:TPU:1, one launch (start us, length us, event | category | flops | bytes accessed | tf_op | source)
XLA Modules:
  0.0 735.0 jit_solution(15938066868100303784)
XLA Ops:
  1.5 4.9 collective-permute-start.3
  15.5 3.2 collective-permute-done.4
  18.7 3.1 collective-permute-start.5
  23.2 4.0 collective-permute-start.2
  36.7 83.7 %all-reduce.43 = (f32[]{:T(128)}, f32[]{:T(128)}) all-reduce(f32[]{:T(128)} %get-tuple-element.3, f32[]{:T(128)} %get-tuple-element.2), channel_id=1, replica_groups=mesh['gy'=16,'gz'=16] {'gy','gz'}, use_global_device_ids=true, to_apply=%region_1.2 | all-reduce | flops 2 | bytes 16 | tf_op jit(solution)/shard_map/psum | solution.py:175
  122.4 72.8 %psum.65 = f32[]{:T(128)} all-reduce(f32[]{:T(128)} %multiply_reduce_fusion.4), channel_id=1, replica_groups=mesh['gy'=16,'gz'=16] {'gy','gz'}, use_global_device_ids=true, to_apply=%region_6.7 | all-reduce | flops 1 | bytes 8 | tf_op jit(solution)/shard_map/psum | solution.py:175
  196.6 4.2 collective-permute-start.8
  202.8 3.2 collective-permute-done.9
  210.2 3.3 collective-permute-done.11
  218.0 76.7 %psum.66 = f32[]{:T(128)} all-reduce(f32[]{:T(128)} %multiply_reduce_fusion.3), channel_id=1, replica_groups=mesh['gy'=16,'gz'=16] {'gy','gz'}, use_global_device_ids=true, to_apply=%region_8.9 | all-reduce | flops 1 | bytes 8 | tf_op jit(solution)/shard_map/psum | solution.py:207
  296.7 73.6 %psum.67 = f32[]{:T(128)} all-reduce(f32[]{:T(128)} %get-tuple-element.26), channel_id=1, replica_groups=mesh['gy'=16,'gz'=16] {'gy','gz'}, use_global_device_ids=true, to_apply=%region_10.11 | all-reduce | flops 1 | bytes 8 | tf_op jit(solution)/shard_map/psum | solution.py:175
  371.8 4.1 collective-permute-start.12
  377.8 3.2 collective-permute-done.13
  381.1 3.0 collective-permute-start.14
  385.4 3.3 collective-permute-done.15
  393.2 76.7 %psum.68 = f32[]{:T(128)} all-reduce(f32[]{:T(128)} %multiply_reduce_fusion.1), channel_id=1, replica_groups=mesh['gy'=16,'gz'=16] {'gy','gz'}, use_global_device_ids=true, to_apply=%region_12.13 | all-reduce | flops 1 | bytes 8 | tf_op jit(solution)/shard_map/psum | solution.py:207
  471.9 73.4 %psum.69 = f32[]{:T(128)} all-reduce(f32[]{:T(128)} %multiply_reduce_fusion), channel_id=1, replica_groups=mesh['gy'=16,'gz'=16] {'gy','gz'}, use_global_device_ids=true, to_apply=%region_14.15 | all-reduce | flops 1 | bytes 8 | tf_op jit(solution)/shard_map/psum | solution.py:175
  546.8 4.1 collective-permute-start.16
  552.8 3.2 collective-permute-done.17
  556.1 3.0 collective-permute-start.18
  560.4 3.3 collective-permute-done.19
  568.2 76.6 %psum.70 = f32[]{:T(128)} all-reduce(f32[]{:T(128)} %fusion.17), channel_id=1, replica_groups=mesh['gy'=16,'gz'=16] {'gy','gz'}, use_global_device_ids=true, to_apply=%region_16.17 | all-reduce | flops 1 | bytes 8 | tf_op jit(solution)/shard_map/psum | solution.py:207
  652.8 3.3 collective-permute-done.21
  657.8 76.7 %psum.71 = f32[32]{0:T(128)S(1)} all-reduce(f32[32]{0:T(128)S(1)} %select_reduce_fusion), channel_id=1, replica_groups=mesh['gy'=16,'gz'=16] {'gy','gz'}, use_global_device_ids=true, to_apply=%region_18.19 | all-reduce | flops 32 | bytes 256 | tf_op jit(solution)/shard_map/psum | solution.py:219
  (209 shorter events, 56.9 us)
Async XLA Ops:
  0.6 14.8 %copy-start = (f32[3,8,8,256]{3,2,1,0:T(8,128)S(1)}, f32[3,8,8,256]{3,2,1,0:T(8,128)}, u32[]{:S(2)}) copy-start(f32[3,8,8,256]{3,2,1,0:T(8,128)} %param.6) | copy-start | bytes 589828
  0.6 22.5 %copy-start.2 = (f32[3,8,8,256]{3,2,1,0:T(8,128)S(1)}, f32[3,8,8,256]{3,2,1,0:T(8,128)}, u32[]{:S(2)}) copy-start(f32[3,8,8,256]{3,2,1,0:T(8,128)} %param.5) | copy-start | bytes 589828
  1.5 13.9 %collective-permute-start.3 = (f32[3,1,8,256]{3,2,1,0:T(8,128)S(1)}, f32[3,1,8,256]{3,2,1,0:T(8,128)S(1)}, u32[]{:S(2)}, u32[]{:S(2)}) collective-permute-start(f32[3,1,8,256]{3,2,1,0:T(8,128)S(1)} %get-tuple-element.132), channel_id=1, source_target_pairs={{0,16},{16,32},{32,48},{48,64},{64,80},{80,96},{96,112},{112,128},... | collective-permute-start | bytes 73736 | tf_op jit(solution)/shard_map/ppermute | solution.py:22
  9.1 13.9 %collective-permute-start = (f32[5,1,8,256]{3,2,1,0:T(8,128)S(1)}, f32[5,1,8,256]{3,2,1,0:T(8,128)S(1)}, u32[]{:S(2)}, u32[]{:S(2)}) collective-permute-start(f32[5,1,8,256]{3,2,1,0:T(8,128)S(1)} %get-tuple-element.115), channel_id=1, source_target_pairs={{0,16},{16,32},{32,48},{48,64},{64,80},{80,96},{96,112},{112,128},... | collective-permute-start | bytes 122888 | tf_op jit(solution)/shard_map/ppermute | solution.py:22
  11.1 12.0 %collective-permute-start.1 = (f32[5,1,8,256]{3,2,1,0:T(8,128)S(1)}, f32[5,1,8,256]{3,2,1,0:T(8,128)S(1)}, u32[]{:S(2)}, u32[]{:S(2)}) collective-permute-start(f32[5,1,8,256]{3,2,1,0:T(8,128)S(1)} %get-tuple-element.116), channel_id=1, source_target_pairs={{16,0},{32,16},{48,32},{64,48},{80,64},{96,80},{112,96},{128,112},... | collective-permute-start | bytes 122888 | tf_op jit(solution)/shard_map/ppermute | solution.py:25
  13.5 5.1 collective-permute-start.4
  18.7 9.8 %collective-permute-start.5 = (f32[3,10,1,256]{3,2,1,0:T(1,128)S(1)}, f32[3,10,1,256]{3,2,1,0:T(1,128)S(1)}, u32[]{:S(2)}, u32[]{:S(2)}) collective-permute-start(f32[3,10,1,256]{3,2,1,0:T(1,128)S(1)} %get-tuple-element.123), channel_id=1, source_target_pairs={{0,1},{1,2},{2,3},{3,4},{4,5},{5,6},{6,7},{7,8},{8,9},{9,10},{10,1... | collective-permute-start | bytes 92168 | tf_op jit(solution)/shard_map/ppermute | solution.py:22
  21.8 6.7 collective-permute-start.6
  23.2 6.2 collective-permute-start.2
  27.2 4.9 collective-permute-start.7
  196.6 6.2 collective-permute-start.8
  200.9 5.1 collective-permute-start.9
  206.1 4.1 collective-permute-start.10
  208.9 4.6 collective-permute-start.11
  371.8 6.1 collective-permute-start.12
  375.9 5.1 collective-permute-start.13
  381.1 4.3 collective-permute-start.14
  384.1 4.6 collective-permute-start.15
  546.8 6.1 collective-permute-start.16
  550.9 5.1 collective-permute-start.17
  556.1 4.3 collective-permute-start.18
  559.1 4.6 collective-permute-start.19
  646.3 5.1 collective-permute-start.20
  651.5 4.6 collective-permute-start.21
  (2 other events, 10.9 us)
where the time goes:
time: 737 us; the launch traced here: 735 us
  blocking collectives  610 us (83%)
  starting transfers between devices  55.7 us (8%)
  waiting for transfers between devices  31.3 us (4%)
  other arithmetic  23.7 us (3%)
  between operations  11.3 us (2%)
    psum x4, blocking collectives, squares(): return lax.psum(jnp.sum(residual * residual), ('gy', 'gz'))  304 us
    psum x3, blocking collectives, per_device(): alpha = norm_now / lax.psum(jnp.sum(direction * image), ('gy', 'gz'))  230 us
    psum x1, blocking collectives, per_device(): total = lax.psum(local_sums, ('gy', 'gz'))  76.7 us
    ppermute x10, starting transfers between devices, padded(): lax.ppermute(lax.slice_in_dim(block, block.shape[dim] - width, None, axis...  35.3 us
    ppermute x10, waiting for transfers between devices, padded(): lax.ppermute(lax.slice_in_dim(block, 0, width, axis=dim), axis, backward)  25.4 us
    ppermute x10, starting transfers between devices, padded(): lax.ppermute(lax.slice_in_dim(block, 0, width, axis=dim), axis, backward)  16.5 us
  transfers between devices with their start and end apart: 22, of which 10 were waited for; matrix products, arithmetic and copies ran while one was open for 1% of the time, Pallas kernels for 0%

commit v1 on v0

v1 whole, which is shorter than its diff:
```python
import functools
import math

import jax
import jax.numpy as jnp
from jax import lax
from jax.experimental import pallas as pl
from jax.experimental.pallas import tpu as pltpu
from jax.sharding import PartitionSpec as P

SHEAR = 1.0
LAME = 4.0
MASS = 0.05

LOW, HIGH = 3, 4
SIGMA = 16.0
SHIFTS = (0.0, 9.95, 1.95)
NB = 4
LANES = 128
SUB = 8
TERMS = 15
QUADS = tuple((zt, h) for zt in range(2) for h in range(2))


class Tile:
    def __init__(self):
        self.lane = lax.broadcasted_iota(jnp.int32, (SUB, LANES), 1)
        self.sub = lax.broadcasted_iota(jnp.int32, (SUB, LANES), 0)
        self.last_lane = self.lane == LANES - 1
        self.first_lane = self.lane == 0
        self.last_sub = self.sub == SUB - 1
        self.first_sub = self.sub == 0

    def xup(self, v):
        out = {}
        for zt in range(2):
            r0 = pltpu.roll(v[zt, 0], LANES - 1, 1)
            r1 = pltpu.roll(v[zt, 1], LANES - 1, 1)
            out[zt, 0] = jnp.where(self.last_lane, r1, r0)
            out[zt, 1] = jnp.where(self.last_lane, 0.0, r1)
        return out

    def xdown(self, v):
        out = {}
        for zt in range(2):
            r0 = pltpu.roll(v[zt, 0], 1, 1)
            r1 = pltpu.roll(v[zt, 1], 1, 1)
            out[zt, 0] = jnp.where(self.first_lane, 0.0, r0)
            out[zt, 1] = jnp.where(self.first_lane, r0, r1)
        return out

    def zup(self, v):
        out = {}
        for h in range(2):
            r0 = pltpu.roll(v[0, h], SUB - 1, 0)
            r1 = pltpu.roll(v[1, h], SUB - 1, 0)
            out[0, h] = jnp.where(self.last_sub, r1, r0)
            out[1, h] = r1
        return out

    def zdown(self, v):
        out = {}
        for h in range(2):
            r0 = pltpu.roll(v[0, h], 1, 0)
            r1 = pltpu.roll(v[1, h], 1, 0)
            out[0, h] = r0
            out[1, h] = jnp.where(self.first_sub, r0, r1)
        return out

    def own(self, v):
        out = []
        for h in range(2):
            r0 = pltpu.roll(v[0, h], SUB - LOW, 0)
            r1 = pltpu.roll(v[1, h], SUB - LOW, 0)
            out.append(jnp.where(self.sub < SUB - LOW, r0, r1))
        return out


def get(ref, *index):
    return {
        (zt, h): ref[(*index, pl.ds(SUB * zt, SUB), pl.ds(LANES * h, LANES))] for zt, h in QUADS
    }


def put(ref, value, *index):
    for zt, h in QUADS:
        ref[(*index, pl.ds(SUB * zt, SUB), pl.ds(LANES * h, LANES))] = value[zt, h]


def add(a, b):
    return {k: a[k] + b[k] for k in QUADS}


def sub(a, b):
    return {k: a[k] - b[k] for k in QUADS}


def raw_gradient(tile, ref, lead, q):
    result = []
    for comp in range(3):
        here = get(ref, *lead, comp, q)
        above = get(ref, *lead, comp, q + 1)
        both, step = add(here, above), sub(above, here)
        both_x, step_x = tile.xup(both), tile.xup(step)
        wide, slope, rise = add(both, both_x), sub(both_x, both), add(step, step_x)
        result.append(
            (
                add(slope, tile.zup(slope)),
                add(rise, tile.zup(rise)),
                sub(tile.zup(wide), wide),
            )
        )
    return result


def row_terms(tile, ext, terms, q):
    grad = raw_gradient(tile, ext, (), q)
    occ, level = get(ext, 6, q), get(ext, 7, q)
    for k in QUADS:
        deform = [
            [0.25 * grad[r][c][k] + (1.0 if r == c else 0.0) for c in range(3)] for r in range(3)
        ]
        cof = [
            [
                deform[(r + 1) % 3][(c + 1) % 3] * deform[(r + 2) % 3][(c + 2) % 3]
                - deform[(r + 1) % 3][(c + 2) % 3] * deform[(r + 2) % 3][(c + 1) % 3]
                for c in range(3)
            ]
            for r in range(3)
        ]
        volume = deform[0][0] * cof[0][0] + deform[0][1] * cof[0][1] + deform[0][2] * cof[0][2]
        inverse = 1.0 / volume
        scaled = occ[k] * (1.0 / (16.0 * SIGMA))
        values = [cof[r][c] * inverse for r in range(3) for c in range(3)]
        values.append(scaled * (SHEAR - LAME * jnp.log(volume)))
        values.append(scaled)
        values.append(scaled * (SHEAR + level[k]))
        quarter = 0.25 * occ[k]
        values += [quarter * deform[r][0] for r in range(3)]
        zt, h = k
        for i, value in enumerate(values):
            terms[i, q, pl.ds(SUB * zt, SUB), pl.ds(LANES * h, LANES)] = value


def row_rate(grad, terms, works, step, q, need_work=True):
    rate = [[{} for _ in range(3)] for _ in range(3)]
    for k in QUADS:
        zt, h = k

        def term(i):
            return terms[i, q, pl.ds(SUB * zt, SUB), pl.ds(LANES * h, LANES)]

        g = [[grad[r][c][k] for c in range(3)] for r in range(3)]
        inv_t = [[term(3 * r + c) for c in range(3)] for r in range(3)]
        shear, occ, fibre = term(9), term(10), term(11)
        pulled = [
            [
                inv_t[0][a] * g[0][b] + inv_t[1][a] * g[1][b] + inv_t[2][a] * g[2][b]
                for b in range(3)
            ]
            for a in range(3)
        ]
        spread = (LAME * occ) * (pulled[0][0] + pulled[1][1] + pulled[2][2])
        z = [
            [shear * pulled[c][m] + (spread if c == m else 0.0) for c in range(3)]
            for m in range(3)
        ]
        for r in range(3):
            for c in range(3):
                rate[r][c][k] = (
                    (fibre if c == 0 else occ) * g[r][c]
                    + inv_t[r][0] * z[0][c]
                    + inv_t[r][1] * z[1][c]
                    + inv_t[r][2] * z[2][c]
                )
        if need_work:
            works[step, q, pl.ds(SUB * zt, SUB), pl.ds(LANES * h, LANES)] = (
                term(12) * g[0][0] + term(13) * g[1][0] + term(14) * g[2][0]
            )
    return rate


def row_force(tile, before, rate, comp):
    p = {k: before[comp, 0][k] + rate[comp][0][k] for k in QUADS}
    a = {k: before[comp, 1][k] - rate[comp][1][k] for k in QUADS}
    b = {k: before[comp, 2][k] + rate[comp][2][k] for k in QUADS}
    along = add(p, tile.zdown(p))
    across = add(tile.zdown(add(a, b)), sub(a, b))
    return add(tile.xdown(add(along, across)), sub(across, along))


def krylov_kernel(
    axes, e_ref, ylo_ref, yhi_ref, load_ref, group_ref, sums_ref, basis_ref, ext, fields, terms, last, works, table
):
    rows = load_ref.shape[1]
    tile = Tile()
    top_y = jnp.where(lax.axis_index(axes[0]) == lax.axis_size(axes[0]) - 1, LOW + rows, -1)
    top_z = jnp.where(lax.axis_index(axes[1]) == lax.axis_size(axes[1]) - 1, LOW + rows, -1)
    keep_z = {
        (zt, h): jnp.where(tile.sub + SUB * zt == top_z, 0.0, 1.0) for zt, h in QUADS
    }
    count = LOW + rows + HIGH
    blank = jnp.zeros((SUB, ext.shape[-1]), jnp.float32)

    def assemble(c, carry):
        for q in range(count):
            ext[c, q, pl.ds(SUB, SUB), :] = blank
            if q < LOW:
                ext[c, q, pl.ds(0, count), :] = ylo_ref[c, q]
            elif q < LOW + rows:
                ext[c, q, pl.ds(0, count), :] = e_ref[c, q - LOW]
            else:
                ext[c, q, pl.ds(0, count), :] = yhi_ref[c, q - LOW - rows]
        return carry

    lax.fori_loop(0, ext.shape[0], assemble, 0)

    def remember(rate):
        for r in range(3):
            for c in range(3):
                put(last, rate[r][c], 3 * r + c)

    for step in range(3):
        source, lead = (ext, ()) if step == 0 else (fields, (step - 1,))
        base = 3 if step == 0 else 0

        class View:
            pass

        def grad_of(q, source=source, lead=lead, base=base):
            result = []
            for comp in range(3):
                here = get(source, *lead, base + comp, q)
                above = get(source, *lead, base + comp, q + 1)
                both, rise0 = add(here, above), sub(above, here)
                both_x, rise_x = tile.xup(both), tile.xup(rise0)
                wide, slope, rise = add(both, both_x), sub(both_x, both), add(rise0, rise_x)
                result.append(
                    (
                        add(slope, tile.zup(slope)),
                        add(rise, tile.zup(rise)),
                        sub(tile.zup(wide), wide),
                    )
                )
            return result

        def rate_of(q, step=step, grad_of=grad_of):
            if step == 0:
                row_terms(tile, ext, terms, q)
            return row_rate(grad_of(q), terms, works, step, q)

        def body(q, carry, step=step, rate_of=rate_of, source=source, lead=lead, base=base):
            rate = rate_of(q)
            before = {(r, c): get(last, 3 * r + c) for r in range(3) for c in range(3)}
            keep_y = jnp.where(q == top_y, 0.0, 1.0)
            for comp in range(3):
                force = row_force(tile, before, rate, comp)
                if SHIFTS[step] != 0.0:
                    here = get(source, *lead, base + comp, q)
                    force = {k: force[k] - (SHIFTS[step] / SIGMA) * here[k] for k in QUADS}
                force = {k: force[k] * (keep_z[k] * keep_y) for k in QUADS}
                put(fields, force, step, comp, q)
            remember(rate)
            return carry

        remember(rate_of(step))
        lax.fori_loop(step + 1, count - 1 - step, body, 0)

    inside = {
        (zt, h): (tile.sub + SUB * zt >= LOW) & (tile.sub + SUB * zt < LOW + rows)
        for zt, h in QUADS
    }
    zero = jnp.zeros((SUB, LANES), jnp.float32)
    pairs = [(i, j) for i in range(NB) for j in range(i, NB)]

    def finish(y, acc):
        acc = list(acc)
        q = y + LOW
        grad = []
        for comp in range(3):
            here = get(fields, 2, comp, q)
            above = get(fields, 2, comp, q + 1)
            both, rise0 = add(here, above), sub(above, here)
            both_x, rise_x = tile.xup(both), tile.xup(rise0)
            wide, slope, rise = add(both, both_x), sub(both_x, both), add(rise0, rise_x)
            grad.append(
                (
                    add(slope, tile.zup(slope)),
                    add(rise, tile.zup(rise)),
                    sub(tile.zup(wide), wide),
                )
            )
        rate = row_rate(grad, terms, works, 3, q)
        for k in QUADS:
            energy = zero
            for r in range(3):
                for c in range(3):
                    energy = energy + rate[r][c][k] * grad[r][c][k]
            acc[-1] = acc[-1] + jnp.where(inside[k], energy, 0.0)
        for comp in range(3):
            vectors = [[load_ref[comp, y, :, pl.ds(LANES * h, LANES)] for h in range(2)]]
            for step in range(3):
                value = tile.own(get(fields, step, comp, q))
                for h in range(2):
                    basis_ref[step, comp, y, :, pl.ds(LANES * h, LANES)] = value[h]
                vectors.append(value)
            for n, (i, j) in enumerate(pairs):
                acc[n] = acc[n] + (
                    vectors[i][0] * vectors[j][0] + vectors[i][1] * vectors[j][1]
                )
        return tuple(acc)

    acc = lax.fori_loop(0, rows, finish, tuple(zero for _ in range(len(pairs) + 1)))
    table[...] = jnp.zeros_like(table)
    muscles = (table.shape[0] // 2) // NB
    for n, value in enumerate(acc):
        table[pl.ds(NB * muscles + n, 1), :] = jnp.sum(value, axis=0, keepdims=True)

    def compact(y, carry):
        for step in range(NB):
            value = tile.own(get(works, step, y + LOW))
            for h in range(2):
                works[step, y, pl.ds(0, SUB), pl.ds(LANES * h, LANES)] = value[h]
        return carry

    lax.fori_loop(0, rows, compact, 0)

    def muscle(m, carry):
        total = [zero] * NB
        for y in range(rows):
            for h in range(2):
                mine = group_ref[y, :, pl.ds(LANES * h, LANES)] == m
                for step in range(NB):
                    total[step] = total[step] + jnp.where(
                        mine, works[step, y, pl.ds(0, SUB), pl.ds(LANES * h, LANES)], 0.0
                    )
        for step in range(NB):
            table[pl.ds(step * muscles + m, 1), :] = jnp.sum(total[step], axis=0, keepdims=True)
        return carry

    lax.fori_loop(0, muscles, muscle, 0)
    row = lax.dot_general(
        jnp.ones((SUB, LANES), jnp.float32),
        table[...],
        (((1,), (1,)), ((), ())),
        precision=lax.Precision.HIGHEST,
        preferred_element_type=jnp.float32,
    )
    for i in range(sums_ref.shape[0] // SUB):
        sums_ref[pl.ds(SUB * i, SUB), :] = row


def combine_kernel(muscles, scale, sums_ref, load_ref, basis_ref, x_ref, grad_ref):
    total = jnp.sum(sums_ref[...], axis=0, keepdims=True)
    at = NB * muscles
    pairs = [(i, j) for i in range(NB) for j in range(i, NB)]
    gram = {}
    for n, (i, j) in enumerate(pairs):
        gram[i, j] = gram[j, i] = total[:, at + n : at + n + 1]
    energy = total[:, at + len(pairs) : at + len(pairs) + 1]
    shifts = [MASS + s for s in SHIFTS]
    form = {}
    for j in range(NB - 1):
        for i in range(j + 1):
            form[i, j] = form[j, i] = SIGMA * gram[i, j + 1] + shifts[j] * gram[i, j]
    last = NB - 1
    for i in range(last):
        form[i, last] = form[last, i] = SIGMA * gram[i + 1, last] + shifts[i] * gram[i, last]
    form[last, last] = SIGMA * energy + MASS * gram[last, last]

    def quadratic(matrix, v):
        parts = []
        for i in range(NB):
            if v[i] is None:
                continue
            inner = [matrix[i, j] * v[j] for j in range(NB) if v[j] is not None]
            parts.append(v[i] * functools.reduce(lambda s, t: s + t, inner))
        return functools.reduce(lambda s, t: s + t, parts)

    one = jnp.ones((1, 1), jnp.float32)
    x = [None] * NB
    residual = [one] + [None] * (NB - 1)
    direction = list(residual)
    norm = gram[0, 0]

    def axpy(a, u, v):
        out = []
        for s, t in zip(u, v):
            if s is None:
                out.append(t)
            elif t is None:
                out.append(a * s)
            else:
                out.append(t + a * s)
        return out

    for step in range(NB):
        alpha = norm / quadratic(form, direction)
        x = axpy(alpha, direction, x)
        if step == NB - 1:
            break
        image = [None] * NB
        for i in range(NB - 1):
            if direction[i] is not None:
                up = SIGMA * direction[i]
                same = shifts[i] * direction[i]
                image[i] = same if image[i] is None else image[i] + same
                image[i + 1] = up if image[i + 1] is None else image[i + 1] + up
        residual = axpy(-alpha, image, residual)
        new = quadratic(gram, residual)
        direction = axpy(new / norm, direction, residual)
        norm = new

    grad = None
    for k in range(NB):
        part = x[k] * total[:, k * muscles : (k + 1) * muscles]
        grad = part if grad is None else grad + part
    grad_ref[...] = -scale * grad

    width = load_ref.shape[-1]
    coef = [jnp.broadcast_to(x[k], (SUB, width)) for k in range(NB)]

    def row(y, carry):
        for comp in range(3):
            value = coef[0] * load_ref[comp, y]
            for k in range(1, NB):
                value = value + coef[k] * basis_ref[k - 1, comp, y]
            x_ref[comp, y] = value
        return carry

    lax.fori_loop(0, load_ref.shape[1], row, 0)


def shift(shard, axis, by):
    length = lax.axis_size(axis)
    return lax.ppermute(
        shard, axis, [(i, i + by) for i in range(length) if 0 <= i + by < length]
    )


def per_device(displacement, load, occupancy, voxel_muscle_group, activation):
    rows, cols, depth = occupancy.shape
    muscles = activation.shape[0]
    levels = jnp.arange(muscles, dtype=jnp.int32)
    level = jnp.sum(
        jnp.where(
            voxel_muscle_group[None] == levels[:, None, None, None],
            activation[:, None, None, None],
            0.0,
        ),
        axis=0,
    )
    block = jnp.concatenate(
        [displacement, load, occupancy.astype(jnp.float32)[None], level[None]], axis=0
    )
    zlo = shift(block[:, :, cols - LOW :], "gz", 1)
    zhi = shift(block[:, :, :HIGH], "gz", -1)
    e = jnp.concatenate([zlo, block, zhi], axis=2)
    ylo = shift(e[:, rows - LOW :], "gy", 1)
    yhi = shift(e[:, :HIGH], "gy", -1)

    devices = lax.axis_size("gy") * lax.axis_size("gz")
    count = LOW + rows + HIGH
    vmem = pl.BlockSpec(memory_space=pltpu.VMEM)
    sums, basis = pl.pallas_call(
        functools.partial(krylov_kernel, ("gy", "gz")),
        out_shape=(
            jax.ShapeDtypeStruct((devices, 2 * NB * muscles), jnp.float32),
            jax.ShapeDtypeStruct((NB - 1, 3, rows, cols, depth), jnp.float32),
        ),
        in_specs=[vmem] * 5,
        out_specs=(vmem, vmem),
        scratch_shapes=[
            pltpu.VMEM((8, count, 2 * SUB, depth), jnp.float32),
            pltpu.VMEM((NB - 1, 3, count, 2 * SUB, depth), jnp.float32),
            pltpu.VMEM((TERMS, count - 1, 2 * SUB, depth), jnp.float32),
            pltpu.VMEM((9, 2 * SUB, depth), jnp.float32),
            pltpu.VMEM((NB, count - 1, 2 * SUB, depth), jnp.float32),
            pltpu.VMEM((2 * NB * muscles, LANES), jnp.float32),
        ],
        compiler_params=pltpu.CompilerParams(vmem_limit_bytes=48 << 20),
        name="krylov",
    )(e, ylo, yhi, load, voxel_muscle_group)

    every = lax.all_to_all(sums, ("gy", "gz"), 0, 0, tiled=True)

    cells = depth * rows * lax.axis_size("gy") * cols * lax.axis_size("gz")
    scale = 1.0 / math.sqrt(cells / muscles)
    adjoint, muscle_grad = pl.pallas_call(
        functools.partial(combine_kernel, muscles, scale),
        out_shape=(
            jax.ShapeDtypeStruct(load.shape, jnp.float32),
            jax.ShapeDtypeStruct((1, muscles), jnp.float32),
        ),
        in_specs=[vmem] * 3,
        out_specs=(vmem, vmem),
        compiler_params=pltpu.CompilerParams(vmem_limit_bytes=32 << 20),
        name="combine",
    )(every, load, basis)
    return adjoint, muscle_grad.reshape(muscles)


def solution(mesh):
    placed = (
        P(None, "gy", "gz", None),
        P(None, "gy", "gz", None),
        P("gy", "gz", None),
        P("gy", "gz", None),
        P(),
    )
    return jax.shard_map(
        per_device,
        mesh=mesh,
        in_specs=placed,
        out_specs=(P(None, "gy", "gz", None), P()),
        check_vma=False,
    )
```

time: 737 us -> 77.9 us (0.11)
  blocking collectives: 610 us -> 34.6 us
  starting transfers between devices: 55.7 us -> 14.7 us
  waiting for transfers between devices: 31.3 us -> 8.17 us
  other arithmetic: 23.7 us -> 3.28 us
  Pallas kernels: 0 us -> 15.7 us
  between operations: 11.3 us -> 0.76 us
    psum x8 -> x0, blocking collectives: 610 us -> none  [the longest x4 304 us: squares(): return lax.psum(jnp.sum(residual * residual), ('gy', 'gz'))]
    ppermute x22 -> x4, starting transfers between devices: 55.7 us -> 14.7 us  [shift(): lax.ppermute(shard, axis, [(i, i + by) for i in range(length) if 0 <= i +...]
    all_to_all x0 -> x1, blocking collectives: none -> 34.6 us  [per_device(): every = lax.all_to_all(sums, ('gy', 'gz'), 0, 0, tiled=True)]
    ppermute x22 -> x4, waiting for transfers between devices: 31.3 us -> 8.17 us  [shift(): lax.ppermute(shard, axis, [(i, i + by) for i in range(length) if 0 <= i +...]
    pallas_call x0 -> x2, Pallas kernels: none -> 15.7 us  [the longest x1 13.4 us: per_device(): pl.pallas_call(functools.partial(krylov_kernel, ('gy', 'gz')), out_shape=...]
    mul x41 -> x0, other arithmetic: 8.57 us -> none  [the longest x24 7.24 us: stress_rate(): line.append(scaled * value)]
  transfers between devices with their start and end apart: 22 -> 4, of which waited for: 10 -> 3; matrix products, arithmetic and copies ran while one was open for 1% -> 0% of each run, Pallas kernels for 0% -> 0%
where the time goes in v1:
time: 77.9 us; the launch traced here: 77.6 us
  blocking collectives  34.6 us (44%)
  Pallas kernels  15.7 us (20%)
  starting transfers between devices  14.7 us (19%)
  waiting for transfers between devices  8.17 us (10%)
  other arithmetic  3.28 us (4%)
    all_to_all x1, blocking collectives, per_device(): every = lax.all_to_all(sums, ('gy', 'gz'), 0, 0, tiled=True)  34.6 us
    ppermute x4, starting transfers between devices, shift(): lax.ppermute(shard, axis, [(i, i + by) for i in range(length) if 0 <= i +...  14.7 us
    pallas_call x1, Pallas kernels, per_device(): pl.pallas_call(functools.partial(krylov_kernel, ('gy', 'gz')), out_shape=...  13.4 us
    ppermute x4, waiting for transfers between devices, shift(): lax.ppermute(shard, axis, [(i, i + by) for i in range(length) if 0 <= i +...  8.17 us
    pallas_call x1, Pallas kernels, per_device(): pl.pallas_call(functools.partial(combine_kernel, muscles, scale), out_sha...  2.33 us
  transfers between devices with their start and end apart: 4, of which 3 were waited for; matrix products, arithmetic and copies ran while one was open for 0% of the time, Pallas kernels for 0%

profile of v1, /device:TPU:1, one launch (start us, length us, event | category | flops | bytes accessed | tf_op | source)
XLA Modules:
  0.0 77.6 jit_solution(5794695456250736168)
XLA Ops:
  0.6 0.8 %convert_bitcast_fusion = f32[1,8,8,256]{3,2,1,0:T(8,128)S(1)} fusion(s32[8,8,256]{2,1,0:T(8,128)} %param.7), kind=kLoop, calls=%fused_computation.5 | loop fusion | flops 16384 | bytes 131072 | tf_op jit(solution)/shard_map/broadcast_in_dim | solution.py:454
  1.5 1.1 %select_reduce_fusion = f32[8,8,256]{2,1,0:T(8,128)S(1)} fusion(f32[32]{0:T(128)} %param.9, s32[8,8,256]{2,1,0:T(8,128)} %group_ref.1), kind=kLoop, calls=%fused_computation | loop fusion | flops 1556480 | bytes 131200 | tf_op jit(solution)/shard_map/reduce_sum | solution.py:445
  2.6 0.0 copy-start
  2.6 0.0 copy-start.2
  2.6 1.1 %pad_maximum_fusion.1 = f32[8,8,8,256]{3,2,1,0:T(8,128)S(1)} fusion(f32[1,8,8,256]{3,2,1,0:T(8,128)S(1)} %bitcast.10, f32[1,8,8,256]{3,2,1,0:T(8,128)S(1)} %convert_bitcast_fusion, f32[3,8,8,256]{3,2,1,0:T(8,128)} %load_ref.3, f32[3,8,8,256]{3,2,1,0:T(8,128)} %param.5), kind=kLoop, calls=%fused_computation.3 | loop fusion | flops 393216 | bytes 1048576 | tf_op jit(solution)/shard_map/concatenate | solution.py:453
  3.8 1.3 %collective-permute-start.1 = (f32[8,8,4,256]{3,2,1,0:T(4,128)S(1)}, f32[8,8,4,256]{3,2,1,0:T(4,128)S(1)}, u32[]{:S(2)}, u32[]{:S(2)}) collective-permute-start(f32[8,8,4,256]{3,2,1,0:T(4,128)S(1)} %slice.17), channel_id=1, source_target_pairs={{1,0},{2,1},{3,2},{4,3},{5,4},{6,5},{7,6},{8,7},{9,8},{10,9},{11,1... | collective-permute-start | bytes 786440 | tf_op jit(solution)/shard_map/ppermute | solution.py:436
  5.1 0.1 slice.16
  5.2 4.6 %collective-permute-start = (f32[8,8,3,256]{3,2,1,0:T(4,128)S(1)}, f32[8,8,3,256]{3,2,1,0:T(4,128)S(1)}, u32[]{:S(2)}, u32[]{:S(2)}) collective-permute-start(f32[8,8,3,256]{3,2,1,0:T(4,128)S(1)} %slice.16), channel_id=1, source_target_pairs={{0,1},{1,2},{2,3},{3,4},{4,5},{5,6},{6,7},{7,8},{8,9},{9,10},{10,1... | collective-permute-start | bytes 589832 | tf_op jit(solution)/shard_map/ppermute | solution.py:436
  9.8 3.3 %collective-permute-done = f32[8,8,3,256]{3,2,1,0:T(4,128)S(1)} collective-permute-done((f32[8,8,3,256]{3,2,1,0:T(4,128)S(1)}, f32[8,8,3,256]{3,2,1,0:T(4,128)S(1)}, u32[]{:S(2)}, u32[]{:S(2)}) %collective-permute-start) | collective-permute-done | bytes 196640 | tf_op jit(solution)/shard_map/ppermute | solution.py:436
  13.0 0.0 collective-permute-done.1
  13.0 0.0 copy-done
  13.0 0.0 copy-done.2
  13.0 0.2 pad_maximum_fusion.e_ref
  13.2 0.0 copy-start.1
  13.3 5.7 %collective-permute-start.3 = (f32[8,4,15,256]{3,2,1,0:T(8,128)S(1)}, f32[8,4,15,256]{3,2,1,0:T(8,128)S(1)}, u32[]{:S(2)}, u32[]{:S(2)}) collective-permute-start(f32[8,4,15,256]{3,2,1,0:T(8,128)S(1)} %slice.19), channel_id=1, source_target_pairs={{16,0},{32,16},{48,32},{64,48},{80,64},{96,80},{112,96},{128,112},... | collective-permute-start | bytes 1474568 | tf_op jit(solution)/shard_map/ppermute | solution.py:436
  19.0 3.1 %collective-permute-start.2 = (f32[8,3,15,256]{3,2,1,0:T(8,128)S(1)}, f32[8,3,15,256]{3,2,1,0:T(8,128)S(1)}, u32[]{:S(2)}, u32[]{:S(2)}) collective-permute-start(f32[8,3,15,256]{3,2,1,0:T(8,128)S(1)} %slice.18), channel_id=1, source_target_pairs={{0,16},{16,32},{32,48},{48,64},{64,80},{80,96},{96,112},{112,128},... | collective-permute-start | bytes 1105928 | tf_op jit(solution)/shard_map/ppermute | solution.py:436
  22.2 4.7 %collective-permute-done.2.ylo_ref = f32[8,3,15,256]{3,2,1,0:T(8,128)S(1)} collective-permute-done((f32[8,3,15,256]{3,2,1,0:T(8,128)S(1)}, f32[8,3,15,256]{3,2,1,0:T(8,128)S(1)}, u32[]{:S(2)}, u32[]{:S(2)}) %collective-permute-start.2) | collective-permute-done | bytes 368672 | tf_op jit(solution)/shard_map/ppermute | solution.py:436
  26.9 0.2 collective-permute-done.3.yhi_ref
  27.0 0.0 copy-done.1
  27.0 13.4 %krylov.1 = (f32[256,256]{1,0:T(8,128)S(1)}, f32[3,3,8,8,256]{4,3,2,1,0:T(8,128)S(1)}) custom-call(f32[8,8,15,256]{3,2,1,0:T(8,128)S(1)} %pad_maximum_fusion.e_ref, f32[8,3,15,256]{3,2,1,0:T(8,128)S(1)} %collective-permute-done.2.ylo_ref, f32[8,4,15,256]{3,2,1,0:T(8,128)S(1)} %collective-permute-done.3.yhi_ref, f32[3,8,8,256]{3,2,1,0:T(8,128)S(1)} %copy-done, ...), custom_call_target="tpu_custom_call" | custom-call | tf_op jit(solution)/shard_map/krylov/pallas_call | solution.py:465
  40.4 0.3 copy.8
  40.7 34.6 %all_to_all.11 = f32[256,1,256]{2,1,0:T(1,128)S(1)} all-to-all(f32[256,1,256]{2,1,0:T(1,128)S(1)} %copy.8), channel_id=1, replica_groups=mesh['gy'=16,'gz'=16] {'gy','gz'}, dimensions={0} | all-to-all | bytes 524288 | tf_op jit(solution)/shard_map/all_to_all | solution.py:485
  75.3 2.3 %combine.1 = (f32[3,8,8,256]{3,2,1,0:T(8,128)}, f32[1,32]{1,0:T(1,128)}) custom-call(f32[256,256]{1,0:T(8,128)S(1)} %bitcast.8, f32[3,8,8,256]{3,2,1,0:T(8,128)S(1)} %copy-done, f32[3,3,8,8,256]{4,3,2,1,0:T(8,128)S(1)} %get-tuple-element.7.basis_ref), custom_call_target="tpu_custom_call" | custom-call | tf_op jit(solution)/shard_map/combine/pallas_call | solution.py:489
  (4 shorter events, 0.1 us)
Async XLA Ops:
  2.6 10.4 %copy-start = (f32[3,8,8,256]{3,2,1,0:T(8,128)S(1)}, f32[3,8,8,256]{3,2,1,0:T(8,128)}, u32[]{:S(2)}) copy-start(f32[3,8,8,256]{3,2,1,0:T(8,128)} %load_ref.3) | copy-start | bytes 589828
  2.6 10.4 %copy-start.2 = (f32[3,8,8,256]{3,2,1,0:T(8,128)S(1)}, f32[3,8,8,256]{3,2,1,0:T(8,128)}, u32[]{:S(2)}) copy-start(f32[3,8,8,256]{3,2,1,0:T(8,128)} %param.5) | copy-start | bytes 589828
  3.8 9.2 %collective-permute-start.1 = (f32[8,8,4,256]{3,2,1,0:T(4,128)S(1)}, f32[8,8,4,256]{3,2,1,0:T(4,128)S(1)}, u32[]{:S(2)}, u32[]{:S(2)}) collective-permute-start(f32[8,8,4,256]{3,2,1,0:T(4,128)S(1)} %slice.17), channel_id=1, source_target_pairs={{1,0},{2,1},{3,2},{4,3},{5,4},{6,5},{7,6},{8,7},{9,8},{10,9},{11,1... | collective-permute-start | bytes 786440 | tf_op jit(solution)/shard_map/ppermute | solution.py:436
  5.2 7.9 %collective-permute-start = (f32[8,8,3,256]{3,2,1,0:T(4,128)S(1)}, f32[8,8,3,256]{3,2,1,0:T(4,128)S(1)}, u32[]{:S(2)}, u32[]{:S(2)}) collective-permute-start(f32[8,8,3,256]{3,2,1,0:T(4,128)S(1)} %slice.16), channel_id=1, source_target_pairs={{0,1},{1,2},{2,3},{3,4},{4,5},{5,6},{6,7},{7,8},{8,9},{9,10},{10,1... | collective-permute-start | bytes 589832 | tf_op jit(solution)/shard_map/ppermute | solution.py:436
  13.2 13.8 %copy-start.1 = (s32[8,8,256]{2,1,0:T(8,128)S(1)}, s32[8,8,256]{2,1,0:T(8,128)}, u32[]{:S(2)}) copy-start(s32[8,8,256]{2,1,0:T(8,128)} %group_ref.1) | copy-start | bytes 196612
  13.3 13.7 %collective-permute-start.3 = (f32[8,4,15,256]{3,2,1,0:T(8,128)S(1)}, f32[8,4,15,256]{3,2,1,0:T(8,128)S(1)}, u32[]{:S(2)}, u32[]{:S(2)}) collective-permute-start(f32[8,4,15,256]{3,2,1,0:T(8,128)S(1)} %slice.19), channel_id=1, source_target_pairs={{16,0},{32,16},{48,32},{64,48},{80,64},{96,80},{112,96},{128,112},... | collective-permute-start | bytes 1474568 | tf_op jit(solution)/shard_map/ppermute | solution.py:436
  19.0 7.8 %collective-permute-start.2 = (f32[8,3,15,256]{3,2,1,0:T(8,128)S(1)}, f32[8,3,15,256]{3,2,1,0:T(8,128)S(1)}, u32[]{:S(2)}, u32[]{:S(2)}) collective-permute-start(f32[8,3,15,256]{3,2,1,0:T(8,128)S(1)} %slice.18), channel_id=1, source_target_pairs={{0,16},{16,32},{32,48},{48,64},{64,80},{80,96},{96,112},{112,128},... | collective-permute-start | bytes 1105928 | tf_op jit(solution)/shard_map/ppermute | solution.py:436

commit v2 on v1

v2 whole, which is shorter than its diff:
```python
import functools
import math

import jax
import jax.numpy as jnp
from jax import lax
from jax.experimental import pallas as pl
from jax.experimental.pallas import tpu as pltpu
from jax.sharding import PartitionSpec as P

SHEAR = 1.0
LAME = 4.0
MASS = 0.05

LOW, HIGH = 3, 4
SIGMA = 16.0
SHIFTS = (0.0, 9.95, 1.95)
NB = 4
LANES = 128
SUB = 8
CHANNELS = 8
TERMS = 15
ALL = tuple((zt, h) for zt in range(2) for h in range(2))
OWN = ((0, 0), (0, 1))
VMEM = pl.BlockSpec(memory_space=pltpu.VMEM)
SMEM = pl.BlockSpec(memory_space=pltpu.SMEM)


class Shifts:
    def __init__(self):
        lane = lax.broadcasted_iota(jnp.int32, (SUB, LANES), 1)
        self.sub = lax.broadcasted_iota(jnp.int32, (SUB, LANES), 0)
        self.last_lane = lane == LANES - 1
        self.first_lane = lane == 0
        self.last_sub = self.sub == SUB - 1
        self.first_sub = self.sub == 0

    def xup(self, v):
        out = {}
        for zt in {zt for zt, _ in v}:
            r0 = pltpu.roll(v[zt, 0], LANES - 1, 1)
            r1 = pltpu.roll(v[zt, 1], LANES - 1, 1)
            out[zt, 0] = jnp.where(self.last_lane, r1, r0)
            out[zt, 1] = jnp.where(self.last_lane, 0.0, r1)
        return out

    def xdown(self, v):
        out = {}
        for zt in {zt for zt, _ in v}:
            r0 = pltpu.roll(v[zt, 0], 1, 1)
            r1 = pltpu.roll(v[zt, 1], 1, 1)
            out[zt, 0] = jnp.where(self.first_lane, 0.0, r0)
            out[zt, 1] = jnp.where(self.first_lane, r0, r1)
        return out

    def zup(self, v, keys):
        out = {}
        for h in range(2):
            r0 = pltpu.roll(v[0, h], SUB - 1, 0)
            r1 = pltpu.roll(v[1, h], SUB - 1, 0)
            out[0, h] = jnp.where(self.last_sub, r1, r0)
            if (1, h) in keys:
                out[1, h] = jnp.where(self.last_sub, r0, r1)
        return out

    def zdown(self, v):
        out = {}
        for h in range(2):
            r0 = pltpu.roll(v[0, h], 1, 0)
            r1 = pltpu.roll(v[1, h], 1, 0)
            out[0, h] = jnp.where(self.first_sub, r1, r0)
            out[1, h] = jnp.where(self.first_sub, r0, r1)
        return out


def part(k):
    return pl.ds(SUB * k[0], SUB), pl.ds(LANES * k[1], LANES)


def get(ref, *index):
    return {k: ref[(*index, *part(k))] for k in ALL}


def put(ref, value, *index):
    for k in value:
        ref[(*index, *part(k))] = value[k]


def add(a, b):
    return {k: a[k] + b[k] for k in a}


def sub(a, b):
    return {k: a[k] - b[k] for k in a}


def raw_gradient(sh, read, q, keys=ALL):
    result = []
    for comp in range(3):
        here, above = read(comp, q), read(comp, q + 1)
        both, step = add(here, above), sub(above, here)
        both_x, step_x = sh.xup(both), sh.xup(step)
        wide, slope, rise = add(both, both_x), sub(both_x, both), add(step, step_x)
        result.append(
            tuple(
                {k: up[k] + sign * v[k] if sign > 0 else up[k] - v[k] for k in keys}
                for v, up, sign in (
                    (slope, sh.zup(slope, keys), 1),
                    (rise, sh.zup(rise, keys), 1),
                    (wide, sh.zup(wide, keys), -1),
                )
            )
        )
    return result


def row_terms(sh, ext, terms, q):
    grad = raw_gradient(sh, lambda comp, at: get(ext, comp, at), q)
    for k in ALL:
        occ, level = ext[(6, q, *part(k))], ext[(7, q, *part(k))]
        deform = [
            [0.25 * grad[r][c][k] + (1.0 if r == c else 0.0) for c in range(3)] for r in range(3)
        ]
        cof = [
            [
                deform[(r + 1) % 3][(c + 1) % 3] * deform[(r + 2) % 3][(c + 2) % 3]
                - deform[(r + 1) % 3][(c + 2) % 3] * deform[(r + 2) % 3][(c + 1) % 3]
                for c in range(3)
            ]
            for r in range(3)
        ]
        volume = deform[0][0] * cof[0][0] + deform[0][1] * cof[0][1] + deform[0][2] * cof[0][2]
        inverse = 1.0 / volume
        scaled = occ * (1.0 / (16.0 * SIGMA))
        values = [cof[r][c] * inverse for r in range(3) for c in range(3)]
        values.append(scaled * (SHEAR - LAME * jnp.log(volume)))
        values.append(scaled)
        values.append(scaled * (SHEAR + level))
        quarter = 0.25 * occ
        values += [quarter * deform[r][0] for r in range(3)]
        for i, value in enumerate(values):
            terms[(i, q, *part(k))] = value


def row_rate(grad, terms, works, step, q, keys=ALL):
    rate = [[{} for _ in range(3)] for _ in range(3)]
    for k in keys:

        def term(i):
            return terms[(i, q, *part(k))]

        g = [[grad[r][c][k] for c in range(3)] for r in range(3)]
        inv_t = [[term(3 * r + c) for c in range(3)] for r in range(3)]
        shear, occ, fibre = term(9), term(10), term(11)
        pulled = [
            [
                inv_t[0][a] * g[0][b] + inv_t[1][a] * g[1][b] + inv_t[2][a] * g[2][b]
                for b in range(3)
            ]
            for a in range(3)
        ]
        spread = (LAME * occ) * (pulled[0][0] + pulled[1][1] + pulled[2][2])
        z = [
            [shear * pulled[c][m] + spread if c == m else shear * pulled[c][m] for c in range(3)]
            for m in range(3)
        ]
        for r in range(3):
            for c in range(3):
                rate[r][c][k] = (
                    (fibre if c == 0 else occ) * g[r][c]
                    + inv_t[r][0] * z[0][c]
                    + inv_t[r][1] * z[1][c]
                    + inv_t[r][2] * z[2][c]
                )
        if k in OWN:
            works[(step, q, *part(k))] = (
                term(12) * g[0][0] + term(13) * g[1][0] + term(14) * g[2][0]
            )
    return rate


def row_force(sh, before, rate, comp):
    p = add(before[comp][0], rate[comp][0])
    a = sub(before[comp][1], rate[comp][1])
    b = add(before[comp][2], rate[comp][2])
    along = add(p, sh.zdown(p))
    across = add(sh.zdown(add(a, b)), sub(a, b))
    return add(sh.xdown(add(along, across)), sub(across, along))


def load_rate(ref, *index):
    return [[get(ref, *index, 3 * r + c) for c in range(3)] for r in range(3)]


def save_rate(ref, rate, *index):
    for r in range(3):
        for c in range(3):
            put(ref, rate[r][c], *index, 3 * r + c)


class Sweep:
    def __init__(self, axes, rows, ext, fields, terms, works, last):
        self.sh = Shifts()
        self.ext, self.fields, self.terms, self.works, self.last = ext, fields, terms, works, last
        ends = [lax.axis_index(axis) == lax.axis_size(axis) - 1 for axis in axes]
        self.top_y = jnp.where(ends[0], LOW + rows, -1)
        top_z = jnp.where(ends[1], SUB, -1)
        self.keep_z = {k: jnp.where(self.sh.sub + SUB * k[0] == top_z, 0.0, 1.0) for k in ALL}

    def read(self, step):
        if step == 0:
            return lambda comp, q: get(self.ext, 3 + comp, q)
        return lambda comp, q: get(self.fields, step - 1, comp, q)

    def rate(self, step, q):
        if step == 0:
            row_terms(self.sh, self.ext, self.terms, q)
        grad = raw_gradient(self.sh, self.read(step), q)
        return row_rate(grad, self.terms, self.works, step, q)

    def node(self, step, q, rate):
        before = load_rate(self.last)
        keep_y = jnp.where(q == self.top_y, 0.0, 1.0)
        for comp in range(3):
            force = row_force(self.sh, before, rate, comp)
            if SHIFTS[step] != 0.0:
                here = self.read(step)(comp, q)
                force = {k: force[k] - (SHIFTS[step] / SIGMA) * here[k] for k in ALL}
            put(
                self.fields,
                {k: force[k] * (self.keep_z[k] * keep_y) for k in ALL},
                step,
                comp,
                q,
            )

    def rows(self, step, start, stop):
        def body(q, carry):
            rate = self.rate(step, q)
            self.node(step, q, rate)
            save_rate(self.last, rate)
            return carry

        lax.fori_loop(start, stop, body, 0)


def pack_kernel(
    disp_ref, load_ref, occ_ref, group_ref, act_ref, block_ref, zhi_ref, zlo_ref, yhi_ref, ylo_ref
):
    rows, cols, depth = occ_ref.shape
    muscles = act_ref.shape[0]

    def row(y, carry):
        group = group_ref[y]
        level = jnp.zeros((cols, depth), jnp.float32)
        for m in range(muscles):
            level = jnp.where(group == m, act_ref[m], level)
        values = [disp_ref[c, y] for c in range(3)] + [load_ref[c, y] for c in range(3)]
        values += [occ_ref[y].astype(jnp.float32), level]
        for c, value in enumerate(values):
            block_ref[c, y] = value
            zhi_ref[c, y] = value[:HIGH]
            zlo_ref[c, y] = value[cols - LOW :]
        return carry

    lax.fori_loop(0, rows, row, 0)

    def channel(c, carry):
        for y in range(HIGH):
            yhi_ref[c, y] = block_ref[c, y]
        for y in range(LOW):
            ylo_ref[c, y] = block_ref[c, rows - LOW + y]
        return carry

    lax.fori_loop(0, CHANNELS, channel, 0)


def inner_kernel(axes, block_ref, zlo_ref, zhi_ref, ext, fields, terms, works, edge, last):
    rows, depth = block_ref.shape[1], block_ref.shape[-1]
    blank = jnp.zeros((1, depth), jnp.float32)

    def assemble(c, carry):
        for y in range(rows):
            ext[c, LOW + y, pl.ds(0, SUB), :] = block_ref[c, y]
            ext[c, LOW + y, pl.ds(SUB, HIGH), :] = zhi_ref[c, y]
            ext[c, LOW + y, pl.ds(SUB + HIGH, 1), :] = blank
            ext[c, LOW + y, pl.ds(2 * SUB - LOW, LOW), :] = zlo_ref[c, y]
        return carry

    lax.fori_loop(0, CHANNELS, assemble, 0)
    sweep = Sweep(axes, rows, ext, fields, terms, works, last)
    for step in range(NB - 1):
        first, final = LOW + step, LOW + rows - 2 - step
        rate = sweep.rate(step, first)
        save_rate(last, rate)
        save_rate(edge, rate, step, 0)
        sweep.rows(step, first + 1, final + 1)
        save_rate(edge, load_rate(last), step, 1)


def outer_kernel(
    axes,
    group_ref,
    ylo_ref,
    yhi_ref,
    clo_ref,
    chi_ref,
    ext_in,
    fields_in,
    terms_in,
    works_in,
    edge,
    sums_ref,
    ext,
    fields,
    terms,
    works,
    last,
    table,
):
    del ext_in, fields_in, terms_in, works_in
    rows = group_ref.shape[0]

    def assemble(c, carry):
        for q in range(LOW):
            ext[c, q, pl.ds(0, SUB), :] = ylo_ref[c, q]
            ext[c, q, pl.ds(SUB, SUB), :] = clo_ref[c, q]
        for q in range(HIGH):
            ext[c, LOW + rows + q, pl.ds(0, SUB), :] = yhi_ref[c, q]
            ext[c, LOW + rows + q, pl.ds(SUB, SUB), :] = chi_ref[c, q]
        return carry

    lax.fori_loop(0, CHANNELS, assemble, 0)
    sweep = Sweep(axes, rows, ext, fields, terms, works, last)
    for step in range(NB - 1):
        save_rate(last, sweep.rate(step, step))
        sweep.rows(step, step + 1, LOW + step)
        sweep.node(step, LOW + step, load_rate(edge, step, 0))
        save_rate(last, load_rate(edge, step, 1))
        sweep.rows(step, LOW + rows - 1 - step, LOW + rows + HIGH - 1 - step)

    zero = jnp.zeros((SUB, LANES), jnp.float32)
    pairs = [(i, j) for i in range(NB) for j in range(i, NB)]

    def finish(q, acc):
        acc = list(acc)
        grad = raw_gradient(sweep.sh, sweep.read(NB - 1), q, OWN)
        rate = row_rate(grad, terms, works, NB - 1, q, OWN)
        for k in OWN:
            for r in range(3):
                for c in range(3):
                    acc[-1] = acc[-1] + rate[r][c][k] * grad[r][c][k]
            for comp in range(3):
                vectors = [ext[(3 + comp, q, *part(k))]]
                vectors += [fields[(s, comp, q, *part(k))] for s in range(NB - 1)]
                for n, (i, j) in enumerate(pairs):
                    acc[n] = acc[n] + vectors[i] * vectors[j]
        return tuple(acc)

    acc = lax.fori_loop(LOW, LOW + rows, finish, tuple(zero for _ in range(len(pairs) + 1)))
    table[...] = jnp.zeros_like(table)
    muscles = (table.shape[0] // 2) // NB
    for n, value in enumerate(acc):
        table[pl.ds(NB * muscles + n, 1), :] = jnp.sum(value, axis=0, keepdims=True)

    def muscle(m, carry):
        total = [zero] * NB
        for y in range(rows):
            for h in range(2):
                mine = group_ref[y, :, pl.ds(LANES * h, LANES)] == m
                for step in range(NB):
                    total[step] = total[step] + jnp.where(
                        mine, works[(step, LOW + y, *part((0, h)))], 0.0
                    )
        for step in range(NB):
            table[pl.ds(step * muscles + m, 1), :] = jnp.sum(total[step], axis=0, keepdims=True)
        return carry

    lax.fori_loop(0, muscles, muscle, 0)
    row = lax.dot_general(
        jnp.ones((SUB, LANES), jnp.float32),
        table[...],
        (((1,), (1,)), ((), ())),
        precision=lax.Precision.HIGHEST,
        preferred_element_type=jnp.float32,
    )
    for i in range(sums_ref.shape[0] // SUB):
        sums_ref[pl.ds(SUB * i, SUB), :] = row


def combine_kernel(muscles, scale, sums_ref, load_ref, fields, x_ref, grad_ref):
    total = jnp.sum(sums_ref[...], axis=0, keepdims=True)
    at = NB * muscles
    pairs = [(i, j) for i in range(NB) for j in range(i, NB)]
    gram = {}
    for n, (i, j) in enumerate(pairs):
        gram[i, j] = gram[j, i] = total[:, at + n : at + n + 1]
    energy = total[:, at + len(pairs) : at + len(pairs) + 1]
    shifts = [MASS + s for s in SHIFTS]
    form = {}
    for j in range(NB - 1):
        for i in range(j + 1):
            form[i, j] = form[j, i] = SIGMA * gram[i, j + 1] + shifts[j] * gram[i, j]
    last = NB - 1
    for i in range(last):
        form[i, last] = form[last, i] = SIGMA * gram[i + 1, last] + shifts[i] * gram[i, last]
    form[last, last] = SIGMA * energy + MASS * gram[last, last]

    def quadratic(matrix, v):
        parts = []
        for i in range(NB):
            if v[i] is None:
                continue
            inner = [matrix[i, j] * v[j] for j in range(NB) if v[j] is not None]
            parts.append(v[i] * functools.reduce(lambda s, t: s + t, inner))
        return functools.reduce(lambda s, t: s + t, parts)

    one = jnp.ones((1, 1), jnp.float32)
    x = [None] * NB
    residual = [one] + [None] * (NB - 1)
    direction = list(residual)
    norm = gram[0, 0]

    def axpy(a, u, v):
        out = []
        for s, t in zip(u, v):
            if s is None:
                out.append(t)
            elif t is None:
                out.append(a * s)
            else:
                out.append(t + a * s)
        return out

    for step in range(NB):
        alpha = norm / quadratic(form, direction)
        x = axpy(alpha, direction, x)
        if step == NB - 1:
            break
        image = [None] * NB
        for i in range(NB - 1):
            if direction[i] is not None:
                up = SIGMA * direction[i]
                same = shifts[i] * direction[i]
                image[i] = same if image[i] is None else image[i] + same
                image[i + 1] = up if image[i + 1] is None else image[i + 1] + up
        residual = axpy(-alpha, image, residual)
        new = quadratic(gram, residual)
        direction = axpy(new / norm, direction, residual)
        norm = new

    grad = None
    for k in range(NB):
        part = x[k] * total[:, k * muscles : (k + 1) * muscles]
        grad = part if grad is None else grad + part
    grad_ref[...] = -scale * grad

    width = load_ref.shape[-1]
    coef = [jnp.broadcast_to(x[k], (SUB, width)) for k in range(NB)]

    def row(y, carry):
        for comp in range(3):
            value = coef[0] * load_ref[comp, y]
            for k in range(1, NB):
                value = value + coef[k] * fields[k - 1, comp, LOW + y, pl.ds(0, SUB), :]
            x_ref[comp, y] = value
        return carry

    lax.fori_loop(0, load_ref.shape[1], row, 0)


def shift(shard, axis, by):
    length = lax.axis_size(axis)
    return lax.ppermute(
        shard, axis, [(i, i + by) for i in range(length) if 0 <= i + by < length]
    )


def per_device(displacement, load, occupancy, voxel_muscle_group, activation):
    rows, cols, depth = occupancy.shape
    muscles = activation.shape[0]
    axes = ("gy", "gz")
    count = LOW + rows + HIGH

    def arr(*shape):
        return jax.ShapeDtypeStruct(shape, jnp.float32)

    block, face_hi, face_lo, row_hi, row_lo = pl.pallas_call(
        pack_kernel,
        out_shape=(
            arr(CHANNELS, rows, cols, depth),
            arr(CHANNELS, rows, HIGH, depth),
            arr(CHANNELS, rows, LOW, depth),
            arr(CHANNELS, HIGH, cols, depth),
            arr(CHANNELS, LOW, cols, depth),
        ),
        in_specs=[VMEM] * 4 + [SMEM],
        out_specs=(VMEM,) * 5,
        compiler_params=pltpu.CompilerParams(vmem_limit_bytes=32 << 20),
        name="pack",
    )(displacement, load, occupancy, voxel_muscle_group, activation)

    zhi = shift(face_hi, "gz", -1)
    zlo = shift(face_lo, "gz", 1)
    yhi = shift(row_hi, "gy", -1)
    ylo = shift(row_lo, "gy", 1)
    gap = jnp.zeros((CHANNELS, rows, 1, depth), jnp.float32)
    around = jnp.concatenate([zhi, gap, zlo], axis=2)
    chi = shift(around[:, :HIGH], "gy", -1)
    clo = shift(around[:, rows - LOW :], "gy", 1)

    state = (
        arr(CHANNELS, count, 2 * SUB, depth),
        arr(NB - 1, 3, count, 2 * SUB, depth),
        arr(TERMS, count - 1, 2 * SUB, depth),
        arr(NB, count - 1, SUB, depth),
    )
    kept = pltpu.VMEM((9, 2 * SUB, depth), jnp.float32)
    inner = pl.pallas_call(
        functools.partial(inner_kernel, axes),
        out_shape=(*state, arr(NB - 1, 2, 9, 2 * SUB, depth)),
        in_specs=[VMEM] * 3,
        out_specs=(VMEM,) * 5,
        scratch_shapes=[kept],
        compiler_params=pltpu.CompilerParams(vmem_limit_bytes=32 << 20),
        name="inner",
    )(block, zlo, zhi)

    devices = lax.axis_size("gy") * lax.axis_size("gz")
    sums, _, fields, _, _ = pl.pallas_call(
        functools.partial(outer_kernel, axes),
        out_shape=(arr(devices, 2 * NB * muscles), *state),
        in_specs=[VMEM] * 10,
        out_specs=(VMEM,) * 5,
        scratch_shapes=[kept, pltpu.VMEM((2 * NB * muscles, LANES), jnp.float32)],
        input_output_aliases={5: 1, 6: 2, 7: 3, 8: 4},
        compiler_params=pltpu.CompilerParams(vmem_limit_bytes=32 << 20),
        name="outer",
    )(voxel_muscle_group, ylo, yhi, clo, chi, *inner)

    every = lax.all_to_all(sums, ("gy", "gz"), 0, 0, tiled=True)

    cells = depth * rows * lax.axis_size("gy") * cols * lax.axis_size("gz")
    scale = 1.0 / math.sqrt(cells / muscles)
    adjoint, muscle_grad = pl.pallas_call(
        functools.partial(combine_kernel, muscles, scale),
        out_shape=(
            jax.ShapeDtypeStruct(load.shape, jnp.float32),
            jax.ShapeDtypeStruct((1, muscles), jnp.float32),
        ),
        in_specs=[VMEM] * 3,
        out_specs=(VMEM, VMEM),
        compiler_params=pltpu.CompilerParams(vmem_limit_bytes=32 << 20),
        name="combine",
    )(every, load, fields)
    return adjoint, muscle_grad.reshape(muscles)


def solution(mesh):
    placed = (
        P(None, "gy", "gz", None),
        P(None, "gy", "gz", None),
        P("gy", "gz", None),
        P("gy", "gz", None),
        P(),
    )
    return jax.shard_map(
        per_device,
        mesh=mesh,
        in_specs=placed,
        out_specs=(P(None, "gy", "gz", None), P()),
        check_vma=False,
    )
```

time: 77.9 us -> 75.7 us (0.972)
  waiting for transfers between devices: 8.17 us -> 0.02 us
  starting transfers between devices: 14.7 us -> 20.3 us
  local copies, waits for them, and re-layouts: 0.47 us -> 4.59 us
  other arithmetic: 3.28 us -> 0.14 us
  blocking collectives: 34.6 us -> 32.9 us
  Pallas kernels: 15.7 us -> 16.5 us
    ppermute x4 -> x6, waiting for transfers between devices: 8.17 us -> 0.02 us  [shift(): lax.ppermute(shard, axis, [(i, i + by) for i in range(length) if 0 <= i +...]
    ppermute x4 -> x6, starting transfers between devices: 14.7 us -> 20.3 us  [shift(): lax.ppermute(shard, axis, [(i, i + by) for i in range(length) if 0 <= i +...]
    unnamed x7 -> x15, local copies, waits for them, and re-layouts: 0.04 us -> 4.21 us
    all_to_all x1, blocking collectives: 34.6 us -> 32.9 us  [per_device(): every = lax.all_to_all(sums, ('gy', 'gz'), 0, 0, tiled=True)]
    concatenate x2 -> x1, other arithmetic: 1.3 us -> 0.14 us  [per_device(): around = jnp.concatenate([zhi, gap, zlo], axis=2)]
    reduce_sum x1 -> x0, other arithmetic: 1.13 us -> none  [per_device(): jnp.sum(jnp.where(voxel_muscle_group[None] == levels[:, None, None, None]...]
    broadcast_in_dim x1 -> x0, other arithmetic: 0.85 us -> none  [per_device(): occupancy.astype(jnp.float32)[None]]
    pallas_call x1 -> x3, Pallas kernels: 13.4 us -> 14.2 us  [the longest x1 8.9 us: per_device(): pl.pallas_call(functools.partial(outer_kernel, axes), out_shape=(arr(devi...]
  transfers between devices with their start and end apart: 4 -> 6, of which waited for: 3 -> 0; matrix products, arithmetic and copies ran while one was open for 0% -> 0% of each run, Pallas kernels for 0% -> 6%
where the time goes in v2:
time: 75.7 us; the launch traced here: 75.2 us
  blocking collectives  32.9 us (43%)
  starting transfers between devices  20.3 us (27%)
  Pallas kernels  16.5 us (22%)
  local copies, waits for them, and re-layouts  4.59 us (6%)
  between operations  0.8 us (1%)
    all_to_all x1, blocking collectives, per_device(): every = lax.all_to_all(sums, ('gy', 'gz'), 0, 0, tiled=True)  32.9 us
    ppermute x6, starting transfers between devices, shift(): lax.ppermute(shard, axis, [(i, i + by) for i in range(length) if 0 <= i +...  20.3 us
    pallas_call x1, Pallas kernels, per_device(): pl.pallas_call(functools.partial(outer_kernel, axes), out_shape=(arr(devi...  8.9 us
    pallas_call x1, Pallas kernels, per_device(): pl.pallas_call(functools.partial(inner_kernel, axes), out_shape=(*state,...  4.34 us
    unnamed x15, local copies, waits for them, and re-layouts  4.21 us
    pallas_call x1, Pallas kernels, per_device(): pl.pallas_call(functools.partial(combine_kernel, muscles, scale), out_sha...  2.33 us
  transfers between devices with their start and end apart: 6, of which 0 were waited for; matrix products, arithmetic and copies ran while one was open for 0% of the time, Pallas kernels for 6%

profile of v2, /device:TPU:1, one launch (start us, length us, event | category | flops | bytes accessed | tf_op | source)
XLA Modules:
  0.0 75.2 jit_solution(1834518037161103822)
XLA Ops:
  0.6 0.0 copy-start
  0.6 0.9 %copy-done = f32[3,8,8,256]{3,2,1,0:T(8,128)S(1)} copy-done((f32[3,8,8,256]{3,2,1,0:T(8,128)S(1)}, f32[3,8,8,256]{3,2,1,0:T(8,128)}, u32[]{:S(2)}) %copy-start) | copy-done | bytes 196632
  1.6 0.8 %copy-done.2 = s32[8,8,256]{2,1,0:T(8,128)S(1)} copy-done((s32[8,8,256]{2,1,0:T(8,128)S(1)}, s32[8,8,256]{2,1,0:T(8,128)}, u32[]{:S(2)}) %copy-start.2) | copy-done | bytes 65560
  2.4 0.9 %copy-done.4 = f32[3,8,8,256]{3,2,1,0:T(8,128)S(1)} copy-done((f32[3,8,8,256]{3,2,1,0:T(8,128)S(1)}, f32[3,8,8,256]{3,2,1,0:T(8,128)}, u32[]{:S(2)}) %copy-start.4) | copy-done | bytes 196632
  3.3 0.8 %copy-done.5 = s32[8,8,256]{2,1,0:T(8,128)S(1)} copy-done((s32[8,8,256]{2,1,0:T(8,128)S(1)}, s32[8,8,256]{2,1,0:T(8,128)}, u32[]{:S(2)}) %copy-start.5) | copy-done | bytes 65560
  4.2 0.7 copy-done.6
  4.8 0.9 %pack.1 = (f32[8,8,8,256]{3,2,1,0:T(8,128)S(1)}, f32[8,8,4,256]{3,2,1,0:T(4,128)S(1)}, f32[8,8,3,256]{3,2,1,0:T(4,128)S(1)}, f32[8,4,8,256]{3,2,1,0:T(8,128)S(1)}, f32[8,3,8,256]{3,2,1,0:T(8,128)S(1)}) custom-call(f32[3,8,8,256]{3,2,1,0:T(8,128)S(1)} %copy-done.4, f32[3,8,8,256]{3,2,1,0:T(8,128)S(1)} %copy-done, s32[8,8,256]{2,1,0:T(8,128)S(1)} %copy-done.5, ...), custom_call_target="tpu_custom_call" | custom-call | tf_op jit(solution)/shard_map/pack/pallas_call | solution.py:488
  5.8 1.3 %collective-permute-start.2 = (f32[8,8,4,256]{3,2,1,0:T(4,128)S(1)}, f32[8,8,4,256]{3,2,1,0:T(4,128)S(1)}, u32[]{:S(2)}, u32[]{:S(2)}) collective-permute-start(f32[8,8,4,256]{3,2,1,0:T(4,128)S(1)} %get-tuple-element.18), channel_id=1, source_target_pairs={{1,0},{2,1},{3,2},{4,3},{5,4},{6,5},{7,6},{8,7},{9,8},{10,9},{11,1... | collective-permute-start | bytes 786440 | tf_op jit(solution)/shard_map/ppermute | solution.py:474
  7.1 4.6 %collective-permute-start.3 = (f32[8,8,3,256]{3,2,1,0:T(4,128)S(1)}, f32[8,8,3,256]{3,2,1,0:T(4,128)S(1)}, u32[]{:S(2)}, u32[]{:S(2)}) collective-permute-start(f32[8,8,3,256]{3,2,1,0:T(4,128)S(1)} %get-tuple-element.19), channel_id=1, source_target_pairs={{0,1},{1,2},{2,3},{3,4},{4,5},{5,6},{6,7},{7,8},{8,9},{9,10},{10,1... | collective-permute-start | bytes 589832 | tf_op jit(solution)/shard_map/ppermute | solution.py:474
  11.6 5.1 %collective-permute-start.1 = (f32[8,4,8,256]{3,2,1,0:T(8,128)S(1)}, f32[8,4,8,256]{3,2,1,0:T(8,128)S(1)}, u32[]{:S(2)}, u32[]{:S(2)}) collective-permute-start(f32[8,4,8,256]{3,2,1,0:T(8,128)S(1)} %get-tuple-element.17), channel_id=1, source_target_pairs={{16,0},{32,16},{48,32},{64,48},{80,64},{96,80},{112,96},{128,112},... | collective-permute-start | bytes 786440 | tf_op jit(solution)/shard_map/ppermute | solution.py:474
  16.8 0.1 pad.1.clone
  16.9 0.1 pad_maximum_fusion
  17.0 3.8 %collective-permute-start.5 = (f32[8,4,8,256]{3,2,1,0:T(8,128)S(1)}, f32[8,4,8,256]{3,2,1,0:T(8,128)S(1)}, u32[]{:S(2)}, u32[]{:S(2)}) collective-permute-start(f32[8,4,8,256]{3,2,1,0:T(8,128)S(1)} %slice.9), channel_id=1, source_target_pairs={{16,0},{32,16},{48,32},{64,48},{80,64},{96,80},{112,96},{128,112},... | collective-permute-start | bytes 786440 | tf_op jit(solution)/shard_map/ppermute | solution.py:474
  20.8 3.1 %collective-permute-start = (f32[8,3,8,256]{3,2,1,0:T(8,128)S(1)}, f32[8,3,8,256]{3,2,1,0:T(8,128)S(1)}, u32[]{:S(2)}, u32[]{:S(2)}) collective-permute-start(f32[8,3,8,256]{3,2,1,0:T(8,128)S(1)} %get-tuple-element.16), channel_id=1, source_target_pairs={{0,16},{16,32},{32,48},{48,64},{64,80},{80,96},{96,112},{112,128},... | collective-permute-start | bytes 589832 | tf_op jit(solution)/shard_map/ppermute | solution.py:474
  23.9 2.4 %collective-permute-start.4 = (f32[8,3,8,256]{3,2,1,0:T(8,128)S(1)}, f32[8,3,8,256]{3,2,1,0:T(8,128)S(1)}, u32[]{:S(2)}, u32[]{:S(2)}) collective-permute-start(f32[8,3,8,256]{3,2,1,0:T(8,128)S(1)} %slice.8), channel_id=1, source_target_pairs={{0,16},{16,32},{32,48},{48,64},{64,80},{80,96},{96,112},{112,128},... | collective-permute-start | bytes 589832 | tf_op jit(solution)/shard_map/ppermute | solution.py:474
  26.4 4.3 %inner.1 = (f32[8,15,16,256]{3,2,1,0:T(8,128)S(1)}, f32[3,3,15,16,256]{4,3,2,1,0:T(8,128)S(1)}, f32[15,14,16,256]{3,2,1,0:T(8,128)S(1)}, f32[4,14,8,256]{3,2,1,0:T(8,128)S(1)}, f32[3,2,9,16,256]{4,3,2,1,0:T(8,128)S(1)}) custom-call(f32[8,8,8,256]{3,2,1,0:T(8,128)S(1)} %get-tuple-element.20.block_ref, f32[8,8,3,256]{3,2,1,0:T(4,128)S(1)} %collective-permute-done.3.zlo_ref, ...), custom_call_target="tpu_custom_call" | custom-call | tf_op jit(solution)/shard_map/inner/pallas_call | solution.py:519
  30.7 0.0 collective-permute-done.ylo_ref
  30.7 0.0 collective-permute-done.4.clo_ref
  30.7 0.0 collective-permute-done.5.chi_ref
  30.8 0.0 copy-start.1
  30.8 8.9 %outer.1 = (f32[256,256]{1,0:T(8,128)S(1)}, f32[8,15,16,256]{3,2,1,0:T(8,128)S(1)}, f32[3,3,15,16,256]{4,3,2,1,0:T(8,128)S(1)}, f32[15,14,16,256]{3,2,1,0:T(8,128)S(1)}, f32[4,14,8,256]{3,2,1,0:T(8,128)S(1)}) custom-call(s32[8,8,256]{2,1,0:T(8,128)S(1)} %copy-done.3, ...), custom_call_target="tpu_custom_call", output_to_operand_aliasing={{1}: (5, {}), {2}: (6, {}), {3}: (7, {}), {4}: (8, {})} | custom-call | tf_op jit(solution)/shard_map/outer/pallas_call | solution.py:530
  39.7 0.3 copy.11
  40.0 32.9 %all_to_all.11 = f32[256,1,256]{2,1,0:T(1,128)S(1)} all-to-all(f32[256,1,256]{2,1,0:T(1,128)S(1)} %copy.11), channel_id=1, replica_groups=mesh['gy'=16,'gz'=16] {'gy','gz'}, dimensions={0} | all-to-all | bytes 524288 | tf_op jit(solution)/shard_map/all_to_all | solution.py:541
  72.9 2.3 %combine.1 = (f32[3,8,8,256]{3,2,1,0:T(8,128)}, f32[1,32]{1,0:T(1,128)}) custom-call(f32[256,256]{1,0:T(8,128)S(1)} %bitcast.6, f32[3,8,8,256]{3,2,1,0:T(8,128)S(1)} %copy-done.1, f32[3,3,15,16,256]{4,3,2,1,0:T(8,128)S(1)} %get-tuple-element.27.fields), custom_call_target="tpu_custom_call" | custom-call | tf_op jit(solution)/shard_map/combine/pallas_call | solution.py:545
  (13 shorter events, 0.1 us)
Async XLA Ops:
  0.6 0.9 %copy-start = (f32[3,8,8,256]{3,2,1,0:T(8,128)S(1)}, f32[3,8,8,256]{3,2,1,0:T(8,128)}, u32[]{:S(2)}) copy-start(f32[3,8,8,256]{3,2,1,0:T(8,128)} %load_ref.3) | copy-start | bytes 589828
  1.6 0.8 %copy-start.2 = (s32[8,8,256]{2,1,0:T(8,128)S(1)}, s32[8,8,256]{2,1,0:T(8,128)}, u32[]{:S(2)}) copy-start(s32[8,8,256]{2,1,0:T(8,128)} %group_ref.3) | copy-start | bytes 196612
  2.4 0.9 %copy-start.4 = (f32[3,8,8,256]{3,2,1,0:T(8,128)S(1)}, f32[3,8,8,256]{3,2,1,0:T(8,128)}, u32[]{:S(2)}) copy-start(f32[3,8,8,256]{3,2,1,0:T(8,128)} %disp_ref.1) | copy-start | bytes 589828
  3.3 0.8 %copy-start.5 = (s32[8,8,256]{2,1,0:T(8,128)S(1)}, s32[8,8,256]{2,1,0:T(8,128)}, u32[]{:S(2)}) copy-start(s32[8,8,256]{2,1,0:T(8,128)} %occ_ref.1) | copy-start | bytes 196612
  4.2 0.7 copy-start.6
  4.8 25.9 %copy-start.3 = (s32[8,8,256]{2,1,0:T(8,128)S(1)}, s32[8,8,256]{2,1,0:T(8,128)}, u32[]{:S(2)}) copy-start(s32[8,8,256]{2,1,0:T(8,128)} %group_ref.3) | copy-start | bytes 196612
  5.8 11.1 %collective-permute-start.2 = (f32[8,8,4,256]{3,2,1,0:T(4,128)S(1)}, f32[8,8,4,256]{3,2,1,0:T(4,128)S(1)}, u32[]{:S(2)}, u32[]{:S(2)}) collective-permute-start(f32[8,8,4,256]{3,2,1,0:T(4,128)S(1)} %get-tuple-element.18), channel_id=1, source_target_pairs={{1,0},{2,1},{3,2},{4,3},{5,4},{6,5},{7,6},{8,7},{9,8},{10,9},{11,1... | collective-permute-start | bytes 786440 | tf_op jit(solution)/shard_map/ppermute | solution.py:474
  7.1 9.8 %collective-permute-start.3 = (f32[8,8,3,256]{3,2,1,0:T(4,128)S(1)}, f32[8,8,3,256]{3,2,1,0:T(4,128)S(1)}, u32[]{:S(2)}, u32[]{:S(2)}) collective-permute-start(f32[8,8,3,256]{3,2,1,0:T(4,128)S(1)} %get-tuple-element.19), channel_id=1, source_target_pairs={{0,1},{1,2},{2,3},{3,4},{4,5},{5,6},{6,7},{7,8},{8,9},{9,10},{10,1... | collective-permute-start | bytes 589832 | tf_op jit(solution)/shard_map/ppermute | solution.py:474
  11.6 19.1 %collective-permute-start.1 = (f32[8,4,8,256]{3,2,1,0:T(8,128)S(1)}, f32[8,4,8,256]{3,2,1,0:T(8,128)S(1)}, u32[]{:S(2)}, u32[]{:S(2)}) collective-permute-start(f32[8,4,8,256]{3,2,1,0:T(8,128)S(1)} %get-tuple-element.17), channel_id=1, source_target_pairs={{16,0},{32,16},{48,32},{64,48},{80,64},{96,80},{112,96},{128,112},... | collective-permute-start | bytes 786440 | tf_op jit(solution)/shard_map/ppermute | solution.py:474
  17.0 13.7 %collective-permute-start.5 = (f32[8,4,8,256]{3,2,1,0:T(8,128)S(1)}, f32[8,4,8,256]{3,2,1,0:T(8,128)S(1)}, u32[]{:S(2)}, u32[]{:S(2)}) collective-permute-start(f32[8,4,8,256]{3,2,1,0:T(8,128)S(1)} %slice.9), channel_id=1, source_target_pairs={{16,0},{32,16},{48,32},{64,48},{80,64},{96,80},{112,96},{128,112},... | collective-permute-start | bytes 786440 | tf_op jit(solution)/shard_map/ppermute | solution.py:474
  20.8 9.9 %collective-permute-start = (f32[8,3,8,256]{3,2,1,0:T(8,128)S(1)}, f32[8,3,8,256]{3,2,1,0:T(8,128)S(1)}, u32[]{:S(2)}, u32[]{:S(2)}) collective-permute-start(f32[8,3,8,256]{3,2,1,0:T(8,128)S(1)} %get-tuple-element.16), channel_id=1, source_target_pairs={{0,16},{16,32},{32,48},{48,64},{64,80},{80,96},{96,112},{112,128},... | collective-permute-start | bytes 589832 | tf_op jit(solution)/shard_map/ppermute | solution.py:474
  23.9 6.8 %collective-permute-start.4 = (f32[8,3,8,256]{3,2,1,0:T(8,128)S(1)}, f32[8,3,8,256]{3,2,1,0:T(8,128)S(1)}, u32[]{:S(2)}, u32[]{:S(2)}) collective-permute-start(f32[8,3,8,256]{3,2,1,0:T(8,128)S(1)} %slice.8), channel_id=1, source_target_pairs={{0,16},{16,32},{32,48},{48,64},{64,80},{80,96},{96,112},{112,128},... | collective-permute-start | bytes 589832 | tf_op jit(solution)/shard_map/ppermute | solution.py:474
  30.8 42.2 %copy-start.1 = (f32[3,8,8,256]{3,2,1,0:T(8,128)S(1)}, f32[3,8,8,256]{3,2,1,0:T(8,128)}, u32[]{:S(2)}) copy-start(f32[3,8,8,256]{3,2,1,0:T(8,128)} %load_ref.3) | copy-start | bytes 589828

commit v3 on v2

--- a/solution.py
+++ b/solution.py
@@ -23,7 +23,6 @@
 ALL = tuple((zt, h) for zt in range(2) for h in range(2))
 OWN = ((0, 0), (0, 1))
 VMEM = pl.BlockSpec(memory_space=pltpu.VMEM)
-SMEM = pl.BlockSpec(memory_space=pltpu.SMEM)
 
 
 class Shifts:
@@ -244,11 +243,48 @@
         lax.fori_loop(start, stop, body, 0)
 
 
+def even(axis):
+    return lax.rem(lax.axis_index(axis), 2) == 0
+
+
 def pack_kernel(
-    disp_ref, load_ref, occ_ref, group_ref, act_ref, block_ref, zhi_ref, zlo_ref, yhi_ref, ylo_ref
+    axes,
+    disp_hbm,
+    load_hbm,
+    occ_hbm,
+    group_hbm,
+    act_hbm,
+    block_ref,
+    zpair_ref,
+    znext_ref,
+    ypair_ref,
+    ynext_ref,
+    disp_ref,
+    load_ref,
+    occ_ref,
+    group_ref,
+    act_ref,
+    sems,
 ):
+    copies = [
+        pltpu.make_async_copy(source, target, sems.at[i])
+        for i, (source, target) in enumerate(
+            (
+                (act_hbm, act_ref),
+                (group_hbm, group_ref),
+                (occ_hbm, occ_ref),
+                (disp_hbm, disp_ref),
+                (load_hbm, load_ref),
+            )
+        )
+    ]
+    for copy in copies:
+        copy.start()
     rows, cols, depth = occ_ref.shape
     muscles = act_ref.shape[0]
+    even_y, even_z = even(axes[0]), even(axes[1])
+    for copy in copies:
+        copy.wait()
 
     def row(y, carry):
         group = group_ref[y]
@@ -259,32 +295,49 @@
         values += [occ_ref[y].astype(jnp.float32), level]
         for c, value in enumerate(values):
             block_ref[c, y] = value
-            zhi_ref[c, y] = value[:HIGH]
-            zlo_ref[c, y] = value[cols - LOW :]
+            bottom, top = value[:HIGH], value[cols - HIGH :]
+            zpair_ref[c, y] = jnp.where(even_z, top, bottom)
+            znext_ref[c, y] = jnp.where(even_z, bottom, top)
         return carry
 
     lax.fori_loop(0, rows, row, 0)
+    send_rows(block_ref, ypair_ref, ynext_ref, even_y)
+
+
+def send_rows(block_ref, pair_ref, next_ref, is_even):
+    rows = block_ref.shape[1]
+    pair_at = jnp.where(is_even, rows - HIGH, 0)
 
     def channel(c, carry):
         for y in range(HIGH):
-            yhi_ref[c, y] = block_ref[c, y]
-        for y in range(LOW):
-            ylo_ref[c, y] = block_ref[c, rows - LOW + y]
+            pair_ref[c, y] = block_ref[c, pair_at + y]
+            next_ref[c, y] = block_ref[c, rows - HIGH - pair_at + y]
         return carry
 
     lax.fori_loop(0, CHANNELS, channel, 0)
 
 
-def inner_kernel(axes, block_ref, zlo_ref, zhi_ref, ext, fields, terms, works, edge, last):
-    rows, depth = block_ref.shape[1], block_ref.shape[-1]
-    blank = jnp.zeros((1, depth), jnp.float32)
+def corner_kernel(axes, zpair_ref, znext_ref, around_ref, ypair_ref, ynext_ref):
+    even_y, even_z = even(axes[0]), even(axes[1])
+
+    def channel(c, carry):
+        for y in range(around_ref.shape[1]):
+            pair, far = zpair_ref[c, y], znext_ref[c, y]
+            around_ref[c, y, pl.ds(0, HIGH), :] = jnp.where(even_z, pair, far)
+            around_ref[c, y, pl.ds(HIGH, HIGH), :] = jnp.where(even_z, far, pair)
+        return carry
+
+    lax.fori_loop(0, CHANNELS, channel, 0)
+    send_rows(around_ref, ypair_ref, ynext_ref, even_y)
+
+
+def inner_kernel(axes, block_ref, around_ref, ext, fields, terms, works, edge, last):
+    rows = block_ref.shape[1]
 
     def assemble(c, carry):
         for y in range(rows):
             ext[c, LOW + y, pl.ds(0, SUB), :] = block_ref[c, y]
-            ext[c, LOW + y, pl.ds(SUB, HIGH), :] = zhi_ref[c, y]
-            ext[c, LOW + y, pl.ds(SUB + HIGH, 1), :] = blank
-            ext[c, LOW + y, pl.ds(2 * SUB - LOW, LOW), :] = zlo_ref[c, y]
+            ext[c, LOW + y, pl.ds(SUB, SUB), :] = around_ref[c, y]
         return carry
 
     lax.fori_loop(0, CHANNELS, assemble, 0)
@@ -301,10 +354,10 @@
 def outer_kernel(
     axes,
     group_ref,
-    ylo_ref,
-    yhi_ref,
-    clo_ref,
-    chi_ref,
+    ypair_ref,
+    ynext_ref,
+    cpair_ref,
+    cnext_ref,
     ext_in,
     fields_in,
     terms_in,
@@ -320,14 +373,15 @@
 ):
     del ext_in, fields_in, terms_in, works_in
     rows = group_ref.shape[0]
+    even_y = even(axes[0])
 
     def assemble(c, carry):
-        for q in range(LOW):
-            ext[c, q, pl.ds(0, SUB), :] = ylo_ref[c, q]
-            ext[c, q, pl.ds(SUB, SUB), :] = clo_ref[c, q]
-        for q in range(HIGH):
-            ext[c, LOW + rows + q, pl.ds(0, SUB), :] = yhi_ref[c, q]
-            ext[c, LOW + rows + q, pl.ds(SUB, SUB), :] = chi_ref[c, q]
+        for zt, pair_ref, next_ref in ((0, ypair_ref, ynext_ref), (1, cpair_ref, cnext_ref)):
+            for y in range(HIGH):
+                pair, far = pair_ref[c, y], next_ref[c, y]
+                ext[c, LOW + rows + y, pl.ds(SUB * zt, SUB), :] = jnp.where(even_y, pair, far)
+                if y >= HIGH - LOW:
+                    ext[c, y - HIGH + LOW, pl.ds(SUB * zt, SUB), :] = jnp.where(even_y, far, pair)
         return carry
 
     lax.fori_loop(0, CHANNELS, assemble, 0)
@@ -388,7 +442,7 @@
         sums_ref[pl.ds(SUB * i, SUB), :] = row
 
 
-def combine_kernel(muscles, scale, sums_ref, load_ref, fields, x_ref, grad_ref):
+def combine_kernel(muscles, scale, sums_ref, block_ref, fields, x_ref, grad_ref):
     total = jnp.sum(sums_ref[...], axis=0, keepdims=True)
     at = NB * muscles
     pairs = [(i, j) for i in range(NB) for j in range(i, NB)]
@@ -455,25 +509,24 @@
         grad = part if grad is None else grad + part
     grad_ref[...] = -scale * grad
 
-    width = load_ref.shape[-1]
+    width = block_ref.shape[-1]
     coef = [jnp.broadcast_to(x[k], (SUB, width)) for k in range(NB)]
 
     def row(y, carry):
         for comp in range(3):
-            value = coef[0] * load_ref[comp, y]
+            value = coef[0] * block_ref[3 + comp, y]
             for k in range(1, NB):
                 value = value + coef[k] * fields[k - 1, comp, LOW + y, pl.ds(0, SUB), :]
             x_ref[comp, y] = value
         return carry
 
-    lax.fori_loop(0, load_ref.shape[1], row, 0)
-
-
-def shift(shard, axis, by):
+    lax.fori_loop(0, block_ref.shape[1], row, 0)
+
+
+def swap(shard, axis, first):
     length = lax.axis_size(axis)
-    return lax.ppermute(
-        shard, axis, [(i, i + by) for i in range(length) if 0 <= i + by < length]
-    )
+    pairs = [(i, i + 1) for i in range(first, length - 1, 2)]
+    return lax.ppermute(shard, axis, pairs + [(j, i) for i, j in pairs])
 
 
 def per_device(displacement, load, occupancy, voxel_muscle_group, activation):
@@ -485,29 +538,48 @@
     def arr(*shape):
         return jax.ShapeDtypeStruct(shape, jnp.float32)
 
-    block, face_hi, face_lo, row_hi, row_lo = pl.pallas_call(
-        pack_kernel,
-        out_shape=(
-            arr(CHANNELS, rows, cols, depth),
-            arr(CHANNELS, rows, HIGH, depth),
-            arr(CHANNELS, rows, LOW, depth),
-            arr(CHANNELS, HIGH, cols, depth),
-            arr(CHANNELS, LOW, cols, depth),
-        ),
-        in_specs=[VMEM] * 4 + [SMEM],
+    anywhere = pl.BlockSpec(memory_space=pltpu.HBM)
+    faces = (arr(CHANNELS, rows, HIGH, depth),) * 2
+    edges = (arr(CHANNELS, HIGH, cols, depth),) * 2
+    block, zpair, znext, ypair, ynext = pl.pallas_call(
+        functools.partial(pack_kernel, axes),
+        out_shape=(arr(CHANNELS, rows, cols, depth), *faces, *edges),
+        in_specs=[anywhere] * 5,
         out_specs=(VMEM,) * 5,
+        scratch_shapes=[
+            pltpu.VMEM(displacement.shape, jnp.float32),
+            pltpu.VMEM(load.shape, jnp.float32),
+            pltpu.VMEM(occupancy.shape, jnp.int32),
+            pltpu.VMEM(occupancy.shape, jnp.int32),
+            pltpu.SMEM((muscles,), jnp.float32),
+            pltpu.SemaphoreType.DMA((5,)),
+        ],
         compiler_params=pltpu.CompilerParams(vmem_limit_bytes=32 << 20),
         name="pack",
-    )(displacement, load, occupancy, voxel_muscle_group, activation)
-
-    zhi = shift(face_hi, "gz", -1)
-    zlo = shift(face_lo, "gz", 1)
-    yhi = shift(row_hi, "gy", -1)
-    ylo = shift(row_lo, "gy", 1)
-    gap = jnp.zeros((CHANNELS, rows, 1, depth), jnp.float32)
-    around = jnp.concatenate([zhi, gap, zlo], axis=2)
-    chi = shift(around[:, :HIGH], "gy", -1)
-    clo = shift(around[:, rows - LOW :], "gy", 1)
+    )(
+        *(
+            pltpu.with_memory_space_constraint(value, pltpu.HBM)
+            for value in (displacement, load, occupancy, voxel_muscle_group, activation)
+        )
+    )
+
+    received = [
+        swap(znext, "gz", 1),
+        swap(zpair, "gz", 0),
+        swap(ynext, "gy", 1),
+        swap(ypair, "gy", 0),
+    ]
+    znext, zpair, ynext, ypair = lax.optimization_barrier(received)
+    around, cpair, cnext = pl.pallas_call(
+        functools.partial(corner_kernel, axes),
+        out_shape=(arr(CHANNELS, rows, 2 * HIGH, depth), *edges),
+        in_specs=[VMEM] * 2,
+        out_specs=(VMEM,) * 3,
+        compiler_params=pltpu.CompilerParams(vmem_limit_bytes=32 << 20),
+        name="corner",
+    )(zpair, znext)
+    cnext = swap(cnext, "gy", 1)
+    cpair = swap(cpair, "gy", 0)
 
     state = (
         arr(CHANNELS, count, 2 * SUB, depth),
@@ -519,12 +591,12 @@
     inner = pl.pallas_call(
         functools.partial(inner_kernel, axes),
         out_shape=(*state, arr(NB - 1, 2, 9, 2 * SUB, depth)),
-        in_specs=[VMEM] * 3,
+        in_specs=[VMEM] * 2,
         out_specs=(VMEM,) * 5,
         scratch_shapes=[kept],
         compiler_params=pltpu.CompilerParams(vmem_limit_bytes=32 << 20),
         name="inner",
-    )(block, zlo, zhi)
+    )(block, around)
 
     devices = lax.axis_size("gy") * lax.axis_size("gz")
     sums, _, fields, _, _ = pl.pallas_call(
@@ -536,7 +608,7 @@
         input_output_aliases={5: 1, 6: 2, 7: 3, 8: 4},
         compiler_params=pltpu.CompilerParams(vmem_limit_bytes=32 << 20),
         name="outer",
-    )(voxel_muscle_group, ylo, yhi, clo, chi, *inner)
+    )(voxel_muscle_group, ypair, ynext, cpair, cnext, *inner)
 
     every = lax.all_to_all(sums, ("gy", "gz"), 0, 0, tiled=True)
 
@@ -552,7 +624,7 @@
         out_specs=(VMEM, VMEM),
         compiler_params=pltpu.CompilerParams(vmem_limit_bytes=32 << 20),
         name="combine",
-    )(every, load, fields)
+    )(every, block, fields)
     return adjoint, muscle_grad.reshape(muscles)
 
 

time: 75.7 us -> 68.4 us (0.904)
  starting transfers between devices: 20.3 us -> 14 us
  waiting for transfers between devices: 0.02 us -> 3.94 us
  local copies, waits for them, and re-layouts: 4.59 us -> 1.12 us
  blocking collectives: 32.9 us -> 31.2 us
    ppermute x6, starting transfers between devices: 20.3 us -> 14 us  [swap(): return lax.ppermute(shard, axis, pairs + [(j, i) for i, j in pairs])]
    ppermute x6, waiting for transfers between devices: 0.02 us -> 3.94 us  [swap(): return lax.ppermute(shard, axis, pairs + [(j, i) for i, j in pairs])]
    unnamed x15 -> x3, local copies, waits for them, and re-layouts: 4.21 us -> 0.85 us
    all_to_all x1, blocking collectives: 32.9 us -> 31.2 us  [per_device(): every = lax.all_to_all(sums, ('gy', 'gz'), 0, 0, tiled=True)]
    pallas_call x1 -> x2, Pallas kernels: 0.92 us -> 1.73 us  [the longest x1 1.54 us: per_device(): pl.pallas_call(functools.partial(pack_kernel, axes), out_shape=(arr(CHANN...]
  transfers between devices with their start and end apart: 6 -> 6, of which waited for: 0 -> 2; matrix products, arithmetic and copies ran while one was open for 0% -> 0% of each run, Pallas kernels for 6% -> 6%
where the time goes in v3:
time: 68.4 us; the launch traced here: 68.1 us
  blocking collectives  31.2 us (46%)
  Pallas kernels  17.1 us (25%)
  starting transfers between devices  14 us (20%)
  waiting for transfers between devices  3.94 us (6%)
  local copies, waits for them, and re-layouts  1.12 us (2%)
  between operations  0.75 us (1%)
    all_to_all x1, blocking collectives, per_device(): every = lax.all_to_all(sums, ('gy', 'gz'), 0, 0, tiled=True)  31.2 us
    ppermute x6, starting transfers between devices, swap(): return lax.ppermute(shard, axis, pairs + [(j, i) for i, j in pairs])  14 us
    pallas_call x1, Pallas kernels, per_device(): pl.pallas_call(functools.partial(outer_kernel, axes), out_shape=(arr(devi...  8.78 us
    pallas_call x1, Pallas kernels, per_device(): pl.pallas_call(functools.partial(inner_kernel, axes), out_shape=(*state,...  4.28 us
    ppermute x6, waiting for transfers between devices, swap(): return lax.ppermute(shard, axis, pairs + [(j, i) for i, j in pairs])  3.94 us
    pallas_call x1, Pallas kernels, per_device(): pl.pallas_call(functools.partial(combine_kernel, muscles, scale), out_sha...  2.33 us
    pallas_call x1, Pallas kernels, per_device(): pl.pallas_call(functools.partial(pack_kernel, axes), out_shape=(arr(CHANN...  1.54 us
  transfers between devices with their start and end apart: 6, of which 2 were waited for; matrix products, arithmetic and copies ran while one was open for 0% of the time, Pallas kernels for 6%

profile of v3, /device:TPU:1, one launch (start us, length us, event | category | flops | bytes accessed | tf_op | source)
XLA Modules:
  0.0 68.1 jit_solution(17653267460151205575)
XLA Ops:
  0.6 1.5 %pack.1 = (f32[8,8,8,256]{3,2,1,0:T(8,128)S(1)}, f32[8,8,4,256]{3,2,1,0:T(4,128)S(1)}, f32[8,8,4,256]{3,2,1,0:T(4,128)S(1)}, f32[8,4,8,256]{3,2,1,0:T(8,128)S(1)}, f32[8,4,8,256]{3,2,1,0:T(8,128)S(1)}) custom-call(f32[3,8,8,256]{3,2,1,0:T(8,128)} %disp_hbm.1, f32[3,8,8,256]{3,2,1,0:T(8,128)} %load_hbm.1, s32[8,8,256]{2,1,0:T(8,128)} %occ_hbm.1, ...), custom_call_target="tpu_custom_call" | custom-call | tf_op jit(solution)/shard_map/pack/pallas_call | solution.py:544
  2.2 0.7 collective-permute-start
  2.9 4.6 %collective-permute-start.1 = (f32[8,8,4,256]{3,2,1,0:T(4,128)S(1)}, f32[8,8,4,256]{3,2,1,0:T(4,128)S(1)}, u32[]{:S(2)}, u32[]{:S(2)}) collective-permute-start(f32[8,8,4,256]{3,2,1,0:T(4,128)S(1)} %get-tuple-element.24), channel_id=1, source_target_pairs={{0,1},{2,3},{4,5},{6,7},{8,9},{10,11},{12,13},{14,15},{1,0},{3,2},... | collective-permute-start | bytes 786440 | tf_op jit(solution)/shard_map/ppermute | solution.py:529
  7.4 4.7 %collective-permute-start.2 = (f32[8,4,8,256]{3,2,1,0:T(8,128)S(1)}, f32[8,4,8,256]{3,2,1,0:T(8,128)S(1)}, u32[]{:S(2)}, u32[]{:S(2)}) collective-permute-start(f32[8,4,8,256]{3,2,1,0:T(8,128)S(1)} %get-tuple-element.25), channel_id=1, source_target_pairs={{16,32},{48,64},{80,96},{112,128},{144,160},{176,192},{208,224},{3... | collective-permute-start | bytes 786440 | tf_op jit(solution)/shard_map/ppermute | solution.py:529
  12.1 0.1 collective-permute-start.3
  12.2 0.0 collective-permute-done.znext_ref
  12.2 0.9 %collective-permute-done.1.zpair_ref = f32[8,8,4,256]{3,2,1,0:T(4,128)S(1)} collective-permute-done((f32[8,8,4,256]{3,2,1,0:T(4,128)S(1)}, f32[8,8,4,256]{3,2,1,0:T(4,128)S(1)}, u32[]{:S(2)}, u32[]{:S(2)}) %collective-permute-start.1) | collective-permute-done | bytes 262176 | tf_op jit(solution)/shard_map/ppermute | solution.py:529
  13.1 3.0 %collective-permute-done.2.ynext_ref = f32[8,4,8,256]{3,2,1,0:T(8,128)S(1)} collective-permute-done((f32[8,4,8,256]{3,2,1,0:T(8,128)S(1)}, f32[8,4,8,256]{3,2,1,0:T(8,128)S(1)}, u32[]{:S(2)}, u32[]{:S(2)}) %collective-permute-start.2) | collective-permute-done | bytes 262176 | tf_op jit(solution)/shard_map/ppermute | solution.py:529
  16.1 0.0 collective-permute-done.3.ypair_ref
  16.1 0.2 corner.1
  16.3 0.1 collective-permute-start.4
  16.4 3.9 %collective-permute-start.5 = (f32[8,4,8,256]{3,2,1,0:T(8,128)S(1)}, f32[8,4,8,256]{3,2,1,0:T(8,128)S(1)}, u32[]{:S(2)}, u32[]{:S(2)}) collective-permute-start(f32[8,4,8,256]{3,2,1,0:T(8,128)S(1)} %get-tuple-element.32), channel_id=1, source_target_pairs={{16,32},{48,64},{80,96},{112,128},{144,160},{176,192},{208,224},{3... | collective-permute-start | bytes 786440 | tf_op jit(solution)/shard_map/ppermute | solution.py:529
  20.4 4.3 %inner.1 = (f32[8,15,16,256]{3,2,1,0:T(8,128)S(1)}, f32[3,3,15,16,256]{4,3,2,1,0:T(8,128)S(1)}, f32[15,14,16,256]{3,2,1,0:T(8,128)S(1)}, f32[4,14,8,256]{3,2,1,0:T(8,128)S(1)}, f32[3,2,9,16,256]{4,3,2,1,0:T(8,128)S(1)}) custom-call(f32[8,8,8,256]{3,2,1,0:T(8,128)S(1)} %get-tuple-element.33.block_ref, f32[8,8,8,256]{3,2,1,0:T(8,128)S(1)} %get-tuple-element.34.around_ref), custom_call_target="tpu_custom_call" | custom-call | tf_op jit(solution)/shard_map/inner/pallas_call | solution.py:591
  24.7 0.0 collective-permute-done.4.cpair_ref
  24.7 0.0 collective-permute-done.5.cnext_ref
  24.7 0.0 copy-start
  24.7 0.8 %copy-done = s32[8,8,256]{2,1,0:T(8,128)S(1)} copy-done((s32[8,8,256]{2,1,0:T(8,128)S(1)}, s32[8,8,256]{2,1,0:T(8,128)}, u32[]{:S(2)}) %copy-start) | copy-done | bytes 65560
  25.5 8.8 %outer.1 = (f32[256,256]{1,0:T(8,128)S(1)}, f32[8,15,16,256]{3,2,1,0:T(8,128)S(1)}, f32[3,3,15,16,256]{4,3,2,1,0:T(8,128)S(1)}, f32[15,14,16,256]{3,2,1,0:T(8,128)S(1)}, f32[4,14,8,256]{3,2,1,0:T(8,128)S(1)}) custom-call(s32[8,8,256]{2,1,0:T(8,128)S(1)} %copy-done, ...), custom_call_target="tpu_custom_call", output_to_operand_aliasing={{1}: (5, {}), {2}: (6, {}), {3}: (7, {}), {4}: (8, {})} | custom-call | tf_op jit(solution)/shard_map/outer/pallas_call | solution.py:602
  34.3 0.3 copy.11
  34.6 31.2 %all_to_all.11 = f32[256,1,256]{2,1,0:T(1,128)S(1)} all-to-all(f32[256,1,256]{2,1,0:T(1,128)S(1)} %copy.11), channel_id=1, replica_groups=mesh['gy'=16,'gz'=16] {'gy','gz'}, dimensions={0} | all-to-all | bytes 524288 | tf_op jit(solution)/shard_map/all_to_all | solution.py:613
  65.8 2.3 %combine.1 = (f32[3,8,8,256]{3,2,1,0:T(8,128)}, f32[1,32]{1,0:T(1,128)}) custom-call(f32[256,256]{1,0:T(8,128)S(1)} %bitcast.5, f32[8,8,8,256]{3,2,1,0:T(8,128)S(1)} %get-tuple-element.33.block_ref, f32[3,3,15,16,256]{4,3,2,1,0:T(8,128)S(1)} %get-tuple-element.41.fields), custom_call_target="tpu_custom_call" | custom-call | tf_op jit(solution)/shard_map/combine/pallas_call | solution.py:617
  (1 shorter events, 0.0 us)
Async XLA Ops:
  2.2 10.0 %collective-permute-start = (f32[8,8,4,256]{3,2,1,0:T(4,128)S(1)}, f32[8,8,4,256]{3,2,1,0:T(4,128)S(1)}, u32[]{:S(2)}, u32[]{:S(2)}) collective-permute-start(f32[8,8,4,256]{3,2,1,0:T(4,128)S(1)} %get-tuple-element.23), channel_id=1, source_target_pairs={{1,2},{3,4},{5,6},{7,8},{9,10},{11,12},{13,14},{2,1},{4,3},{6,5},{... | collective-permute-start | bytes 786440 | tf_op jit(solution)/shard_map/ppermute | solution.py:529
  2.9 10.3 %collective-permute-start.1 = (f32[8,8,4,256]{3,2,1,0:T(4,128)S(1)}, f32[8,8,4,256]{3,2,1,0:T(4,128)S(1)}, u32[]{:S(2)}, u32[]{:S(2)}) collective-permute-start(f32[8,8,4,256]{3,2,1,0:T(4,128)S(1)} %get-tuple-element.24), channel_id=1, source_target_pairs={{0,1},{2,3},{4,5},{6,7},{8,9},{10,11},{12,13},{14,15},{1,0},{3,2},... | collective-permute-start | bytes 786440 | tf_op jit(solution)/shard_map/ppermute | solution.py:529
  7.4 8.7 %collective-permute-start.2 = (f32[8,4,8,256]{3,2,1,0:T(8,128)S(1)}, f32[8,4,8,256]{3,2,1,0:T(8,128)S(1)}, u32[]{:S(2)}, u32[]{:S(2)}) collective-permute-start(f32[8,4,8,256]{3,2,1,0:T(8,128)S(1)} %get-tuple-element.25), channel_id=1, source_target_pairs={{16,32},{48,64},{80,96},{112,128},{144,160},{176,192},{208,224},{3... | collective-permute-start | bytes 786440 | tf_op jit(solution)/shard_map/ppermute | solution.py:529
  12.1 4.0 %collective-permute-start.3 = (f32[8,4,8,256]{3,2,1,0:T(8,128)S(1)}, f32[8,4,8,256]{3,2,1,0:T(8,128)S(1)}, u32[]{:S(2)}, u32[]{:S(2)}) collective-permute-start(f32[8,4,8,256]{3,2,1,0:T(8,128)S(1)} %get-tuple-element.26), channel_id=1, source_target_pairs={{0,16},{32,48},{64,80},{96,112},{128,144},{160,176},{192,208},{224... | collective-permute-start | bytes 786440 | tf_op jit(solution)/shard_map/ppermute | solution.py:529
  16.3 8.3 %collective-permute-start.4 = (f32[8,4,8,256]{3,2,1,0:T(8,128)S(1)}, f32[8,4,8,256]{3,2,1,0:T(8,128)S(1)}, u32[]{:S(2)}, u32[]{:S(2)}) collective-permute-start(f32[8,4,8,256]{3,2,1,0:T(8,128)S(1)} %get-tuple-element.31), channel_id=1, source_target_pairs={{0,16},{32,48},{64,80},{96,112},{128,144},{160,176},{192,208},{224... | collective-permute-start | bytes 786440 | tf_op jit(solution)/shard_map/ppermute | solution.py:529
  16.4 8.2 %collective-permute-start.5 = (f32[8,4,8,256]{3,2,1,0:T(8,128)S(1)}, f32[8,4,8,256]{3,2,1,0:T(8,128)S(1)}, u32[]{:S(2)}, u32[]{:S(2)}) collective-permute-start(f32[8,4,8,256]{3,2,1,0:T(8,128)S(1)} %get-tuple-element.32), channel_id=1, source_target_pairs={{16,32},{48,64},{80,96},{112,128},{144,160},{176,192},{208,224},{3... | collective-permute-start | bytes 786440 | tf_op jit(solution)/shard_map/ppermute | solution.py:529
  24.7 0.8 %copy-start = (s32[8,8,256]{2,1,0:T(8,128)S(1)}, s32[8,8,256]{2,1,0:T(8,128)}, u32[]{:S(2)}) copy-start(s32[8,8,256]{2,1,0:T(8,128)} %group_ref.1) | copy-start | bytes 196612

commit v4 on v3

--- a/solution.py
+++ b/solution.py
@@ -259,10 +259,10 @@
     znext_ref,
     ypair_ref,
     ynext_ref,
+    group_ref,
     disp_ref,
     load_ref,
     occ_ref,
-    group_ref,
     act_ref,
     sems,
 ):
@@ -354,10 +354,10 @@
 def outer_kernel(
     axes,
     group_ref,
+    ynext_ref,
     ypair_ref,
-    ynext_ref,
+    cnext_ref,
     cpair_ref,
-    cnext_ref,
     ext_in,
     fields_in,
     terms_in,
@@ -442,7 +442,7 @@
         sums_ref[pl.ds(SUB * i, SUB), :] = row
 
 
-def combine_kernel(muscles, scale, sums_ref, block_ref, fields, x_ref, grad_ref):
+def combine_kernel(muscles, scale, sums_ref, block_ref, fields, x_hbm, grad_ref, x_ref, sems):
     total = jnp.sum(sums_ref[...], axis=0, keepdims=True)
     at = NB * muscles
     pairs = [(i, j) for i in range(NB) for j in range(i, NB)]
@@ -460,48 +460,21 @@
         form[i, last] = form[last, i] = SIGMA * gram[i + 1, last] + shifts[i] * gram[i, last]
     form[last, last] = SIGMA * energy + MASS * gram[last, last]
 
-    def quadratic(matrix, v):
-        parts = []
-        for i in range(NB):
-            if v[i] is None:
-                continue
-            inner = [matrix[i, j] * v[j] for j in range(NB) if v[j] is not None]
-            parts.append(v[i] * functools.reduce(lambda s, t: s + t, inner))
-        return functools.reduce(lambda s, t: s + t, parts)
-
-    one = jnp.ones((1, 1), jnp.float32)
+    rhs = [gram[0, i] for i in range(NB)]
+    inverse = []
+    for k in range(NB):
+        inverse.append(1.0 / form[k, k])
+        for i in range(k + 1, NB):
+            factor = form[k, i] * inverse[k]
+            rhs[i] = rhs[i] - factor * rhs[k]
+            for j in range(i, NB):
+                form[i, j] = form[i, j] - factor * form[k, j]
     x = [None] * NB
-    residual = [one] + [None] * (NB - 1)
-    direction = list(residual)
-    norm = gram[0, 0]
-
-    def axpy(a, u, v):
-        out = []
-        for s, t in zip(u, v):
-            if s is None:
-                out.append(t)
-            elif t is None:
-                out.append(a * s)
-            else:
-                out.append(t + a * s)
-        return out
-
-    for step in range(NB):
-        alpha = norm / quadratic(form, direction)
-        x = axpy(alpha, direction, x)
-        if step == NB - 1:
-            break
-        image = [None] * NB
-        for i in range(NB - 1):
-            if direction[i] is not None:
-                up = SIGMA * direction[i]
-                same = shifts[i] * direction[i]
-                image[i] = same if image[i] is None else image[i] + same
-                image[i + 1] = up if image[i + 1] is None else image[i + 1] + up
-        residual = axpy(-alpha, image, residual)
-        new = quadratic(gram, residual)
-        direction = axpy(new / norm, direction, residual)
-        norm = new
+    for k in reversed(range(NB)):
+        value = rhs[k]
+        for j in range(k + 1, NB):
+            value = value - form[k, j] * x[j]
+        x[k] = value * inverse[k]
 
     grad = None
     for k in range(NB):
@@ -511,16 +484,17 @@
 
     width = block_ref.shape[-1]
     coef = [jnp.broadcast_to(x[k], (SUB, width)) for k in range(NB)]
-
-    def row(y, carry):
-        for comp in range(3):
+    copies = []
+    for comp in range(3):
+        for y in range(block_ref.shape[1]):
             value = coef[0] * block_ref[3 + comp, y]
             for k in range(1, NB):
                 value = value + coef[k] * fields[k - 1, comp, LOW + y, pl.ds(0, SUB), :]
             x_ref[comp, y] = value
-        return carry
-
-    lax.fori_loop(0, block_ref.shape[1], row, 0)
+        copies.append(pltpu.make_async_copy(x_ref.at[comp], x_hbm.at[comp], sems.at[comp]))
+        copies[-1].start()
+    for copy in copies:
+        copy.wait()
 
 
 def swap(shard, axis, first):
@@ -541,15 +515,19 @@
     anywhere = pl.BlockSpec(memory_space=pltpu.HBM)
     faces = (arr(CHANNELS, rows, HIGH, depth),) * 2
     edges = (arr(CHANNELS, HIGH, cols, depth),) * 2
-    block, zpair, znext, ypair, ynext = pl.pallas_call(
+    block, zpair, znext, ypair, ynext, group = pl.pallas_call(
         functools.partial(pack_kernel, axes),
-        out_shape=(arr(CHANNELS, rows, cols, depth), *faces, *edges),
+        out_shape=(
+            arr(CHANNELS, rows, cols, depth),
+            *faces,
+            *edges,
+            jax.ShapeDtypeStruct(occupancy.shape, jnp.int32),
+        ),
         in_specs=[anywhere] * 5,
-        out_specs=(VMEM,) * 5,
+        out_specs=(VMEM,) * 6,
         scratch_shapes=[
             pltpu.VMEM(displacement.shape, jnp.float32),
             pltpu.VMEM(load.shape, jnp.float32),
-            pltpu.VMEM(occupancy.shape, jnp.int32),
             pltpu.VMEM(occupancy.shape, jnp.int32),
             pltpu.SMEM((muscles,), jnp.float32),
             pltpu.SemaphoreType.DMA((5,)),
@@ -608,7 +586,7 @@
         input_output_aliases={5: 1, 6: 2, 7: 3, 8: 4},
         compiler_params=pltpu.CompilerParams(vmem_limit_bytes=32 << 20),
         name="outer",
-    )(voxel_muscle_group, ypair, ynext, cpair, cnext, *inner)
+    )(group, ynext, ypair, cnext, cpair, *inner)
 
     every = lax.all_to_all(sums, ("gy", "gz"), 0, 0, tiled=True)
 
@@ -621,7 +599,8 @@
             jax.ShapeDtypeStruct((1, muscles), jnp.float32),
         ),
         in_specs=[VMEM] * 3,
-        out_specs=(VMEM, VMEM),
+        out_specs=(anywhere, VMEM),
+        scratch_shapes=[pltpu.VMEM(load.shape, jnp.float32), pltpu.SemaphoreType.DMA((3,))],
         compiler_params=pltpu.CompilerParams(vmem_limit_bytes=32 << 20),
         name="combine",
     )(every, block, fields)

time: 68.4 us -> 67.4 us (0.985)
  local copies, waits for them, and re-layouts: 1.12 us -> 0.29 us
    unnamed x3 -> x1, local copies, waits for them, and re-layouts: 0.85 us -> 0.02 us
where the time goes in v4:
time: 67.4 us; the launch traced here: 67.2 us
  blocking collectives  31.4 us (47%)
  Pallas kernels  17.1 us (25%)
  starting transfers between devices  13.7 us (20%)
  waiting for transfers between devices  3.94 us (6%)
  between operations  0.74 us (1%)
    all_to_all x1, blocking collectives, per_device(): every = lax.all_to_all(sums, ('gy', 'gz'), 0, 0, tiled=True)  31.4 us
    ppermute x6, starting transfers between devices, swap(): return lax.ppermute(shard, axis, pairs + [(j, i) for i, j in pairs])  13.7 us
    pallas_call x1, Pallas kernels, per_device(): pl.pallas_call(functools.partial(outer_kernel, axes), out_shape=(arr(devi...  8.8 us
    pallas_call x1, Pallas kernels, per_device(): pl.pallas_call(functools.partial(inner_kernel, axes), out_shape=(*state,...  4.28 us
    ppermute x6, waiting for transfers between devices, swap(): return lax.ppermute(shard, axis, pairs + [(j, i) for i, j in pairs])  3.94 us
    pallas_call x1, Pallas kernels, per_device(): pl.pallas_call(functools.partial(combine_kernel, muscles, scale), out_sha...  2.29 us
    pallas_call x1, Pallas kernels, per_device(): pl.pallas_call(functools.partial(pack_kernel, axes), out_shape=(arr(CHANN...  1.54 us
  transfers between devices with their start and end apart: 6, of which 2 were waited for; matrix products, arithmetic and copies ran while one was open for 0% of the time, Pallas kernels for 6%

profile of v4, /device:TPU:1, one launch (start us, length us, event | category | flops | bytes accessed | tf_op | source)
XLA Modules:
  0.0 67.2 jit_solution(2500075287195593587)
XLA Ops:
  0.6 1.5 %pack.1 = (f32[8,8,8,256]{3,2,1,0:T(8,128)S(1)}, f32[8,8,4,256]{3,2,1,0:T(4,128)S(1)}, f32[8,8,4,256]{3,2,1,0:T(4,128)S(1)}, f32[8,4,8,256]{3,2,1,0:T(8,128)S(1)...) custom-call(f32[3,8,8,256]{3,2,1,0:T(8,128)} %disp_hbm.1, f32[3,8,8,256]{3,2,1,0:T(8,128)} %load_hbm.1, ...), custom_call_target="tpu_custom_call" | custom-call | tf_op jit(solution)/shard_map/pack/pallas_call | solution.py:518
  2.2 0.7 %collective-permute-start = (f32[8,8,4,256]{3,2,1,0:T(4,128)S(1)}, f32[8,8,4,256]{3,2,1,0:T(4,128)S(1)}, u32[]{:S(2)}, u32[]{:S(2)}) collective-permute-start(f32[8,8,4,256]{3,2,1,0:T(4,128)S(1)} %get-tuple-element.25), channel_id=1, source_target_pairs={{1,2},{3,4},{5,6},{7,8},{9,10},{11,12},{13,14},{2,1},{4,3},{6,5},{... | collective-permute-start | bytes 786440 | tf_op jit(solution)/shard_map/ppermute | solution.py:503
  2.9 4.6 %collective-permute-start.1 = (f32[8,8,4,256]{3,2,1,0:T(4,128)S(1)}, f32[8,8,4,256]{3,2,1,0:T(4,128)S(1)}, u32[]{:S(2)}, u32[]{:S(2)}) collective-permute-start(f32[8,8,4,256]{3,2,1,0:T(4,128)S(1)} %get-tuple-element.26), channel_id=1, source_target_pairs={{0,1},{2,3},{4,5},{6,7},{8,9},{10,11},{12,13},{14,15},{1,0},{3,2},... | collective-permute-start | bytes 786440 | tf_op jit(solution)/shard_map/ppermute | solution.py:503
  7.4 4.7 %collective-permute-start.2 = (f32[8,4,8,256]{3,2,1,0:T(8,128)S(1)}, f32[8,4,8,256]{3,2,1,0:T(8,128)S(1)}, u32[]{:S(2)}, u32[]{:S(2)}) collective-permute-start(f32[8,4,8,256]{3,2,1,0:T(8,128)S(1)} %get-tuple-element.27), channel_id=1, source_target_pairs={{16,32},{48,64},{80,96},{112,128},{144,160},{176,192},{208,224},{3... | collective-permute-start | bytes 786440 | tf_op jit(solution)/shard_map/ppermute | solution.py:503
  12.1 0.1 collective-permute-start.3
  12.2 0.0 collective-permute-done.znext_ref
  12.2 0.9 %collective-permute-done.1.zpair_ref = f32[8,8,4,256]{3,2,1,0:T(4,128)S(1)} collective-permute-done((f32[8,8,4,256]{3,2,1,0:T(4,128)S(1)}, f32[8,8,4,256]{3,2,1,0:T(4,128)S(1)}, u32[]{:S(2)}, u32[]{:S(2)}) %collective-permute-start.1) | collective-permute-done | bytes 262176 | tf_op jit(solution)/shard_map/ppermute | solution.py:503
  13.1 3.0 %collective-permute-done.2.ynext_ref = f32[8,4,8,256]{3,2,1,0:T(8,128)S(1)} collective-permute-done((f32[8,4,8,256]{3,2,1,0:T(8,128)S(1)}, f32[8,4,8,256]{3,2,1,0:T(8,128)S(1)}, u32[]{:S(2)}, u32[]{:S(2)}) %collective-permute-start.2) | collective-permute-done | bytes 262176 | tf_op jit(solution)/shard_map/ppermute | solution.py:503
  16.1 0.0 collective-permute-done.3.ypair_ref
  16.1 0.2 corner.1
  16.3 3.6 %collective-permute-start.4 = (f32[8,4,8,256]{3,2,1,0:T(8,128)S(1)}, f32[8,4,8,256]{3,2,1,0:T(8,128)S(1)}, u32[]{:S(2)}, u32[]{:S(2)}) collective-permute-start(f32[8,4,8,256]{3,2,1,0:T(8,128)S(1)} %get-tuple-element.33), channel_id=1, source_target_pairs={{16,32},{48,64},{80,96},{112,128},{144,160},{176,192},{208,224},{3... | collective-permute-start | bytes 786440 | tf_op jit(solution)/shard_map/ppermute | solution.py:503
  20.0 0.1 collective-permute-start.5
  20.1 4.3 %inner.1 = (f32[8,15,16,256]{3,2,1,0:T(8,128)S(1)}, f32[3,3,15,16,256]{4,3,2,1,0:T(8,128)S(1)}, f32[15,14,16,256]{3,2,1,0:T(8,128)S(1)}, f32[4,14,8,256]{3,2,1,0:T(8,128)S(1)}, f32[3,2,9,16,256]{4,3,2,1,0:T(8,128)S(1)}) custom-call(f32[8,8,8,256]{3,2,1,0:T(8,128)S(1)} %get-tuple-element.35.block_ref, f32[8,8,8,256]{3,2,1,0:T(8,128)S(1)} %get-tuple-element.36.around_ref), custom_call_target="tpu_custom_call" | custom-call | tf_op jit(solution)/shard_map/inner/pallas_call | solution.py:569
  24.4 0.0 collective-permute-done.4.cnext_ref
  24.4 0.0 collective-permute-done.5.cpair_ref
  24.4 8.8 %outer.1 = (f32[256,256]{1,0:T(8,128)S(1)}, f32[8,15,16,256]{3,2,1,0:T(8,128)S(1)}, f32[3,3,15,16,256]{4,3,2,1,0:T(8,128)S(1)}, f32[15,14,16,256]{3,2,1,0:T(8,128)S(1)}, f32[4,14,8,256]{3,2,1,0:T(8,128)S(1)}) custom-call(s32[8,8,256]{2,1,0:T(8,128)S(1)} %get-tuple-element.24.group_ref, ...), custom_call_target="tpu_custom_call", output_to_operand_aliasing={{1}: (5, {}), {2}: (6, {}), {3}: (7, {}), {4}: (8, {})} | custom-call | tf_op jit(solution)/shard_map/outer/pallas_call | solution.py:580
  33.2 0.3 copy.11
  33.5 31.4 %all_to_all.11 = f32[256,1,256]{2,1,0:T(1,128)S(1)} all-to-all(f32[256,1,256]{2,1,0:T(1,128)S(1)} %copy.11), channel_id=1, replica_groups=mesh['gy'=16,'gz'=16] {'gy','gz'}, dimensions={0} | all-to-all | bytes 524288 | tf_op jit(solution)/shard_map/all_to_all | solution.py:591
  64.9 2.3 %combine.1 = (f32[3,8,8,256]{3,2,1,0:T(8,128)}, f32[1,32]{1,0:T(1,128)}) custom-call(f32[256,256]{1,0:T(8,128)S(1)} %bitcast.5, f32[8,8,8,256]{3,2,1,0:T(8,128)S(1)} %get-tuple-element.35.block_ref, f32[3,3,15,16,256]{4,3,2,1,0:T(8,128)S(1)} %get-tuple-element.43.fields), custom_call_target="tpu_custom_call" | custom-call | tf_op jit(solution)/shard_map/combine/pallas_call | solution.py:595
  (1 shorter events, 0.0 us)
Async XLA Ops:
  2.2 10.0 %collective-permute-start = (f32[8,8,4,256]{3,2,1,0:T(4,128)S(1)}, f32[8,8,4,256]{3,2,1,0:T(4,128)S(1)}, u32[]{:S(2)}, u32[]{:S(2)}) collective-permute-start(f32[8,8,4,256]{3,2,1,0:T(4,128)S(1)} %get-tuple-element.25), channel_id=1, source_target_pairs={{1,2},{3,4},{5,6},{7,8},{9,10},{11,12},{13,14},{2,1},{4,3},{6,5},{... | collective-permute-start | bytes 786440 | tf_op jit(solution)/shard_map/ppermute | solution.py:503
  2.9 10.3 %collective-permute-start.1 = (f32[8,8,4,256]{3,2,1,0:T(4,128)S(1)}, f32[8,8,4,256]{3,2,1,0:T(4,128)S(1)}, u32[]{:S(2)}, u32[]{:S(2)}) collective-permute-start(f32[8,8,4,256]{3,2,1,0:T(4,128)S(1)} %get-tuple-element.26), channel_id=1, source_target_pairs={{0,1},{2,3},{4,5},{6,7},{8,9},{10,11},{12,13},{14,15},{1,0},{3,2},... | collective-permute-start | bytes 786440 | tf_op jit(solution)/shard_map/ppermute | solution.py:503
  7.4 8.7 %collective-permute-start.2 = (f32[8,4,8,256]{3,2,1,0:T(8,128)S(1)}, f32[8,4,8,256]{3,2,1,0:T(8,128)S(1)}, u32[]{:S(2)}, u32[]{:S(2)}) collective-permute-start(f32[8,4,8,256]{3,2,1,0:T(8,128)S(1)} %get-tuple-element.27), channel_id=1, source_target_pairs={{16,32},{48,64},{80,96},{112,128},{144,160},{176,192},{208,224},{3... | collective-permute-start | bytes 786440 | tf_op jit(solution)/shard_map/ppermute | solution.py:503
  12.1 4.0 %collective-permute-start.3 = (f32[8,4,8,256]{3,2,1,0:T(8,128)S(1)}, f32[8,4,8,256]{3,2,1,0:T(8,128)S(1)}, u32[]{:S(2)}, u32[]{:S(2)}) collective-permute-start(f32[8,4,8,256]{3,2,1,0:T(8,128)S(1)} %get-tuple-element.28), channel_id=1, source_target_pairs={{0,16},{32,48},{64,80},{96,112},{128,144},{160,176},{192,208},{224... | collective-permute-start | bytes 786440 | tf_op jit(solution)/shard_map/ppermute | solution.py:503
  16.3 8.0 %collective-permute-start.4 = (f32[8,4,8,256]{3,2,1,0:T(8,128)S(1)}, f32[8,4,8,256]{3,2,1,0:T(8,128)S(1)}, u32[]{:S(2)}, u32[]{:S(2)}) collective-permute-start(f32[8,4,8,256]{3,2,1,0:T(8,128)S(1)} %get-tuple-element.33), channel_id=1, source_target_pairs={{16,32},{48,64},{80,96},{112,128},{144,160},{176,192},{208,224},{3... | collective-permute-start | bytes 786440 | tf_op jit(solution)/shard_map/ppermute | solution.py:503
  20.0 4.4 %collective-permute-start.5 = (f32[8,4,8,256]{3,2,1,0:T(8,128)S(1)}, f32[8,4,8,256]{3,2,1,0:T(8,128)S(1)}, u32[]{:S(2)}, u32[]{:S(2)}) collective-permute-start(f32[8,4,8,256]{3,2,1,0:T(8,128)S(1)} %get-tuple-element.34), channel_id=1, source_target_pairs={{0,16},{32,48},{64,80},{96,112},{128,144},{160,176},{192,208},{224... | collective-permute-start | bytes 786440 | tf_op jit(solution)/shard_map/ppermute | solution.py:503

commit v5 on v4

--- a/solution.py
+++ b/solution.py
@@ -438,18 +438,26 @@
         precision=lax.Precision.HIGHEST,
         preferred_element_type=jnp.float32,
     )
+    is_first = lax.rem(sweep.sh.sub, 2) == 0
+    message = jnp.where(is_first, row[:, :LANES], row[:, LANES:])
     for i in range(sums_ref.shape[0] // SUB):
-        sums_ref[pl.ds(SUB * i, SUB), :] = row
-
-
-def combine_kernel(muscles, scale, sums_ref, block_ref, fields, x_hbm, grad_ref, x_ref, sems):
-    total = jnp.sum(sums_ref[...], axis=0, keepdims=True)
-    at = NB * muscles
+        sums_ref[pl.ds(SUB * i, SUB), :] = message
+
+
+def combine_kernel(muscles, scale, sums_ref, block_ref, fields, x_hbm, grad_hbm, x_ref, grad_ref, sems):
+    parts = [sums_ref[pl.ds(SUB * i, SUB), :] for i in range(sums_ref.shape[0] // SUB)]
+    while len(parts) > 1:
+        odd = parts[len(parts) // 2 * 2 :]
+        parts = [a + b for a, b in zip(parts[0::2], parts[1::2])] + odd
+    total = parts[0]
+    is_first = lax.rem(lax.broadcasted_iota(jnp.int32, total.shape, 0), 2) == 0
+    works = jnp.sum(jnp.where(is_first, total, 0.0), axis=0, keepdims=True)
+    dots = jnp.sum(jnp.where(is_first, 0.0, total), axis=0, keepdims=True)
     pairs = [(i, j) for i in range(NB) for j in range(i, NB)]
     gram = {}
     for n, (i, j) in enumerate(pairs):
-        gram[i, j] = gram[j, i] = total[:, at + n : at + n + 1]
-    energy = total[:, at + len(pairs) : at + len(pairs) + 1]
+        gram[i, j] = gram[j, i] = dots[:, n : n + 1]
+    energy = dots[:, len(pairs) : len(pairs) + 1]
     shifts = [MASS + s for s in SHIFTS]
     form = {}
     for j in range(NB - 1):
@@ -478,13 +486,14 @@
 
     grad = None
     for k in range(NB):
-        part = x[k] * total[:, k * muscles : (k + 1) * muscles]
+        part = x[k] * works[:, k * muscles : (k + 1) * muscles]
         grad = part if grad is None else grad + part
     grad_ref[...] = -scale * grad
+    copies = [pltpu.make_async_copy(grad_ref, grad_hbm, sems.at[3])]
+    copies[0].start()
 
     width = block_ref.shape[-1]
     coef = [jnp.broadcast_to(x[k], (SUB, width)) for k in range(NB)]
-    copies = []
     for comp in range(3):
         for y in range(block_ref.shape[1]):
             value = coef[0] * block_ref[3 + comp, y]
@@ -547,7 +556,8 @@
         swap(ynext, "gy", 1),
         swap(ypair, "gy", 0),
     ]
-    znext, zpair, ynext, ypair = lax.optimization_barrier(received)
+    znext, zpair, ynext, ypair = received
+    znext, zpair = lax.optimization_barrier((znext, zpair))
     around, cpair, cnext = pl.pallas_call(
         functools.partial(corner_kernel, axes),
         out_shape=(arr(CHANNELS, rows, 2 * HIGH, depth), *edges),
@@ -579,7 +589,7 @@
     devices = lax.axis_size("gy") * lax.axis_size("gz")
     sums, _, fields, _, _ = pl.pallas_call(
         functools.partial(outer_kernel, axes),
-        out_shape=(arr(devices, 2 * NB * muscles), *state),
+        out_shape=(arr(2 * devices, LANES), *state),
         in_specs=[VMEM] * 10,
         out_specs=(VMEM,) * 5,
         scratch_shapes=[kept, pltpu.VMEM((2 * NB * muscles, LANES), jnp.float32)],
@@ -599,8 +609,12 @@
             jax.ShapeDtypeStruct((1, muscles), jnp.float32),
         ),
         in_specs=[VMEM] * 3,
-        out_specs=(anywhere, VMEM),
-        scratch_shapes=[pltpu.VMEM(load.shape, jnp.float32), pltpu.SemaphoreType.DMA((3,))],
+        out_specs=(anywhere, anywhere),
+        scratch_shapes=[
+            pltpu.VMEM(load.shape, jnp.float32),
+            pltpu.VMEM((1, muscles), jnp.float32),
+            pltpu.SemaphoreType.DMA((4,)),
+        ],
         compiler_params=pltpu.CompilerParams(vmem_limit_bytes=32 << 20),
         name="combine",
     )(every, block, fields)

time: 67.4 us -> 65.1 us (0.966)
  waiting for transfers between devices: 3.94 us -> 0.95 us
  starting transfers between devices: 13.7 us -> 15.1 us
    ppermute x6, waiting for transfers between devices: 3.94 us -> 0.95 us  [swap(): return lax.ppermute(shard, axis, pairs + [(j, i) for i, j in pairs])]
    ppermute x6, starting transfers between devices: 13.7 us -> 15.1 us  [swap(): return lax.ppermute(shard, axis, pairs + [(j, i) for i, j in pairs])]
  transfers between devices with their start and end apart: 6 -> 6, of which waited for: 2 -> 1; matrix products, arithmetic and copies ran while one was open for 0% -> 0% of each run, Pallas kernels for 6% -> 7%
where the time goes in v5:
time: 65.1 us; the launch traced here: 64.9 us
  blocking collectives  31.5 us (48%)
  Pallas kernels  16.6 us (25%)
  starting transfers between devices  15.1 us (23%)
  waiting for transfers between devices  0.95 us (1%)
  between operations  0.74 us (1%)
    all_to_all x1, blocking collectives, per_device(): every = lax.all_to_all(sums, ('gy', 'gz'), 0, 0, tiled=True)  31.5 us
    ppermute x6, starting transfers between devices, swap(): return lax.ppermute(shard, axis, pairs + [(j, i) for i, j in pairs])  15.1 us
    pallas_call x1, Pallas kernels, per_device(): pl.pallas_call(functools.partial(outer_kernel, axes), out_shape=(arr(2 *...  8.8 us
    pallas_call x1, Pallas kernels, per_device(): pl.pallas_call(functools.partial(inner_kernel, axes), out_shape=(*state,...  4.28 us
    pallas_call x1, Pallas kernels, per_device(): pl.pallas_call(functools.partial(combine_kernel, muscles, scale), out_sha...  1.81 us
    pallas_call x1, Pallas kernels, per_device(): pl.pallas_call(functools.partial(pack_kernel, axes), out_shape=(arr(CHANN...  1.54 us
  transfers between devices with their start and end apart: 6, of which 1 were waited for; matrix products, arithmetic and copies ran while one was open for 0% of the time, Pallas kernels for 7%

profile of v5, /device:TPU:1, one launch (start us, length us, event | category | flops | bytes accessed | tf_op | source)
XLA Modules:
  0.0 64.9 jit_solution(475829173241720700)
XLA Ops:
  0.6 1.5 %pack.1 = (f32[8,8,8,256]{3,2,1,0:T(8,128)S(1)}, f32[8,8,4,256]{3,2,1,0:T(4,128)S(1)}, f32[8,8,4,256]{3,2,1,0:T(4,128)S(1)}, f32[8,4,8,256]{3,2,1,0:T(8,128)S(1)...) custom-call(f32[3,8,8,256]{3,2,1,0:T(8,128)} %disp_hbm.1, f32[3,8,8,256]{3,2,1,0:T(8,128)} %load_hbm.1, ...), custom_call_target="tpu_custom_call" | custom-call | tf_op jit(solution)/shard_map/pack/pallas_call | solution.py:527
  2.2 0.7 %collective-permute-start.2 = (f32[8,8,4,256]{3,2,1,0:T(4,128)S(1)}, f32[8,8,4,256]{3,2,1,0:T(4,128)S(1)}, u32[]{:S(2)}, u32[]{:S(2)}) collective-permute-start(f32[8,8,4,256]{3,2,1,0:T(4,128)S(1)} %get-tuple-element.25), channel_id=1, source_target_pairs={{1,2},{3,4},{5,6},{7,8},{9,10},{11,12},{13,14},{2,1},{4,3},{6,5},{... | collective-permute-start | bytes 786440 | tf_op jit(solution)/shard_map/ppermute | solution.py:512
  2.9 4.6 %collective-permute-start.3 = (f32[8,8,4,256]{3,2,1,0:T(4,128)S(1)}, f32[8,8,4,256]{3,2,1,0:T(4,128)S(1)}, u32[]{:S(2)}, u32[]{:S(2)}) collective-permute-start(f32[8,8,4,256]{3,2,1,0:T(4,128)S(1)} %get-tuple-element.26), channel_id=1, source_target_pairs={{0,1},{2,3},{4,5},{6,7},{8,9},{10,11},{12,13},{14,15},{1,0},{3,2},... | collective-permute-start | bytes 786440 | tf_op jit(solution)/shard_map/ppermute | solution.py:512
  7.4 4.7 %collective-permute-start = (f32[8,4,8,256]{3,2,1,0:T(8,128)S(1)}, f32[8,4,8,256]{3,2,1,0:T(8,128)S(1)}, u32[]{:S(2)}, u32[]{:S(2)}) collective-permute-start(f32[8,4,8,256]{3,2,1,0:T(8,128)S(1)} %get-tuple-element.23), channel_id=1, source_target_pairs={{16,32},{48,64},{80,96},{112,128},{144,160},{176,192},{208,224},{3... | collective-permute-start | bytes 786440 | tf_op jit(solution)/shard_map/ppermute | solution.py:512
  12.1 0.1 collective-permute-start.1
  12.2 0.0 collective-permute-done.2.znext_ref
  12.2 0.9 %collective-permute-done.3.zpair_ref = f32[8,8,4,256]{3,2,1,0:T(4,128)S(1)} collective-permute-done((f32[8,8,4,256]{3,2,1,0:T(4,128)S(1)}, f32[8,8,4,256]{3,2,1,0:T(4,128)S(1)}, u32[]{:S(2)}, u32[]{:S(2)}) %collective-permute-start.3) | collective-permute-done | bytes 262176 | tf_op jit(solution)/shard_map/ppermute | solution.py:512
  13.1 0.2 corner.1
  13.3 5.0 %collective-permute-start.4 = (f32[8,4,8,256]{3,2,1,0:T(8,128)S(1)}, f32[8,4,8,256]{3,2,1,0:T(8,128)S(1)}, u32[]{:S(2)}, u32[]{:S(2)}) collective-permute-start(f32[8,4,8,256]{3,2,1,0:T(8,128)S(1)} %get-tuple-element.29), channel_id=1, source_target_pairs={{16,32},{48,64},{80,96},{112,128},{144,160},{176,192},{208,224},{3... | collective-permute-start | bytes 786440 | tf_op jit(solution)/shard_map/ppermute | solution.py:512
  18.3 0.1 collective-permute-start.5
  18.4 4.3 %inner.1 = (f32[8,15,16,256]{3,2,1,0:T(8,128)S(1)}, f32[3,3,15,16,256]{4,3,2,1,0:T(8,128)S(1)}, f32[15,14,16,256]{3,2,1,0:T(8,128)S(1)}, f32[4,14,8,256]{3,2,1,0:T(8,128)S(1)}, f32[3,2,9,16,256]{4,3,2,1,0:T(8,128)S(1)}) custom-call(f32[8,8,8,256]{3,2,1,0:T(8,128)S(1)} %get-tuple-element.31.block_ref, f32[8,8,8,256]{3,2,1,0:T(8,128)S(1)} %get-tuple-element.32.around_ref), custom_call_target="tpu_custom_call" | custom-call | tf_op jit(solution)/shard_map/inner/pallas_call | solution.py:579
  22.7 0.0 collective-permute-done.ynext_ref
  22.7 0.0 collective-permute-done.1.ypair_ref
  22.7 0.0 collective-permute-done.4.cnext_ref
  22.8 0.0 collective-permute-done.5.cpair_ref
  22.8 8.8 %outer.1 = (f32[512,128]{1,0:T(8,128)S(1)}, f32[8,15,16,256]{3,2,1,0:T(8,128)S(1)}, f32[3,3,15,16,256]{4,3,2,1,0:T(8,128)S(1)}, f32[15,14,16,256]{3,2,1,0:T(8,128)S(1)}, f32[4,14,8,256]{3,2,1,0:T(8,128)S(1)}) custom-call(s32[8,8,256]{2,1,0:T(8,128)S(1)} %get-tuple-element.22.group_ref, ...), custom_call_target="tpu_custom_call", output_to_operand_aliasing={{1}: (5, {}), {2}: (6, {}), {3}: (7, {}), {4}: (8, {})} | custom-call | tf_op jit(solution)/shard_map/outer/pallas_call | solution.py:590
  31.6 31.5 %all_to_all.11 = f32[256,2,128]{2,1,0:T(2,128)S(1)} all-to-all(f32[256,2,128]{2,1,0:T(2,128)S(1)} %bitcast.4), channel_id=1, replica_groups=mesh['gy'=16,'gz'=16] {'gy','gz'}, dimensions={0} | all-to-all | bytes 524288 | tf_op jit(solution)/shard_map/all_to_all | solution.py:601
  63.1 1.8 %combine.1 = (f32[3,8,8,256]{3,2,1,0:T(8,128)}, f32[1,32]{1,0:T(1,128)}) custom-call(f32[512,128]{1,0:T(8,128)S(1)} %bitcast.3, f32[8,8,8,256]{3,2,1,0:T(8,128)S(1)} %get-tuple-element.31.block_ref, f32[3,3,15,16,256]{4,3,2,1,0:T(8,128)S(1)} %get-tuple-element.39.fields), custom_call_target="tpu_custom_call" | custom-call | tf_op jit(solution)/shard_map/combine/pallas_call | solution.py:605
Async XLA Ops:
  2.2 10.0 %collective-permute-start.2 = (f32[8,8,4,256]{3,2,1,0:T(4,128)S(1)}, f32[8,8,4,256]{3,2,1,0:T(4,128)S(1)}, u32[]{:S(2)}, u32[]{:S(2)}) collective-permute-start(f32[8,8,4,256]{3,2,1,0:T(4,128)S(1)} %get-tuple-element.25), channel_id=1, source_target_pairs={{1,2},{3,4},{5,6},{7,8},{9,10},{11,12},{13,14},{2,1},{4,3},{6,5},{... | collective-permute-start | bytes 786440 | tf_op jit(solution)/shard_map/ppermute | solution.py:512
  2.9 10.3 %collective-permute-start.3 = (f32[8,8,4,256]{3,2,1,0:T(4,128)S(1)}, f32[8,8,4,256]{3,2,1,0:T(4,128)S(1)}, u32[]{:S(2)}, u32[]{:S(2)}) collective-permute-start(f32[8,8,4,256]{3,2,1,0:T(4,128)S(1)} %get-tuple-element.26), channel_id=1, source_target_pairs={{0,1},{2,3},{4,5},{6,7},{8,9},{10,11},{12,13},{14,15},{1,0},{3,2},... | collective-permute-start | bytes 786440 | tf_op jit(solution)/shard_map/ppermute | solution.py:512
  7.4 15.3 %collective-permute-start = (f32[8,4,8,256]{3,2,1,0:T(8,128)S(1)}, f32[8,4,8,256]{3,2,1,0:T(8,128)S(1)}, u32[]{:S(2)}, u32[]{:S(2)}) collective-permute-start(f32[8,4,8,256]{3,2,1,0:T(8,128)S(1)} %get-tuple-element.23), channel_id=1, source_target_pairs={{16,32},{48,64},{80,96},{112,128},{144,160},{176,192},{208,224},{3... | collective-permute-start | bytes 786440 | tf_op jit(solution)/shard_map/ppermute | solution.py:512
  12.1 10.6 %collective-permute-start.1 = (f32[8,4,8,256]{3,2,1,0:T(8,128)S(1)}, f32[8,4,8,256]{3,2,1,0:T(8,128)S(1)}, u32[]{:S(2)}, u32[]{:S(2)}) collective-permute-start(f32[8,4,8,256]{3,2,1,0:T(8,128)S(1)} %get-tuple-element.24), channel_id=1, source_target_pairs={{0,16},{32,48},{64,80},{96,112},{128,144},{160,176},{192,208},{224... | collective-permute-start | bytes 786440 | tf_op jit(solution)/shard_map/ppermute | solution.py:512
  13.3 9.4 %collective-permute-start.4 = (f32[8,4,8,256]{3,2,1,0:T(8,128)S(1)}, f32[8,4,8,256]{3,2,1,0:T(8,128)S(1)}, u32[]{:S(2)}, u32[]{:S(2)}) collective-permute-start(f32[8,4,8,256]{3,2,1,0:T(8,128)S(1)} %get-tuple-element.29), channel_id=1, source_target_pairs={{16,32},{48,64},{80,96},{112,128},{144,160},{176,192},{208,224},{3... | collective-permute-start | bytes 786440 | tf_op jit(solution)/shard_map/ppermute | solution.py:512
  18.3 4.4 %collective-permute-start.5 = (f32[8,4,8,256]{3,2,1,0:T(8,128)S(1)}, f32[8,4,8,256]{3,2,1,0:T(8,128)S(1)}, u32[]{:S(2)}, u32[]{:S(2)}) collective-permute-start(f32[8,4,8,256]{3,2,1,0:T(8,128)S(1)} %get-tuple-element.30), channel_id=1, source_target_pairs={{0,16},{32,48},{64,80},{96,112},{128,144},{160,176},{192,208},{224... | collective-permute-start | bytes 786440 | tf_op jit(solution)/shard_map/ppermute | solution.py:512

commit v6 on v5

--- a/solution.py
+++ b/solution.py
@@ -93,28 +93,32 @@
     return {k: a[k] - b[k] for k in a}
 
 
-def raw_gradient(sh, read, q, keys=ALL):
+def raw_gradient(sh, read, q, keys=ALL, cache=None):
+    def level(comp, at):
+        if cache is not None and (comp, at) in cache:
+            return cache[comp, at]
+        value = read(comp, at)
+        value_x = sh.xup(value)
+        wide, slope = add(value, value_x), sub(value_x, value)
+        wide_z, slope_z = sh.zup(wide, keys), sh.zup(slope, keys)
+        out = (
+            {k: slope[k] + slope_z[k] for k in keys},
+            {k: wide[k] + wide_z[k] for k in keys},
+            {k: wide_z[k] - wide[k] for k in keys},
+        )
+        if cache is not None:
+            cache[comp, at] = out
+        return out
+
     result = []
     for comp in range(3):
-        here, above = read(comp, q), read(comp, q + 1)
-        both, step = add(here, above), sub(above, here)
-        both_x, step_x = sh.xup(both), sh.xup(step)
-        wide, slope, rise = add(both, both_x), sub(both_x, both), add(step, step_x)
-        result.append(
-            tuple(
-                {k: up[k] + sign * v[k] if sign > 0 else up[k] - v[k] for k in keys}
-                for v, up, sign in (
-                    (slope, sh.zup(slope, keys), 1),
-                    (rise, sh.zup(rise, keys), 1),
-                    (wide, sh.zup(wide, keys), -1),
-                )
-            )
-        )
+        here, above = level(comp, q), level(comp, q + 1)
+        result.append((add(here[0], above[0]), sub(above[1], here[1]), add(here[2], above[2])))
     return result
 
 
-def row_terms(sh, ext, terms, q):
-    grad = raw_gradient(sh, lambda comp, at: get(ext, comp, at), q)
+def row_terms(sh, ext, terms, q, cache):
+    grad = raw_gradient(sh, lambda comp, at: get(ext, comp, at), q, ALL, cache)
     for k in ALL:
         occ, level = ext[(6, q, *part(k))], ext[(7, q, *part(k))]
         deform = [
@@ -198,11 +202,13 @@
 
 
 class Sweep:
-    def __init__(self, axes, rows, ext, fields, terms, works, last):
+    def __init__(self, axes, rows, ext, fields, terms, works):
         self.sh = Shifts()
-        self.ext, self.fields, self.terms, self.works, self.last = ext, fields, terms, works, last
+        self.ext, self.fields, self.terms, self.works = ext, fields, terms, works
         ends = [lax.axis_index(axis) == lax.axis_size(axis) - 1 for axis in axes]
-        self.top_y = jnp.where(ends[0], LOW + rows, -1)
+        self.top = LOW + rows
+        self.cache = {i: {} for i in range(-1, NB)}
+        self.keep_y = jnp.where(ends[0], 0.0, 1.0)
         top_z = jnp.where(ends[1], SUB, -1)
         self.keep_z = {k: jnp.where(self.sh.sub + SUB * k[0] == top_z, 0.0, 1.0) for k in ALL}
 
@@ -213,34 +219,27 @@
 
     def rate(self, step, q):
         if step == 0:
-            row_terms(self.sh, self.ext, self.terms, q)
-        grad = raw_gradient(self.sh, self.read(step), q)
+            row_terms(self.sh, self.ext, self.terms, q, self.cache[-1])
+        grad = raw_gradient(self.sh, self.read(step), q, ALL, self.cache[step])
         return row_rate(grad, self.terms, self.works, step, q)
 
-    def node(self, step, q, rate):
-        before = load_rate(self.last)
-        keep_y = jnp.where(q == self.top_y, 0.0, 1.0)
+    def node(self, step, q, before, rate):
         for comp in range(3):
             force = row_force(self.sh, before, rate, comp)
             if SHIFTS[step] != 0.0:
                 here = self.read(step)(comp, q)
                 force = {k: force[k] - (SHIFTS[step] / SIGMA) * here[k] for k in ALL}
-            put(
-                self.fields,
-                {k: force[k] * (self.keep_z[k] * keep_y) for k in ALL},
-                step,
-                comp,
-                q,
-            )
-
-    def rows(self, step, start, stop):
-        def body(q, carry):
+            if q == self.top:
+                force = {k: force[k] * self.keep_y for k in ALL}
+            force = {k: force[k] * self.keep_z[k] if k[0] else force[k] for k in ALL}
+            put(self.fields, force, step, comp, q)
+
+    def rows(self, step, start, stop, before):
+        for q in range(start, stop):
             rate = self.rate(step, q)
-            self.node(step, q, rate)
-            save_rate(self.last, rate)
-            return carry
-
-        lax.fori_loop(start, stop, body, 0)
+            self.node(step, q, before, rate)
+            before = rate
+        return before
 
 
 def even(axis):
@@ -331,7 +330,7 @@
     send_rows(around_ref, ypair_ref, ynext_ref, even_y)
 
 
-def inner_kernel(axes, block_ref, around_ref, ext, fields, terms, works, edge, last):
+def inner_kernel(axes, block_ref, around_ref, ext, fields, terms, works, edge):
     rows = block_ref.shape[1]
 
     def assemble(c, carry):
@@ -341,14 +340,12 @@
         return carry
 
     lax.fori_loop(0, CHANNELS, assemble, 0)
-    sweep = Sweep(axes, rows, ext, fields, terms, works, last)
+    sweep = Sweep(axes, rows, ext, fields, terms, works)
     for step in range(NB - 1):
         first, final = LOW + step, LOW + rows - 2 - step
         rate = sweep.rate(step, first)
-        save_rate(last, rate)
         save_rate(edge, rate, step, 0)
-        sweep.rows(step, first + 1, final + 1)
-        save_rate(edge, load_rate(last), step, 1)
+        save_rate(edge, sweep.rows(step, first + 1, final + 1, rate), step, 1)
 
 
 def outer_kernel(
@@ -368,7 +365,6 @@
     fields,
     terms,
     works,
-    last,
     table,
 ):
     del ext_in, fields_in, terms_in, works_in
@@ -385,20 +381,19 @@
         return carry
 
     lax.fori_loop(0, CHANNELS, assemble, 0)
-    sweep = Sweep(axes, rows, ext, fields, terms, works, last)
+    sweep = Sweep(axes, rows, ext, fields, terms, works)
     for step in range(NB - 1):
-        save_rate(last, sweep.rate(step, step))
-        sweep.rows(step, step + 1, LOW + step)
-        sweep.node(step, LOW + step, load_rate(edge, step, 0))
-        save_rate(last, load_rate(edge, step, 1))
-        sweep.rows(step, LOW + rows - 1 - step, LOW + rows + HIGH - 1 - step)
+        low = sweep.rows(step, step + 1, LOW + step, sweep.rate(step, step))
+        sweep.node(step, LOW + step, low, load_rate(edge, step, 0))
+        final = LOW + rows - 2 - step
+        sweep.rows(step, final + 1, final + 1 + HIGH, load_rate(edge, step, 1))
 
     zero = jnp.zeros((SUB, LANES), jnp.float32)
     pairs = [(i, j) for i in range(NB) for j in range(i, NB)]
 
     def finish(q, acc):
         acc = list(acc)
-        grad = raw_gradient(sweep.sh, sweep.read(NB - 1), q, OWN)
+        grad = raw_gradient(sweep.sh, sweep.read(NB - 1), q, OWN, sweep.cache[NB - 1])
         rate = row_rate(grad, terms, works, NB - 1, q, OWN)
         for k in OWN:
             for r in range(3):
@@ -411,7 +406,9 @@
                     acc[n] = acc[n] + vectors[i] * vectors[j]
         return tuple(acc)
 
-    acc = lax.fori_loop(LOW, LOW + rows, finish, tuple(zero for _ in range(len(pairs) + 1)))
+    acc = tuple(zero for _ in range(len(pairs) + 1))
+    for q in range(LOW, LOW + rows):
+        acc = finish(q, acc)
     table[...] = jnp.zeros_like(table)
     muscles = (table.shape[0] // 2) // NB
     for n, value in enumerate(acc):
@@ -430,7 +427,7 @@
             table[pl.ds(step * muscles + m, 1), :] = jnp.sum(total[step], axis=0, keepdims=True)
         return carry
 
-    lax.fori_loop(0, muscles, muscle, 0)
+    lax.fori_loop(0, muscles, muscle, 0, unroll=4)
     row = lax.dot_general(
         jnp.ones((SUB, LANES), jnp.float32),
         table[...],
@@ -575,13 +572,11 @@
         arr(TERMS, count - 1, 2 * SUB, depth),
         arr(NB, count - 1, SUB, depth),
     )
-    kept = pltpu.VMEM((9, 2 * SUB, depth), jnp.float32)
     inner = pl.pallas_call(
         functools.partial(inner_kernel, axes),
         out_shape=(*state, arr(NB - 1, 2, 9, 2 * SUB, depth)),
         in_specs=[VMEM] * 2,
         out_specs=(VMEM,) * 5,
-        scratch_shapes=[kept],
         compiler_params=pltpu.CompilerParams(vmem_limit_bytes=32 << 20),
         name="inner",
     )(block, around)
@@ -592,7 +587,7 @@
         out_shape=(arr(2 * devices, LANES), *state),
         in_specs=[VMEM] * 10,
         out_specs=(VMEM,) * 5,
-        scratch_shapes=[kept, pltpu.VMEM((2 * NB * muscles, LANES), jnp.float32)],
+        scratch_shapes=[pltpu.VMEM((2 * NB * muscles, LANES), jnp.float32)],
         input_output_aliases={5: 1, 6: 2, 7: 3, 8: 4},
         compiler_params=pltpu.CompilerParams(vmem_limit_bytes=32 << 20),
         name="outer",

time: 65.1 us -> 62.1 us (0.954)
  Pallas kernels: 16.6 us -> 12.1 us
  waiting for transfers between devices: 0.95 us -> 2.01 us
    pallas_call x1, Pallas kernels: 8.8 us -> 5.75 us  [per_device(): pl.pallas_call(functools.partial(outer_kernel, axes), out_shape=(arr(2 *...]
    pallas_call x1, Pallas kernels: 4.28 us -> 2.86 us  [per_device(): pl.pallas_call(functools.partial(inner_kernel, axes), out_shape=(*state,...]
    ppermute x6, waiting for transfers between devices: 0.95 us -> 2.01 us  [swap(): return lax.ppermute(shard, axis, pairs + [(j, i) for i, j in pairs])]
  transfers between devices with their start and end apart: 6 -> 6, of which waited for: 1 -> 2; matrix products, arithmetic and copies ran while one was open for 0% -> 0% of each run, Pallas kernels for 7% -> 5%
where the time goes in v6:
time: 62.1 us; the launch traced here: 61.9 us
  blocking collectives  31.9 us (51%)
  starting transfers between devices  15.1 us (24%)
  Pallas kernels  12.1 us (19%)
  waiting for transfers between devices  2.01 us (3%)
  between operations  0.73 us (1%)
    all_to_all x1, blocking collectives, per_device(): every = lax.all_to_all(sums, ('gy', 'gz'), 0, 0, tiled=True)  31.9 us
    ppermute x6, starting transfers between devices, swap(): return lax.ppermute(shard, axis, pairs + [(j, i) for i, j in pairs])  15.1 us
    pallas_call x1, Pallas kernels, per_device(): pl.pallas_call(functools.partial(outer_kernel, axes), out_shape=(arr(2 *...  5.75 us
    pallas_call x1, Pallas kernels, per_device(): pl.pallas_call(functools.partial(inner_kernel, axes), out_shape=(*state,...  2.86 us
    ppermute x6, waiting for transfers between devices, swap(): return lax.ppermute(shard, axis, pairs + [(j, i) for i, j in pairs])  2.01 us
    pallas_call x1, Pallas kernels, per_device(): pl.pallas_call(functools.partial(combine_kernel, muscles, scale), out_sha...  1.81 us
    pallas_call x1, Pallas kernels, per_device(): pl.pallas_call(functools.partial(pack_kernel, axes), out_shape=(arr(CHANN...  1.54 us
  transfers between devices with their start and end apart: 6, of which 2 were waited for; matrix products, arithmetic and copies ran while one was open for 0% of the time, Pallas kernels for 5%

profile of v6, /device:TPU:1, one launch (start us, length us, event | category | flops | bytes accessed | tf_op | source)
XLA Modules:
  0.0 61.9 jit_solution(5033544966275334996)
XLA Ops:
  0.6 1.5 %pack.1 = (f32[8,8,8,256]{3,2,1,0:T(8,128)S(1)}, f32[8,8,4,256]{3,2,1,0:T(4,128)S(1)}, f32[8,8,4,256]{3,2,1,0:T(4,128)S(1)}, f32[8,4,8,256]{3,2,1,0:T(8,128)S(1)...) custom-call(f32[3,8,8,256]{3,2,1,0:T(8,128)} %disp_hbm.1, f32[3,8,8,256]{3,2,1,0:T(8,128)} %load_hbm.1, ...), custom_call_target="tpu_custom_call" | custom-call | tf_op jit(solution)/shard_map/pack/pallas_call | solution.py:524
  2.2 0.7 %collective-permute-start.2 = (f32[8,8,4,256]{3,2,1,0:T(4,128)S(1)}, f32[8,8,4,256]{3,2,1,0:T(4,128)S(1)}, u32[]{:S(2)}, u32[]{:S(2)}) collective-permute-start(f32[8,8,4,256]{3,2,1,0:T(4,128)S(1)} %get-tuple-element.25), channel_id=1, source_target_pairs={{1,2},{3,4},{5,6},{7,8},{9,10},{11,12},{13,14},{2,1},{4,3},{6,5},{... | collective-permute-start | bytes 786440 | tf_op jit(solution)/shard_map/ppermute | solution.py:509
  2.9 4.6 %collective-permute-start.3 = (f32[8,8,4,256]{3,2,1,0:T(4,128)S(1)}, f32[8,8,4,256]{3,2,1,0:T(4,128)S(1)}, u32[]{:S(2)}, u32[]{:S(2)}) collective-permute-start(f32[8,8,4,256]{3,2,1,0:T(4,128)S(1)} %get-tuple-element.26), channel_id=1, source_target_pairs={{0,1},{2,3},{4,5},{6,7},{8,9},{10,11},{12,13},{14,15},{1,0},{3,2},... | collective-permute-start | bytes 786440 | tf_op jit(solution)/shard_map/ppermute | solution.py:509
  7.4 4.7 %collective-permute-start = (f32[8,4,8,256]{3,2,1,0:T(8,128)S(1)}, f32[8,4,8,256]{3,2,1,0:T(8,128)S(1)}, u32[]{:S(2)}, u32[]{:S(2)}) collective-permute-start(f32[8,4,8,256]{3,2,1,0:T(8,128)S(1)} %get-tuple-element.23), channel_id=1, source_target_pairs={{16,32},{48,64},{80,96},{112,128},{144,160},{176,192},{208,224},{3... | collective-permute-start | bytes 786440 | tf_op jit(solution)/shard_map/ppermute | solution.py:509
  12.1 0.1 collective-permute-start.1
  12.2 0.0 collective-permute-done.2.znext_ref
  12.2 0.9 %collective-permute-done.3.zpair_ref = f32[8,8,4,256]{3,2,1,0:T(4,128)S(1)} collective-permute-done((f32[8,8,4,256]{3,2,1,0:T(4,128)S(1)}, f32[8,8,4,256]{3,2,1,0:T(4,128)S(1)}, u32[]{:S(2)}, u32[]{:S(2)}) %collective-permute-start.3) | collective-permute-done | bytes 262176 | tf_op jit(solution)/shard_map/ppermute | solution.py:509
  13.1 0.2 corner.1
  13.3 5.0 %collective-permute-start.4 = (f32[8,4,8,256]{3,2,1,0:T(8,128)S(1)}, f32[8,4,8,256]{3,2,1,0:T(8,128)S(1)}, u32[]{:S(2)}, u32[]{:S(2)}) collective-permute-start(f32[8,4,8,256]{3,2,1,0:T(8,128)S(1)} %get-tuple-element.29), channel_id=1, source_target_pairs={{16,32},{48,64},{80,96},{112,128},{144,160},{176,192},{208,224},{3... | collective-permute-start | bytes 786440 | tf_op jit(solution)/shard_map/ppermute | solution.py:509
  18.3 0.1 collective-permute-start.5
  18.4 2.9 %inner.1 = (f32[8,15,16,256]{3,2,1,0:T(8,128)S(1)}, f32[3,3,15,16,256]{4,3,2,1,0:T(8,128)S(1)}, f32[15,14,16,256]{3,2,1,0:T(8,128)S(1)}, f32[4,14,8,256]{3,2,1,0:T(8,128)S(1)}, f32[3,2,9,16,256]{4,3,2,1,0:T(8,128)S(1)}) custom-call(f32[8,8,8,256]{3,2,1,0:T(8,128)S(1)} %get-tuple-element.31.block_ref, f32[8,8,8,256]{3,2,1,0:T(8,128)S(1)} %get-tuple-element.32.around_ref), custom_call_target="tpu_custom_call" | custom-call | tf_op jit(solution)/shard_map/inner/pallas_call | solution.py:575
  21.3 0.0 collective-permute-done.ynext_ref
  21.3 0.0 collective-permute-done.1.ypair_ref
  21.3 1.1 %collective-permute-done.4.cnext_ref = f32[8,4,8,256]{3,2,1,0:T(8,128)S(1)} collective-permute-done((f32[8,4,8,256]{3,2,1,0:T(8,128)S(1)}, f32[8,4,8,256]{3,2,1,0:T(8,128)S(1)}, u32[]{:S(2)}, u32[]{:S(2)}) %collective-permute-start.4) | collective-permute-done | bytes 262176 | tf_op jit(solution)/shard_map/ppermute | solution.py:509
  22.4 0.0 collective-permute-done.5.cpair_ref
  22.4 5.8 %outer.1 = (f32[512,128]{1,0:T(8,128)S(1)}, f32[8,15,16,256]{3,2,1,0:T(8,128)S(1)}, f32[3,3,15,16,256]{4,3,2,1,0:T(8,128)S(1)}, f32[15,14,16,256]{3,2,1,0:T(8,128)S(1)}, f32[4,14,8,256]{3,2,1,0:T(8,128)S(1)}) custom-call(s32[8,8,256]{2,1,0:T(8,128)S(1)} %get-tuple-element.22.group_ref, ...), custom_call_target="tpu_custom_call", output_to_operand_aliasing={{1}: (5, {}), {2}: (6, {}), {3}: (7, {}), {4}: (8, {})} | custom-call | tf_op jit(solution)/shard_map/outer/pallas_call | solution.py:585
  28.1 31.9 %all_to_all.11 = f32[256,2,128]{2,1,0:T(2,128)S(1)} all-to-all(f32[256,2,128]{2,1,0:T(2,128)S(1)} %bitcast.4), channel_id=1, replica_groups=mesh['gy'=16,'gz'=16] {'gy','gz'}, dimensions={0} | all-to-all | bytes 524288 | tf_op jit(solution)/shard_map/all_to_all | solution.py:596
  60.0 1.8 %combine.1 = (f32[3,8,8,256]{3,2,1,0:T(8,128)}, f32[1,32]{1,0:T(1,128)}) custom-call(f32[512,128]{1,0:T(8,128)S(1)} %bitcast.3, f32[8,8,8,256]{3,2,1,0:T(8,128)S(1)} %get-tuple-element.31.block_ref, f32[3,3,15,16,256]{4,3,2,1,0:T(8,128)S(1)} %get-tuple-element.39.fields), custom_call_target="tpu_custom_call" | custom-call | tf_op jit(solution)/shard_map/combine/pallas_call | solution.py:600
Async XLA Ops:
  2.2 10.0 %collective-permute-start.2 = (f32[8,8,4,256]{3,2,1,0:T(4,128)S(1)}, f32[8,8,4,256]{3,2,1,0:T(4,128)S(1)}, u32[]{:S(2)}, u32[]{:S(2)}) collective-permute-start(f32[8,8,4,256]{3,2,1,0:T(4,128)S(1)} %get-tuple-element.25), channel_id=1, source_target_pairs={{1,2},{3,4},{5,6},{7,8},{9,10},{11,12},{13,14},{2,1},{4,3},{6,5},{... | collective-permute-start | bytes 786440 | tf_op jit(solution)/shard_map/ppermute | solution.py:509
  2.9 10.3 %collective-permute-start.3 = (f32[8,8,4,256]{3,2,1,0:T(4,128)S(1)}, f32[8,8,4,256]{3,2,1,0:T(4,128)S(1)}, u32[]{:S(2)}, u32[]{:S(2)}) collective-permute-start(f32[8,8,4,256]{3,2,1,0:T(4,128)S(1)} %get-tuple-element.26), channel_id=1, source_target_pairs={{0,1},{2,3},{4,5},{6,7},{8,9},{10,11},{12,13},{14,15},{1,0},{3,2},... | collective-permute-start | bytes 786440 | tf_op jit(solution)/shard_map/ppermute | solution.py:509
  7.4 13.9 %collective-permute-start = (f32[8,4,8,256]{3,2,1,0:T(8,128)S(1)}, f32[8,4,8,256]{3,2,1,0:T(8,128)S(1)}, u32[]{:S(2)}, u32[]{:S(2)}) collective-permute-start(f32[8,4,8,256]{3,2,1,0:T(8,128)S(1)} %get-tuple-element.23), channel_id=1, source_target_pairs={{16,32},{48,64},{80,96},{112,128},{144,160},{176,192},{208,224},{3... | collective-permute-start | bytes 786440 | tf_op jit(solution)/shard_map/ppermute | solution.py:509
  12.1 9.2 %collective-permute-start.1 = (f32[8,4,8,256]{3,2,1,0:T(8,128)S(1)}, f32[8,4,8,256]{3,2,1,0:T(8,128)S(1)}, u32[]{:S(2)}, u32[]{:S(2)}) collective-permute-start(f32[8,4,8,256]{3,2,1,0:T(8,128)S(1)} %get-tuple-element.24), channel_id=1, source_target_pairs={{0,16},{32,48},{64,80},{96,112},{128,144},{160,176},{192,208},{224... | collective-permute-start | bytes 786440 | tf_op jit(solution)/shard_map/ppermute | solution.py:509
  13.3 9.0 %collective-permute-start.4 = (f32[8,4,8,256]{3,2,1,0:T(8,128)S(1)}, f32[8,4,8,256]{3,2,1,0:T(8,128)S(1)}, u32[]{:S(2)}, u32[]{:S(2)}) collective-permute-start(f32[8,4,8,256]{3,2,1,0:T(8,128)S(1)} %get-tuple-element.29), channel_id=1, source_target_pairs={{16,32},{48,64},{80,96},{112,128},{144,160},{176,192},{208,224},{3... | collective-permute-start | bytes 786440 | tf_op jit(solution)/shard_map/ppermute | solution.py:509
  18.3 4.0 %collective-permute-start.5 = (f32[8,4,8,256]{3,2,1,0:T(8,128)S(1)}, f32[8,4,8,256]{3,2,1,0:T(8,128)S(1)}, u32[]{:S(2)}, u32[]{:S(2)}) collective-permute-start(f32[8,4,8,256]{3,2,1,0:T(8,128)S(1)} %get-tuple-element.30), channel_id=1, source_target_pairs={{0,16},{32,48},{64,80},{96,112},{128,144},{160,176},{192,208},{224... | collective-permute-start | bytes 786440 | tf_op jit(solution)/shard_map/ppermute | solution.py:509

commit v7 on v6

--- a/solution.py
+++ b/solution.py
@@ -330,7 +330,33 @@
     send_rows(around_ref, ypair_ref, ynext_ref, even_y)
 
 
-def inner_kernel(axes, block_ref, around_ref, ext, fields, terms, works, edge):
+def table_row(step, m, muscles):
+    half = muscles // 2
+    return half * step + m + (LANES - half) * lax.div(m, half)
+
+
+def muscle_sums(group_ref, works, muscles, spans, store):
+    zero = jnp.zeros((SUB, LANES), jnp.float32)
+
+    def muscle(m, carry):
+        total = [zero for _ in spans]
+        for q in sorted({q for span in spans for q in span}):
+            for h in range(2):
+                mine = group_ref[q - LOW, :, pl.ds(LANES * h, LANES)] == m
+                for step, span in enumerate(spans):
+                    if q in span:
+                        work = works[(step, q, *part((0, h)))]
+                        total[step] = total[step] + jnp.where(mine, work, 0.0)
+        for step in range(len(spans)):
+            store(step, table_row(step, m, muscles), jnp.sum(total[step], axis=0, keepdims=True))
+        return carry
+
+    lax.fori_loop(0, muscles, muscle, 0, unroll=4)
+
+
+def inner_kernel(
+    axes, muscles, block_ref, around_ref, group_ref, ext, fields, terms, works, edge, partial
+):
     rows = block_ref.shape[1]
 
     def assemble(c, carry):
@@ -347,10 +373,19 @@
         save_rate(edge, rate, step, 0)
         save_rate(edge, sweep.rows(step, first + 1, final + 1, rate), step, 1)
 
+    def store(step, at, value):
+        partial[pl.ds(at, 1), :] = value
+
+    spans = [range(LOW + step, LOW + rows - 1 - step) for step in range(NB - 1)]
+    muscle_sums(group_ref, works, muscles, spans, store)
+
 
 def outer_kernel(
     axes,
+    muscles,
+    group_size,
     group_ref,
+    partial,
     ynext_ref,
     ypair_ref,
     cnext_ref,
@@ -410,24 +445,22 @@
     for q in range(LOW, LOW + rows):
         acc = finish(q, acc)
     table[...] = jnp.zeros_like(table)
-    muscles = (table.shape[0] // 2) // NB
     for n, value in enumerate(acc):
-        table[pl.ds(NB * muscles + n, 1), :] = jnp.sum(value, axis=0, keepdims=True)
-
-    def muscle(m, carry):
-        total = [zero] * NB
-        for y in range(rows):
-            for h in range(2):
-                mine = group_ref[y, :, pl.ds(LANES * h, LANES)] == m
-                for step in range(NB):
-                    total[step] = total[step] + jnp.where(
-                        mine, works[(step, LOW + y, *part((0, h)))], 0.0
-                    )
-        for step in range(NB):
-            table[pl.ds(step * muscles + m, 1), :] = jnp.sum(total[step], axis=0, keepdims=True)
-        return carry
-
-    lax.fori_loop(0, muscles, muscle, 0, unroll=4)
+        total = jnp.sum(value, axis=0, keepdims=True)
+        for core in range(2):
+            table[pl.ds(LANES * core + NB * (muscles // 2) + n, 1), :] = total
+
+    def store(step, at, value):
+        if step < NB - 1:
+            value = value + partial[pl.ds(at, 1), :]
+        table[pl.ds(at, 1), :] = value
+
+    own = range(LOW, LOW + rows)
+    spans = [
+        [q for q in own if not LOW + step <= q < LOW + rows - 1 - step or step == NB - 1]
+        for step in range(NB)
+    ]
+    muscle_sums(group_ref, works, muscles, spans, store)
     row = lax.dot_general(
         jnp.ones((SUB, LANES), jnp.float32),
         table[...],
@@ -435,21 +468,20 @@
         precision=lax.Precision.HIGHEST,
         preferred_element_type=jnp.float32,
     )
-    is_first = lax.rem(sweep.sh.sub, 2) == 0
-    message = jnp.where(is_first, row[:, :LANES], row[:, LANES:])
     for i in range(sums_ref.shape[0] // SUB):
-        sums_ref[pl.ds(SUB * i, SUB), :] = message
-
-
-def combine_kernel(muscles, scale, sums_ref, block_ref, fields, x_hbm, grad_hbm, x_ref, grad_ref, sems):
+        core = i // (group_size // SUB) % 2
+        sums_ref[pl.ds(SUB * i, SUB), :] = row[:, LANES * core : LANES * (core + 1)]
+
+
+def solve_kernel(axes, muscles, scale, sums_ref, coef_ref, grad_ref):
     parts = [sums_ref[pl.ds(SUB * i, SUB), :] for i in range(sums_ref.shape[0] // SUB)]
     while len(parts) > 1:
         odd = parts[len(parts) // 2 * 2 :]
         parts = [a + b for a, b in zip(parts[0::2], parts[1::2])] + odd
     total = parts[0]
-    is_first = lax.rem(lax.broadcasted_iota(jnp.int32, total.shape, 0), 2) == 0
-    works = jnp.sum(jnp.where(is_first, total, 0.0), axis=0, keepdims=True)
-    dots = jnp.sum(jnp.where(is_first, 0.0, total), axis=0, keepdims=True)
+    total = jnp.sum(total, axis=0, keepdims=True)
+    half = muscles // 2
+    works, dots = total[:, : NB * half], total[:, NB * half :]
     pairs = [(i, j) for i in range(NB) for j in range(i, NB)]
     gram = {}
     for n, (i, j) in enumerate(pairs):
@@ -481,22 +513,30 @@
             value = value - form[k, j] * x[j]
         x[k] = value * inverse[k]
 
+    for k in range(NB):
+        coef_ref[k] = jnp.broadcast_to(x[k], (SUB, LANES))
     grad = None
     for k in range(NB):
-        part = x[k] * works[:, k * muscles : (k + 1) * muscles]
-        grad = part if grad is None else grad + part
-    grad_ref[...] = -scale * grad
-    copies = [pltpu.make_async_copy(grad_ref, grad_hbm, sems.at[3])]
-    copies[0].start()
-
-    width = block_ref.shape[-1]
-    coef = [jnp.broadcast_to(x[k], (SUB, width)) for k in range(NB)]
+        piece = x[k] * works[:, k * half : (k + 1) * half]
+        grad = piece if grad is None else grad + piece
+    grad = -scale * grad
+    nothing = jnp.zeros_like(grad)
+    low = even(axes[0])
+    grad_ref[:, pl.ds(0, half)] = jnp.where(low, grad, nothing)
+    grad_ref[:, pl.ds(half, half)] = jnp.where(low, nothing, grad)
+
+
+def update_kernel(coef_ref, block_ref, fields, x_hbm, x_ref, sems):
+    coef = [coef_ref[k] for k in range(NB)]
+    copies = []
     for comp in range(3):
         for y in range(block_ref.shape[1]):
-            value = coef[0] * block_ref[3 + comp, y]
-            for k in range(1, NB):
-                value = value + coef[k] * fields[k - 1, comp, LOW + y, pl.ds(0, SUB), :]
-            x_ref[comp, y] = value
+            for h in range(2):
+                at = pl.ds(LANES * h, LANES)
+                value = coef[0] * block_ref[3 + comp, y, :, at]
+                for k in range(1, NB):
+                    value = value + coef[k] * fields[(k - 1, comp, LOW + y, *part((0, h)))]
+                x_ref[comp, y, :, at] = value
         copies.append(pltpu.make_async_copy(x_ref.at[comp], x_hbm.at[comp], sems.at[comp]))
         copies[-1].start()
     for copy in copies:
@@ -572,48 +612,50 @@
         arr(TERMS, count - 1, 2 * SUB, depth),
         arr(NB, count - 1, SUB, depth),
     )
-    inner = pl.pallas_call(
-        functools.partial(inner_kernel, axes),
-        out_shape=(*state, arr(NB - 1, 2, 9, 2 * SUB, depth)),
-        in_specs=[VMEM] * 2,
-        out_specs=(VMEM,) * 5,
+    *inner, partial = pl.pallas_call(
+        functools.partial(inner_kernel, axes, muscles),
+        out_shape=(*state, arr(NB - 1, 2, 9, 2 * SUB, depth), arr(2 * LANES, LANES)),
+        in_specs=[VMEM] * 3,
+        out_specs=(VMEM,) * 6,
         compiler_params=pltpu.CompilerParams(vmem_limit_bytes=32 << 20),
         name="inner",
-    )(block, around)
+    )(block, around, group)
 
     devices = lax.axis_size("gy") * lax.axis_size("gz")
     sums, _, fields, _, _ = pl.pallas_call(
-        functools.partial(outer_kernel, axes),
-        out_shape=(arr(2 * devices, LANES), *state),
-        in_specs=[VMEM] * 10,
+        functools.partial(outer_kernel, axes, muscles, lax.axis_size("gz")),
+        out_shape=(arr(devices, LANES), *state),
+        in_specs=[VMEM] * 11,
         out_specs=(VMEM,) * 5,
-        scratch_shapes=[pltpu.VMEM((2 * NB * muscles, LANES), jnp.float32)],
-        input_output_aliases={5: 1, 6: 2, 7: 3, 8: 4},
+        scratch_shapes=[pltpu.VMEM((2 * LANES, LANES), jnp.float32)],
+        input_output_aliases={6: 1, 7: 2, 8: 3, 9: 4},
         compiler_params=pltpu.CompilerParams(vmem_limit_bytes=32 << 20),
         name="outer",
-    )(group, ynext, ypair, cnext, cpair, *inner)
+    )(group, partial, ynext, ypair, cnext, cpair, *inner)
 
     every = lax.all_to_all(sums, ("gy", "gz"), 0, 0, tiled=True)
 
     cells = depth * rows * lax.axis_size("gy") * cols * lax.axis_size("gz")
     scale = 1.0 / math.sqrt(cells / muscles)
-    adjoint, muscle_grad = pl.pallas_call(
-        functools.partial(combine_kernel, muscles, scale),
-        out_shape=(
-            jax.ShapeDtypeStruct(load.shape, jnp.float32),
-            jax.ShapeDtypeStruct((1, muscles), jnp.float32),
-        ),
+    coef, mine = pl.pallas_call(
+        functools.partial(solve_kernel, axes, muscles, scale),
+        out_shape=(arr(NB, SUB, LANES), arr(1, muscles)),
+        in_specs=[VMEM],
+        out_specs=(VMEM, VMEM),
+        compiler_params=pltpu.CompilerParams(vmem_limit_bytes=32 << 20),
+        name="solve",
+    )(every)
+    others = swap(mine, "gy", 0)
+    adjoint = pl.pallas_call(
+        update_kernel,
+        out_shape=arr(*load.shape),
         in_specs=[VMEM] * 3,
-        out_specs=(anywhere, anywhere),
-        scratch_shapes=[
-            pltpu.VMEM(load.shape, jnp.float32),
-            pltpu.VMEM((1, muscles), jnp.float32),
-            pltpu.SemaphoreType.DMA((4,)),
-        ],
+        out_specs=anywhere,
+        scratch_shapes=[pltpu.VMEM(load.shape, jnp.float32), pltpu.SemaphoreType.DMA((3,))],
         compiler_params=pltpu.CompilerParams(vmem_limit_bytes=32 << 20),
-        name="combine",
-    )(every, block, fields)
-    return adjoint, muscle_grad.reshape(muscles)
+        name="update",
+    )(coef, block, fields)
+    return adjoint, (mine + others).reshape(muscles)
 
 
 def solution(mesh):

time: 62.1 us -> 60.3 us (0.971)
  blocking collectives: 31.9 us -> 29.2 us
    all_to_all x1, blocking collectives: 31.9 us -> 29.2 us  [per_device(): every = lax.all_to_all(sums, ('gy', 'gz'), 0, 0, tiled=True)]
    ppermute x6 -> x7, starting transfers between devices: 15.1 us -> 15.6 us  [swap(): return lax.ppermute(shard, axis, pairs + [(j, i) for i, j in pairs])]
    ppermute x6 -> x7, waiting for transfers between devices: 2.01 us -> 1.65 us  [swap(): return lax.ppermute(shard, axis, pairs + [(j, i) for i, j in pairs])]
    pallas_call x3 -> x4, Pallas kernels: 10.4 us -> 10.6 us  [the longest x1 5.46 us: per_device(): pl.pallas_call(functools.partial(outer_kernel, axes, muscles, lax.axis_si...]
  transfers between devices with their start and end apart: 6 -> 7, of which waited for: 2 -> 3; matrix products, arithmetic and copies ran while one was open for 0% -> 0% of each run, Pallas kernels for 5% -> 7%
where the time goes in v7:
time: 60.3 us; the launch traced here: 60.1 us
  blocking collectives  29.2 us (48%)
  starting transfers between devices  15.6 us (26%)
  Pallas kernels  12.4 us (21%)
  waiting for transfers between devices  1.65 us (3%)
  between operations  0.73 us (1%)
    all_to_all x1, blocking collectives, per_device(): every = lax.all_to_all(sums, ('gy', 'gz'), 0, 0, tiled=True)  29.2 us
    ppermute x7, starting transfers between devices, swap(): return lax.ppermute(shard, axis, pairs + [(j, i) for i, j in pairs])  15.6 us
    pallas_call x1, Pallas kernels, per_device(): pl.pallas_call(functools.partial(outer_kernel, axes, muscles, lax.axis_si...  5.46 us
    pallas_call x1, Pallas kernels, per_device(): pl.pallas_call(functools.partial(inner_kernel, axes, muscles), out_shape=...  3.31 us
    ppermute x7, waiting for transfers between devices, swap(): return lax.ppermute(shard, axis, pairs + [(j, i) for i, j in pairs])  1.65 us
    pallas_call x1, Pallas kernels, per_device(): pl.pallas_call(functools.partial(pack_kernel, axes), out_shape=(arr(CHANN...  1.54 us
  transfers between devices with their start and end apart: 7, of which 3 were waited for; matrix products, arithmetic and copies ran while one was open for 0% of the time, Pallas kernels for 7%

profile of v7, /device:TPU:1, one launch (start us, length us, event | category | flops | bytes accessed | tf_op | source)
XLA Modules:
  0.0 60.1 jit_solution(10359531727683184094)
XLA Ops:
  0.6 1.5 %pack.1 = (f32[8,8,8,256]{3,2,1,0:T(8,128)S(1)}, f32[8,8,4,256]{3,2,1,0:T(4,128)S(1)}, f32[8,8,4,256]{3,2,1,0:T(4,128)S(1)}, f32[8,4,8,256]{3,2,1,0:T(8,128)S(1)...) custom-call(f32[3,8,8,256]{3,2,1,0:T(8,128)} %disp_hbm.1, f32[3,8,8,256]{3,2,1,0:T(8,128)} %load_hbm.1, ...), custom_call_target="tpu_custom_call" | custom-call | tf_op jit(solution)/shard_map/pack/pallas_call | solution.py:564
  2.2 0.7 %collective-permute-start = (f32[8,8,4,256]{3,2,1,0:T(4,128)S(1)}, f32[8,8,4,256]{3,2,1,0:T(4,128)S(1)}, u32[]{:S(2)}, u32[]{:S(2)}) collective-permute-start(f32[8,8,4,256]{3,2,1,0:T(4,128)S(1)} %get-tuple-element.25), channel_id=1, source_target_pairs={{1,2},{3,4},{5,6},{7,8},{9,10},{11,12},{13,14},{2,1},{4,3},{6,5},{... | collective-permute-start | bytes 786440 | tf_op jit(solution)/shard_map/ppermute | solution.py:549
  2.9 4.6 %collective-permute-start.1 = (f32[8,8,4,256]{3,2,1,0:T(4,128)S(1)}, f32[8,8,4,256]{3,2,1,0:T(4,128)S(1)}, u32[]{:S(2)}, u32[]{:S(2)}) collective-permute-start(f32[8,8,4,256]{3,2,1,0:T(4,128)S(1)} %get-tuple-element.26), channel_id=1, source_target_pairs={{0,1},{2,3},{4,5},{6,7},{8,9},{10,11},{12,13},{14,15},{1,0},{3,2},... | collective-permute-start | bytes 786440 | tf_op jit(solution)/shard_map/ppermute | solution.py:549
  7.4 4.7 %collective-permute-start.2 = (f32[8,4,8,256]{3,2,1,0:T(8,128)S(1)}, f32[8,4,8,256]{3,2,1,0:T(8,128)S(1)}, u32[]{:S(2)}, u32[]{:S(2)}) collective-permute-start(f32[8,4,8,256]{3,2,1,0:T(8,128)S(1)} %get-tuple-element.31), channel_id=1, source_target_pairs={{16,32},{48,64},{80,96},{112,128},{144,160},{176,192},{208,224},{3... | collective-permute-start | bytes 786440 | tf_op jit(solution)/shard_map/ppermute | solution.py:549
  12.1 0.1 collective-permute-start.3
  12.2 0.0 collective-permute-done.znext_ref
  12.2 0.9 %collective-permute-done.1.zpair_ref = f32[8,8,4,256]{3,2,1,0:T(4,128)S(1)} collective-permute-done((f32[8,8,4,256]{3,2,1,0:T(4,128)S(1)}, f32[8,8,4,256]{3,2,1,0:T(4,128)S(1)}, u32[]{:S(2)}, u32[]{:S(2)}) %collective-permute-start.1) | collective-permute-done | bytes 262176 | tf_op jit(solution)/shard_map/ppermute | solution.py:549
  13.1 0.2 corner.1
  13.3 5.0 %collective-permute-start.4 = (f32[8,4,8,256]{3,2,1,0:T(8,128)S(1)}, f32[8,4,8,256]{3,2,1,0:T(8,128)S(1)}, u32[]{:S(2)}, u32[]{:S(2)}) collective-permute-start(f32[8,4,8,256]{3,2,1,0:T(8,128)S(1)} %get-tuple-element.33), channel_id=1, source_target_pairs={{16,32},{48,64},{80,96},{112,128},{144,160},{176,192},{208,224},{3... | collective-permute-start | bytes 786440 | tf_op jit(solution)/shard_map/ppermute | solution.py:549
  18.3 0.1 collective-permute-start.5
  18.4 3.3 %inner.1 = (f32[8,15,16,256]{3,2,1,0:T(8,128)S(1)}, f32[3,3,15,16,256]{4,3,2,1,0:T(8,128)S(1)}, f32[15,14,16,256]{3,2,1,0:T(8,128)S(1)}, f32[4,14,8,256]{3,2,1,0...) custom-call(f32[8,8,8,256]{3,2,1,0:T(8,128)S(1)} %get-tuple-element.24.block_ref, ...), custom_call_target="tpu_custom_call" | custom-call | tf_op jit(solution)/shard_map/inner/pallas_call | solution.py:615
  21.7 0.0 collective-permute-done.2.ynext_ref
  21.8 0.0 collective-permute-done.3.ypair_ref
  21.8 0.6 %collective-permute-done.4.cnext_ref = f32[8,4,8,256]{3,2,1,0:T(8,128)S(1)} collective-permute-done((f32[8,4,8,256]{3,2,1,0:T(8,128)S(1)}, f32[8,4,8,256]{3,2,1,0:T(8,128)S(1)}, u32[]{:S(2)}, u32[]{:S(2)}) %collective-permute-start.4) | collective-permute-done | bytes 262176 | tf_op jit(solution)/shard_map/ppermute | solution.py:549
  22.4 0.0 collective-permute-done.5.cpair_ref
  22.4 5.5 %outer.1 = (f32[256,128]{1,0:T(8,128)S(1)}, f32[8,15,16,256]{3,2,1,0:T(8,128)S(1)}, f32[3,3,15,16,256]{4,3,2,1,0:T(8,128)S(1)}, f32[15,14,16,256]{3,2,1,0:T(8,128)S(1)}, f32[4,14,8,256]{3,2,1,0:T(8,128)S(1)}) custom-call(s32[8,8,256]{2,1,0:T(8,128)S(1)} %get-tuple-element.23.group_ref, ...), custom_call_target="tpu_custom_call", output_to_operand_aliasing={{1}: (6, {}), {2}: (7, {}), {3}: (8, {}), {4}: (9, {})} | custom-call | tf_op jit(solution)/shard_map/outer/pallas_call | solution.py:625
  27.8 29.2 %all_to_all.11 = f32[256,1,128]{2,1,0:T(1,128)S(1)} all-to-all(f32[256,1,128]{2,1,0:T(1,128)S(1)} %bitcast.7), channel_id=1, replica_groups=mesh['gy'=16,'gz'=16] {'gy','gz'}, dimensions={0} | all-to-all | bytes 262144 | tf_op jit(solution)/shard_map/all_to_all | solution.py:636
  57.1 1.2 %solve.1 = (f32[4,8,128]{2,1,0:T(8,128)S(1)}, f32[1,32]{1,0:T(1,128)S(1)}) custom-call(f32[256,128]{1,0:T(8,128)S(1)} %bitcast.6), custom_call_target="tpu_custom_call" | custom-call | tf_op jit(solution)/shard_map/solve/pallas_call | solution.py:640
  58.2 0.6 collective-permute-start.6
  58.8 0.7 %update.1 = f32[3,8,8,256]{3,2,1,0:T(8,128)} custom-call(f32[4,8,128]{2,1,0:T(8,128)S(1)} %get-tuple-element.41.coef_ref, f32[8,8,8,256]{3,2,1,0:T(8,128)S(1)} %get-tuple-element.24.block_ref, f32[3,3,15,16,256]{4,3,2,1,0:T(8,128)S(1)} %get-tuple-element.42.fields), custom_call_target="tpu_custom_call" | custom-call | tf_op jit(solution)/shard_map/update/pallas_call | solution.py:649
  59.5 0.1 collective-permute-done.6
  59.6 0.5 add_bitcast_fusion
Async XLA Ops:
  2.2 10.0 %collective-permute-start = (f32[8,8,4,256]{3,2,1,0:T(4,128)S(1)}, f32[8,8,4,256]{3,2,1,0:T(4,128)S(1)}, u32[]{:S(2)}, u32[]{:S(2)}) collective-permute-start(f32[8,8,4,256]{3,2,1,0:T(4,128)S(1)} %get-tuple-element.25), channel_id=1, source_target_pairs={{1,2},{3,4},{5,6},{7,8},{9,10},{11,12},{13,14},{2,1},{4,3},{6,5},{... | collective-permute-start | bytes 786440 | tf_op jit(solution)/shard_map/ppermute | solution.py:549
  2.9 10.3 %collective-permute-start.1 = (f32[8,8,4,256]{3,2,1,0:T(4,128)S(1)}, f32[8,8,4,256]{3,2,1,0:T(4,128)S(1)}, u32[]{:S(2)}, u32[]{:S(2)}) collective-permute-start(f32[8,8,4,256]{3,2,1,0:T(4,128)S(1)} %get-tuple-element.26), channel_id=1, source_target_pairs={{0,1},{2,3},{4,5},{6,7},{8,9},{10,11},{12,13},{14,15},{1,0},{3,2},... | collective-permute-start | bytes 786440 | tf_op jit(solution)/shard_map/ppermute | solution.py:549
  7.4 14.3 %collective-permute-start.2 = (f32[8,4,8,256]{3,2,1,0:T(8,128)S(1)}, f32[8,4,8,256]{3,2,1,0:T(8,128)S(1)}, u32[]{:S(2)}, u32[]{:S(2)}) collective-permute-start(f32[8,4,8,256]{3,2,1,0:T(8,128)S(1)} %get-tuple-element.31), channel_id=1, source_target_pairs={{16,32},{48,64},{80,96},{112,128},{144,160},{176,192},{208,224},{3... | collective-permute-start | bytes 786440 | tf_op jit(solution)/shard_map/ppermute | solution.py:549
  12.1 9.7 %collective-permute-start.3 = (f32[8,4,8,256]{3,2,1,0:T(8,128)S(1)}, f32[8,4,8,256]{3,2,1,0:T(8,128)S(1)}, u32[]{:S(2)}, u32[]{:S(2)}) collective-permute-start(f32[8,4,8,256]{3,2,1,0:T(8,128)S(1)} %get-tuple-element.32), channel_id=1, source_target_pairs={{0,16},{32,48},{64,80},{96,112},{128,144},{160,176},{192,208},{224... | collective-permute-start | bytes 786440 | tf_op jit(solution)/shard_map/ppermute | solution.py:549
  13.3 9.0 %collective-permute-start.4 = (f32[8,4,8,256]{3,2,1,0:T(8,128)S(1)}, f32[8,4,8,256]{3,2,1,0:T(8,128)S(1)}, u32[]{:S(2)}, u32[]{:S(2)}) collective-permute-start(f32[8,4,8,256]{3,2,1,0:T(8,128)S(1)} %get-tuple-element.33), channel_id=1, source_target_pairs={{16,32},{48,64},{80,96},{112,128},{144,160},{176,192},{208,224},{3... | collective-permute-start | bytes 786440 | tf_op jit(solution)/shard_map/ppermute | solution.py:549
  18.3 4.0 %collective-permute-start.5 = (f32[8,4,8,256]{3,2,1,0:T(8,128)S(1)}, f32[8,4,8,256]{3,2,1,0:T(8,128)S(1)}, u32[]{:S(2)}, u32[]{:S(2)}) collective-permute-start(f32[8,4,8,256]{3,2,1,0:T(8,128)S(1)} %get-tuple-element.34), channel_id=1, source_target_pairs={{0,16},{32,48},{64,80},{96,112},{128,144},{160,176},{192,208},{224... | collective-permute-start | bytes 786440 | tf_op jit(solution)/shard_map/ppermute | solution.py:549
  58.2 1.4 %collective-permute-start.6 = (f32[1,32]{1,0:T(1,128)S(1)}, f32[1,32]{1,0:T(1,128)S(1)}, u32[]{:S(2)}, u32[]{:S(2)}) collective-permute-start(f32[1,32]{1,0:T(1,128)S(1)} %get-tuple-element.43), channel_id=1, source_target_pairs={{0,16},{32,48},{64,80},{96,112},{128,144},{160,176},{192,208},{224... | collective-permute-start | bytes 392 | tf_op jit(solution)/shard_map/ppermute | solution.py:549

commit v8 on v7

--- a/solution.py
+++ b/solution.py
@@ -299,7 +299,7 @@
             znext_ref[c, y] = jnp.where(even_z, bottom, top)
         return carry
 
-    lax.fori_loop(0, rows, row, 0)
+    lax.fori_loop(0, rows, row, 0, unroll=4)
     send_rows(block_ref, ypair_ref, ynext_ref, even_y)
 
 
@@ -313,7 +313,7 @@
             next_ref[c, y] = block_ref[c, rows - HIGH - pair_at + y]
         return carry
 
-    lax.fori_loop(0, CHANNELS, channel, 0)
+    lax.fori_loop(0, CHANNELS, channel, 0, unroll=4)
 
 
 def corner_kernel(axes, zpair_ref, znext_ref, around_ref, ypair_ref, ynext_ref):
@@ -326,7 +326,7 @@
             around_ref[c, y, pl.ds(HIGH, HIGH), :] = jnp.where(even_z, far, pair)
         return carry
 
-    lax.fori_loop(0, CHANNELS, channel, 0)
+    lax.fori_loop(0, CHANNELS, channel, 0, unroll=4)
     send_rows(around_ref, ypair_ref, ynext_ref, even_y)
 
 
@@ -351,7 +351,7 @@
             store(step, table_row(step, m, muscles), jnp.sum(total[step], axis=0, keepdims=True))
         return carry
 
-    lax.fori_loop(0, muscles, muscle, 0, unroll=4)
+    lax.fori_loop(0, muscles, muscle, 0, unroll=8)
 
 
 def inner_kernel(
@@ -365,7 +365,7 @@
             ext[c, LOW + y, pl.ds(SUB, SUB), :] = around_ref[c, y]
         return carry
 
-    lax.fori_loop(0, CHANNELS, assemble, 0)
+    lax.fori_loop(0, CHANNELS, assemble, 0, unroll=4)
     sweep = Sweep(axes, rows, ext, fields, terms, works)
     for step in range(NB - 1):
         first, final = LOW + step, LOW + rows - 2 - step
@@ -415,7 +415,7 @@
                     ext[c, y - HIGH + LOW, pl.ds(SUB * zt, SUB), :] = jnp.where(even_y, far, pair)
         return carry
 
-    lax.fori_loop(0, CHANNELS, assemble, 0)
+    lax.fori_loop(0, CHANNELS, assemble, 0, unroll=4)
     sweep = Sweep(axes, rows, ext, fields, terms, works)
     for step in range(NB - 1):
         low = sweep.rows(step, step + 1, LOW + step, sweep.rate(step, step))
@@ -479,14 +479,17 @@
         odd = parts[len(parts) // 2 * 2 :]
         parts = [a + b for a, b in zip(parts[0::2], parts[1::2])] + odd
     total = parts[0]
-    total = jnp.sum(total, axis=0, keepdims=True)
+    total = jnp.broadcast_to(jnp.sum(total, axis=0, keepdims=True), (SUB, LANES))
     half = muscles // 2
-    works, dots = total[:, : NB * half], total[:, NB * half :]
+
+    def everywhere(lane):
+        return jnp.broadcast_to(total[:, lane : lane + 1], (SUB, LANES))
+
     pairs = [(i, j) for i in range(NB) for j in range(i, NB)]
     gram = {}
     for n, (i, j) in enumerate(pairs):
-        gram[i, j] = gram[j, i] = dots[:, n : n + 1]
-    energy = dots[:, len(pairs) : len(pairs) + 1]
+        gram[i, j] = gram[j, i] = everywhere(NB * half + n)
+    energy = everywhere(NB * half + len(pairs))
     shifts = [MASS + s for s in SHIFTS]
     form = {}
     for j in range(NB - 1):
@@ -514,16 +517,17 @@
         x[k] = value * inverse[k]
 
     for k in range(NB):
-        coef_ref[k] = jnp.broadcast_to(x[k], (SUB, LANES))
-    grad = None
+        coef_ref[k] = x[k]
+    lane = lax.broadcasted_iota(jnp.int32, (SUB, LANES), 1)
+    weight = jnp.zeros((SUB, LANES), jnp.float32)
     for k in range(NB):
-        piece = x[k] * works[:, k * half : (k + 1) * half]
-        grad = piece if grad is None else grad + piece
-    grad = -scale * grad
-    nothing = jnp.zeros_like(grad)
-    low = even(axes[0])
-    grad_ref[:, pl.ds(0, half)] = jnp.where(low, grad, nothing)
-    grad_ref[:, pl.ds(half, half)] = jnp.where(low, nothing, grad)
+        weight = jnp.where((lane >= k * half) & (lane < (k + 1) * half), x[k], weight)
+    grad = total * weight
+    grad = grad + pltpu.roll(grad, LANES - 2 * half, 1)
+    grad = -scale * (grad + pltpu.roll(grad, LANES - half, 1))
+    low = jnp.where(lane < half, grad, 0.0)
+    high = jnp.where((lane >= half) & (lane < 2 * half), pltpu.roll(grad, half, 1), 0.0)
+    grad_ref[...] = jnp.where(even(axes[0]), low, high)[:1, :muscles]
 
 
 def update_kernel(coef_ref, block_ref, fields, x_hbm, x_ref, sems):

time: 60.3 us -> 59.2 us (0.982)
  Pallas kernels: 12.4 us -> 11.2 us
    pallas_call x1, Pallas kernels: 1.15 us -> 0.34 us  [per_device(): pl.pallas_call(functools.partial(solve_kernel, axes, muscles, scale), out...]
where the time goes in v8:
time: 59.2 us; the launch traced here: 59 us
  blocking collectives  29.2 us (49%)
  starting transfers between devices  15.6 us (26%)
  Pallas kernels  11.2 us (19%)
  waiting for transfers between devices  1.7 us (3%)
  between operations  0.74 us (1%)
    all_to_all x1, blocking collectives, per_device(): every = lax.all_to_all(sums, ('gy', 'gz'), 0, 0, tiled=True)  29.2 us
    ppermute x7, starting transfers between devices, swap(): return lax.ppermute(shard, axis, pairs + [(j, i) for i, j in pairs])  15.6 us
    pallas_call x1, Pallas kernels, per_device(): pl.pallas_call(functools.partial(outer_kernel, axes, muscles, lax.axis_si...  5.4 us
    pallas_call x1, Pallas kernels, per_device(): pl.pallas_call(functools.partial(inner_kernel, axes, muscles), out_shape=...  3.26 us
    ppermute x7, waiting for transfers between devices, swap(): return lax.ppermute(shard, axis, pairs + [(j, i) for i, j in pairs])  1.7 us
    pallas_call x1, Pallas kernels, per_device(): pl.pallas_call(functools.partial(pack_kernel, axes), out_shape=(arr(CHANN...  1.4 us
  transfers between devices with their start and end apart: 7, of which 3 were waited for; matrix products, arithmetic and copies ran while one was open for 0% of the time, Pallas kernels for 7%

profile of v8, /device:TPU:1, one launch (start us, length us, event | category | flops | bytes accessed | tf_op | source)
XLA Modules:
  0.0 59.0 jit_solution(13043114810333619283)
XLA Ops:
  0.6 1.4 %pack.1 = (f32[8,8,8,256]{3,2,1,0:T(8,128)S(1)}, f32[8,8,4,256]{3,2,1,0:T(4,128)S(1)}, f32[8,8,4,256]{3,2,1,0:T(4,128)S(1)}, f32[8,4,8,256]{3,2,1,0:T(8,128)S(1)...) custom-call(f32[3,8,8,256]{3,2,1,0:T(8,128)} %disp_hbm.1, f32[3,8,8,256]{3,2,1,0:T(8,128)} %load_hbm.1, ...), custom_call_target="tpu_custom_call" | custom-call | tf_op jit(solution)/shard_map/pack/pallas_call | solution.py:568
  2.0 0.7 %collective-permute-start = (f32[8,8,4,256]{3,2,1,0:T(4,128)S(1)}, f32[8,8,4,256]{3,2,1,0:T(4,128)S(1)}, u32[]{:S(2)}, u32[]{:S(2)}) collective-permute-start(f32[8,8,4,256]{3,2,1,0:T(4,128)S(1)} %get-tuple-element.25), channel_id=1, source_target_pairs={{1,2},{3,4},{5,6},{7,8},{9,10},{11,12},{13,14},{2,1},{4,3},{6,5},{... | collective-permute-start | bytes 786440 | tf_op jit(solution)/shard_map/ppermute | solution.py:553
  2.7 4.6 %collective-permute-start.1 = (f32[8,8,4,256]{3,2,1,0:T(4,128)S(1)}, f32[8,8,4,256]{3,2,1,0:T(4,128)S(1)}, u32[]{:S(2)}, u32[]{:S(2)}) collective-permute-start(f32[8,8,4,256]{3,2,1,0:T(4,128)S(1)} %get-tuple-element.26), channel_id=1, source_target_pairs={{0,1},{2,3},{4,5},{6,7},{8,9},{10,11},{12,13},{14,15},{1,0},{3,2},... | collective-permute-start | bytes 786440 | tf_op jit(solution)/shard_map/ppermute | solution.py:553
  7.3 4.7 %collective-permute-start.2 = (f32[8,4,8,256]{3,2,1,0:T(8,128)S(1)}, f32[8,4,8,256]{3,2,1,0:T(8,128)S(1)}, u32[]{:S(2)}, u32[]{:S(2)}) collective-permute-start(f32[8,4,8,256]{3,2,1,0:T(8,128)S(1)} %get-tuple-element.31), channel_id=1, source_target_pairs={{16,32},{48,64},{80,96},{112,128},{144,160},{176,192},{208,224},{3... | collective-permute-start | bytes 786440 | tf_op jit(solution)/shard_map/ppermute | solution.py:553
  12.0 0.1 collective-permute-start.3
  12.1 0.0 collective-permute-done.znext_ref
  12.1 0.9 %collective-permute-done.1.zpair_ref = f32[8,8,4,256]{3,2,1,0:T(4,128)S(1)} collective-permute-done((f32[8,8,4,256]{3,2,1,0:T(4,128)S(1)}, f32[8,8,4,256]{3,2,1,0:T(4,128)S(1)}, u32[]{:S(2)}, u32[]{:S(2)}) %collective-permute-start.1) | collective-permute-done | bytes 262176 | tf_op jit(solution)/shard_map/ppermute | solution.py:553
  13.0 0.1 corner.1
  13.1 5.0 %collective-permute-start.4 = (f32[8,4,8,256]{3,2,1,0:T(8,128)S(1)}, f32[8,4,8,256]{3,2,1,0:T(8,128)S(1)}, u32[]{:S(2)}, u32[]{:S(2)}) collective-permute-start(f32[8,4,8,256]{3,2,1,0:T(8,128)S(1)} %get-tuple-element.33), channel_id=1, source_target_pairs={{16,32},{48,64},{80,96},{112,128},{144,160},{176,192},{208,224},{3... | collective-permute-start | bytes 786440 | tf_op jit(solution)/shard_map/ppermute | solution.py:553
  18.1 0.1 collective-permute-start.5
  18.2 3.3 %inner.1 = (f32[8,15,16,256]{3,2,1,0:T(8,128)S(1)}, f32[3,3,15,16,256]{4,3,2,1,0:T(8,128)S(1)}, f32[15,14,16,256]{3,2,1,0:T(8,128)S(1)}, f32[4,14,8,256]{3,2,1,0...) custom-call(f32[8,8,8,256]{3,2,1,0:T(8,128)S(1)} %get-tuple-element.24.block_ref, ...), custom_call_target="tpu_custom_call" | custom-call | tf_op jit(solution)/shard_map/inner/pallas_call | solution.py:619
  21.5 0.0 collective-permute-done.2.ynext_ref
  21.5 0.0 collective-permute-done.3.ypair_ref
  21.5 0.7 %collective-permute-done.4.cnext_ref = f32[8,4,8,256]{3,2,1,0:T(8,128)S(1)} collective-permute-done((f32[8,4,8,256]{3,2,1,0:T(8,128)S(1)}, f32[8,4,8,256]{3,2,1,0:T(8,128)S(1)}, u32[]{:S(2)}, u32[]{:S(2)}) %collective-permute-start.4) | collective-permute-done | bytes 262176 | tf_op jit(solution)/shard_map/ppermute | solution.py:553
  22.2 0.0 collective-permute-done.5.cpair_ref
  22.2 5.4 %outer.1 = (f32[256,128]{1,0:T(8,128)S(1)}, f32[8,15,16,256]{3,2,1,0:T(8,128)S(1)}, f32[3,3,15,16,256]{4,3,2,1,0:T(8,128)S(1)}, f32[15,14,16,256]{3,2,1,0:T(8,128)S(1)}, f32[4,14,8,256]{3,2,1,0:T(8,128)S(1)}) custom-call(s32[8,8,256]{2,1,0:T(8,128)S(1)} %get-tuple-element.23.group_ref, ...), custom_call_target="tpu_custom_call", output_to_operand_aliasing={{1}: (6, {}), {2}: (7, {}), {3}: (8, {}), {4}: (9, {})} | custom-call | tf_op jit(solution)/shard_map/outer/pallas_call | solution.py:629
  27.6 29.2 %all_to_all.11 = f32[256,1,128]{2,1,0:T(1,128)S(1)} all-to-all(f32[256,1,128]{2,1,0:T(1,128)S(1)} %bitcast.7), channel_id=1, replica_groups=mesh['gy'=16,'gz'=16] {'gy','gz'}, dimensions={0} | all-to-all | bytes 262144 | tf_op jit(solution)/shard_map/all_to_all | solution.py:640
  56.8 0.3 solve.1
  57.1 0.5 collective-permute-start.6
  57.7 0.7 %update.1 = f32[3,8,8,256]{3,2,1,0:T(8,128)} custom-call(f32[4,8,128]{2,1,0:T(8,128)S(1)} %get-tuple-element.41.coef_ref, f32[8,8,8,256]{3,2,1,0:T(8,128)S(1)} %get-tuple-element.24.block_ref, f32[3,3,15,16,256]{4,3,2,1,0:T(8,128)S(1)} %get-tuple-element.42.fields), custom_call_target="tpu_custom_call" | custom-call | tf_op jit(solution)/shard_map/update/pallas_call | solution.py:653
  58.4 0.1 collective-permute-done.6
  58.5 0.5 add_bitcast_fusion
Async XLA Ops:
  2.0 10.0 %collective-permute-start = (f32[8,8,4,256]{3,2,1,0:T(4,128)S(1)}, f32[8,8,4,256]{3,2,1,0:T(4,128)S(1)}, u32[]{:S(2)}, u32[]{:S(2)}) collective-permute-start(f32[8,8,4,256]{3,2,1,0:T(4,128)S(1)} %get-tuple-element.25), channel_id=1, source_target_pairs={{1,2},{3,4},{5,6},{7,8},{9,10},{11,12},{13,14},{2,1},{4,3},{6,5},{... | collective-permute-start | bytes 786440 | tf_op jit(solution)/shard_map/ppermute | solution.py:553
  2.7 10.3 %collective-permute-start.1 = (f32[8,8,4,256]{3,2,1,0:T(4,128)S(1)}, f32[8,8,4,256]{3,2,1,0:T(4,128)S(1)}, u32[]{:S(2)}, u32[]{:S(2)}) collective-permute-start(f32[8,8,4,256]{3,2,1,0:T(4,128)S(1)} %get-tuple-element.26), channel_id=1, source_target_pairs={{0,1},{2,3},{4,5},{6,7},{8,9},{10,11},{12,13},{14,15},{1,0},{3,2},... | collective-permute-start | bytes 786440 | tf_op jit(solution)/shard_map/ppermute | solution.py:553
  7.3 14.2 %collective-permute-start.2 = (f32[8,4,8,256]{3,2,1,0:T(8,128)S(1)}, f32[8,4,8,256]{3,2,1,0:T(8,128)S(1)}, u32[]{:S(2)}, u32[]{:S(2)}) collective-permute-start(f32[8,4,8,256]{3,2,1,0:T(8,128)S(1)} %get-tuple-element.31), channel_id=1, source_target_pairs={{16,32},{48,64},{80,96},{112,128},{144,160},{176,192},{208,224},{3... | collective-permute-start | bytes 786440 | tf_op jit(solution)/shard_map/ppermute | solution.py:553
  12.0 9.5 %collective-permute-start.3 = (f32[8,4,8,256]{3,2,1,0:T(8,128)S(1)}, f32[8,4,8,256]{3,2,1,0:T(8,128)S(1)}, u32[]{:S(2)}, u32[]{:S(2)}) collective-permute-start(f32[8,4,8,256]{3,2,1,0:T(8,128)S(1)} %get-tuple-element.32), channel_id=1, source_target_pairs={{0,16},{32,48},{64,80},{96,112},{128,144},{160,176},{192,208},{224... | collective-permute-start | bytes 786440 | tf_op jit(solution)/shard_map/ppermute | solution.py:553
  13.1 9.0 %collective-permute-start.4 = (f32[8,4,8,256]{3,2,1,0:T(8,128)S(1)}, f32[8,4,8,256]{3,2,1,0:T(8,128)S(1)}, u32[]{:S(2)}, u32[]{:S(2)}) collective-permute-start(f32[8,4,8,256]{3,2,1,0:T(8,128)S(1)} %get-tuple-element.33), channel_id=1, source_target_pairs={{16,32},{48,64},{80,96},{112,128},{144,160},{176,192},{208,224},{3... | collective-permute-start | bytes 786440 | tf_op jit(solution)/shard_map/ppermute | solution.py:553
  18.1 4.0 %collective-permute-start.5 = (f32[8,4,8,256]{3,2,1,0:T(8,128)S(1)}, f32[8,4,8,256]{3,2,1,0:T(8,128)S(1)}, u32[]{:S(2)}, u32[]{:S(2)}) collective-permute-start(f32[8,4,8,256]{3,2,1,0:T(8,128)S(1)} %get-tuple-element.34), channel_id=1, source_target_pairs={{0,16},{32,48},{64,80},{96,112},{128,144},{160,176},{192,208},{224... | collective-permute-start | bytes 786440 | tf_op jit(solution)/shard_map/ppermute | solution.py:553
  57.1 1.3 %collective-permute-start.6 = (f32[1,32]{1,0:T(1,128)S(1)}, f32[1,32]{1,0:T(1,128)S(1)}, u32[]{:S(2)}, u32[]{:S(2)}) collective-permute-start(f32[1,32]{1,0:T(1,128)S(1)} %get-tuple-element.43), channel_id=1, source_target_pairs={{0,16},{32,48},{64,80},{96,112},{128,144},{160,176},{192,208},{224... | collective-permute-start | bytes 392 | tf_op jit(solution)/shard_map/ppermute | solution.py:553

commit v9 on v8

--- a/solution.py
+++ b/solution.py
@@ -282,24 +282,26 @@
     rows, cols, depth = occ_ref.shape
     muscles = act_ref.shape[0]
     even_y, even_z = even(axes[0]), even(axes[1])
-    for copy in copies:
+    for copy in copies[:2]:
         copy.wait()
-
-    def row(y, carry):
+    for y in range(rows):
         group = group_ref[y]
         level = jnp.zeros((cols, depth), jnp.float32)
         for m in range(muscles):
             level = jnp.where(group == m, act_ref[m], level)
+        block_ref[CHANNELS - 1, y] = level
+    for copy in copies[2:]:
+        copy.wait()
+    for y in range(rows):
         values = [disp_ref[c, y] for c in range(3)] + [load_ref[c, y] for c in range(3)]
-        values += [occ_ref[y].astype(jnp.float32), level]
+        values.append(occ_ref[y].astype(jnp.float32))
         for c, value in enumerate(values):
             block_ref[c, y] = value
+        values.append(block_ref[CHANNELS - 1, y])
+        for c, value in enumerate(values):
             bottom, top = value[:HIGH], value[cols - HIGH :]
             zpair_ref[c, y] = jnp.where(even_z, top, bottom)
             znext_ref[c, y] = jnp.where(even_z, bottom, top)
-        return carry
-
-    lax.fori_loop(0, rows, row, 0, unroll=4)
     send_rows(block_ref, ypair_ref, ynext_ref, even_y)
 
 
@@ -351,7 +353,7 @@
             store(step, table_row(step, m, muscles), jnp.sum(total[step], axis=0, keepdims=True))
         return carry
 
-    lax.fori_loop(0, muscles, muscle, 0, unroll=8)
+    lax.fori_loop(0, muscles, muscle, 0, unroll=16)
 
 
 def inner_kernel(

time: 59.2 us -> 59 us (level)
  no operation moved by 1% of the time
where the time goes in v9:
time: 59 us; the launch traced here: 58.8 us
  blocking collectives  29.2 us (49%)
  starting transfers between devices  15.6 us (26%)
  Pallas kernels  11.1 us (19%)
  waiting for transfers between devices  1.71 us (3%)
  between operations  0.74 us (1%)
    all_to_all x1, blocking collectives, per_device(): every = lax.all_to_all(sums, ('gy', 'gz'), 0, 0, tiled=True)  29.2 us
    ppermute x7, starting transfers between devices, swap(): return lax.ppermute(shard, axis, pairs + [(j, i) for i, j in pairs])  15.6 us
    pallas_call x1, Pallas kernels, per_device(): pl.pallas_call(functools.partial(outer_kernel, axes, muscles, lax.axis_si...  5.38 us
    pallas_call x1, Pallas kernels, per_device(): pl.pallas_call(functools.partial(inner_kernel, axes, muscles), out_shape=...  3.24 us
    ppermute x7, waiting for transfers between devices, swap(): return lax.ppermute(shard, axis, pairs + [(j, i) for i, j in pairs])  1.71 us
    pallas_call x1, Pallas kernels, per_device(): pl.pallas_call(functools.partial(pack_kernel, axes), out_shape=(arr(CHANN...  1.26 us
  transfers between devices with their start and end apart: 7, of which 3 were waited for; matrix products, arithmetic and copies ran while one was open for 0% of the time, Pallas kernels for 7%

profile of v9, /device:TPU:1, one launch (start us, length us, event | category | flops | bytes accessed | tf_op | source)
XLA Modules:
  0.0 58.8 jit_solution(1672102232915805143)
XLA Ops:
  0.6 1.3 %pack.1 = (f32[8,8,8,256]{3,2,1,0:T(8,128)S(1)}, f32[8,8,4,256]{3,2,1,0:T(4,128)S(1)}, f32[8,8,4,256]{3,2,1,0:T(4,128)S(1)}, f32[8,4,8,256]{3,2,1,0:T(8,128)S(1)...) custom-call(f32[3,8,8,256]{3,2,1,0:T(8,128)} %disp_hbm.1, f32[3,8,8,256]{3,2,1,0:T(8,128)} %load_hbm.1, ...), custom_call_target="tpu_custom_call" | custom-call | tf_op jit(solution)/shard_map/pack/pallas_call | solution.py:570
  1.9 0.7 %collective-permute-start = (f32[8,8,4,256]{3,2,1,0:T(4,128)S(1)}, f32[8,8,4,256]{3,2,1,0:T(4,128)S(1)}, u32[]{:S(2)}, u32[]{:S(2)}) collective-permute-start(f32[8,8,4,256]{3,2,1,0:T(4,128)S(1)} %get-tuple-element.25), channel_id=1, source_target_pairs={{1,2},{3,4},{5,6},{7,8},{9,10},{11,12},{13,14},{2,1},{4,3},{6,5},{... | collective-permute-start | bytes 786440 | tf_op jit(solution)/shard_map/ppermute | solution.py:555
  2.6 4.6 %collective-permute-start.1 = (f32[8,8,4,256]{3,2,1,0:T(4,128)S(1)}, f32[8,8,4,256]{3,2,1,0:T(4,128)S(1)}, u32[]{:S(2)}, u32[]{:S(2)}) collective-permute-start(f32[8,8,4,256]{3,2,1,0:T(4,128)S(1)} %get-tuple-element.26), channel_id=1, source_target_pairs={{0,1},{2,3},{4,5},{6,7},{8,9},{10,11},{12,13},{14,15},{1,0},{3,2},... | collective-permute-start | bytes 786440 | tf_op jit(solution)/shard_map/ppermute | solution.py:555
  7.2 4.7 %collective-permute-start.2 = (f32[8,4,8,256]{3,2,1,0:T(8,128)S(1)}, f32[8,4,8,256]{3,2,1,0:T(8,128)S(1)}, u32[]{:S(2)}, u32[]{:S(2)}) collective-permute-start(f32[8,4,8,256]{3,2,1,0:T(8,128)S(1)} %get-tuple-element.31), channel_id=1, source_target_pairs={{16,32},{48,64},{80,96},{112,128},{144,160},{176,192},{208,224},{3... | collective-permute-start | bytes 786440 | tf_op jit(solution)/shard_map/ppermute | solution.py:555
  11.8 0.1 collective-permute-start.3
  11.9 0.0 collective-permute-done.znext_ref
  11.9 0.9 %collective-permute-done.1.zpair_ref = f32[8,8,4,256]{3,2,1,0:T(4,128)S(1)} collective-permute-done((f32[8,8,4,256]{3,2,1,0:T(4,128)S(1)}, f32[8,8,4,256]{3,2,1,0:T(4,128)S(1)}, u32[]{:S(2)}, u32[]{:S(2)}) %collective-permute-start.1) | collective-permute-done | bytes 262176 | tf_op jit(solution)/shard_map/ppermute | solution.py:555
  12.9 0.1 corner.1
  13.0 5.0 %collective-permute-start.4 = (f32[8,4,8,256]{3,2,1,0:T(8,128)S(1)}, f32[8,4,8,256]{3,2,1,0:T(8,128)S(1)}, u32[]{:S(2)}, u32[]{:S(2)}) collective-permute-start(f32[8,4,8,256]{3,2,1,0:T(8,128)S(1)} %get-tuple-element.33), channel_id=1, source_target_pairs={{16,32},{48,64},{80,96},{112,128},{144,160},{176,192},{208,224},{3... | collective-permute-start | bytes 786440 | tf_op jit(solution)/shard_map/ppermute | solution.py:555
  18.0 0.1 collective-permute-start.5
  18.1 3.2 %inner.1 = (f32[8,15,16,256]{3,2,1,0:T(8,128)S(1)}, f32[3,3,15,16,256]{4,3,2,1,0:T(8,128)S(1)}, f32[15,14,16,256]{3,2,1,0:T(8,128)S(1)}, f32[4,14,8,256]{3,2,1,0...) custom-call(f32[8,8,8,256]{3,2,1,0:T(8,128)S(1)} %get-tuple-element.24.block_ref, ...), custom_call_target="tpu_custom_call" | custom-call | tf_op jit(solution)/shard_map/inner/pallas_call | solution.py:621
  21.3 0.0 collective-permute-done.2.ynext_ref
  21.3 0.0 collective-permute-done.3.ypair_ref
  21.4 0.7 %collective-permute-done.4.cnext_ref = f32[8,4,8,256]{3,2,1,0:T(8,128)S(1)} collective-permute-done((f32[8,4,8,256]{3,2,1,0:T(8,128)S(1)}, f32[8,4,8,256]{3,2,1,0:T(8,128)S(1)}, u32[]{:S(2)}, u32[]{:S(2)}) %collective-permute-start.4) | collective-permute-done | bytes 262176 | tf_op jit(solution)/shard_map/ppermute | solution.py:555
  22.0 0.0 collective-permute-done.5.cpair_ref
  22.0 5.4 %outer.1 = (f32[256,128]{1,0:T(8,128)S(1)}, f32[8,15,16,256]{3,2,1,0:T(8,128)S(1)}, f32[3,3,15,16,256]{4,3,2,1,0:T(8,128)S(1)}, f32[15,14,16,256]{3,2,1,0:T(8,128)S(1)}, f32[4,14,8,256]{3,2,1,0:T(8,128)S(1)}) custom-call(s32[8,8,256]{2,1,0:T(8,128)S(1)} %get-tuple-element.23.group_ref, ...), custom_call_target="tpu_custom_call", output_to_operand_aliasing={{1}: (6, {}), {2}: (7, {}), {3}: (8, {}), {4}: (9, {})} | custom-call | tf_op jit(solution)/shard_map/outer/pallas_call | solution.py:631
  27.4 29.2 %all_to_all.11 = f32[256,1,128]{2,1,0:T(1,128)S(1)} all-to-all(f32[256,1,128]{2,1,0:T(1,128)S(1)} %bitcast.7), channel_id=1, replica_groups=mesh['gy'=16,'gz'=16] {'gy','gz'}, dimensions={0} | all-to-all | bytes 262144 | tf_op jit(solution)/shard_map/all_to_all | solution.py:642
  56.6 0.3 solve.1
  57.0 0.5 collective-permute-start.6
  57.5 0.7 %update.1 = f32[3,8,8,256]{3,2,1,0:T(8,128)} custom-call(f32[4,8,128]{2,1,0:T(8,128)S(1)} %get-tuple-element.41.coef_ref, f32[8,8,8,256]{3,2,1,0:T(8,128)S(1)} %get-tuple-element.24.block_ref, f32[3,3,15,16,256]{4,3,2,1,0:T(8,128)S(1)} %get-tuple-element.42.fields), custom_call_target="tpu_custom_call" | custom-call | tf_op jit(solution)/shard_map/update/pallas_call | solution.py:655
  58.2 0.1 collective-permute-done.6
  58.3 0.5 add_bitcast_fusion
Async XLA Ops:
  1.9 10.0 %collective-permute-start = (f32[8,8,4,256]{3,2,1,0:T(4,128)S(1)}, f32[8,8,4,256]{3,2,1,0:T(4,128)S(1)}, u32[]{:S(2)}, u32[]{:S(2)}) collective-permute-start(f32[8,8,4,256]{3,2,1,0:T(4,128)S(1)} %get-tuple-element.25), channel_id=1, source_target_pairs={{1,2},{3,4},{5,6},{7,8},{9,10},{11,12},{13,14},{2,1},{4,3},{6,5},{... | collective-permute-start | bytes 786440 | tf_op jit(solution)/shard_map/ppermute | solution.py:555
  2.6 10.3 %collective-permute-start.1 = (f32[8,8,4,256]{3,2,1,0:T(4,128)S(1)}, f32[8,8,4,256]{3,2,1,0:T(4,128)S(1)}, u32[]{:S(2)}, u32[]{:S(2)}) collective-permute-start(f32[8,8,4,256]{3,2,1,0:T(4,128)S(1)} %get-tuple-element.26), channel_id=1, source_target_pairs={{0,1},{2,3},{4,5},{6,7},{8,9},{10,11},{12,13},{14,15},{1,0},{3,2},... | collective-permute-start | bytes 786440 | tf_op jit(solution)/shard_map/ppermute | solution.py:555
  7.2 14.2 %collective-permute-start.2 = (f32[8,4,8,256]{3,2,1,0:T(8,128)S(1)}, f32[8,4,8,256]{3,2,1,0:T(8,128)S(1)}, u32[]{:S(2)}, u32[]{:S(2)}) collective-permute-start(f32[8,4,8,256]{3,2,1,0:T(8,128)S(1)} %get-tuple-element.31), channel_id=1, source_target_pairs={{16,32},{48,64},{80,96},{112,128},{144,160},{176,192},{208,224},{3... | collective-permute-start | bytes 786440 | tf_op jit(solution)/shard_map/ppermute | solution.py:555
  11.8 9.5 %collective-permute-start.3 = (f32[8,4,8,256]{3,2,1,0:T(8,128)S(1)}, f32[8,4,8,256]{3,2,1,0:T(8,128)S(1)}, u32[]{:S(2)}, u32[]{:S(2)}) collective-permute-start(f32[8,4,8,256]{3,2,1,0:T(8,128)S(1)} %get-tuple-element.32), channel_id=1, source_target_pairs={{0,16},{32,48},{64,80},{96,112},{128,144},{160,176},{192,208},{224... | collective-permute-start | bytes 786440 | tf_op jit(solution)/shard_map/ppermute | solution.py:555
  13.0 9.0 %collective-permute-start.4 = (f32[8,4,8,256]{3,2,1,0:T(8,128)S(1)}, f32[8,4,8,256]{3,2,1,0:T(8,128)S(1)}, u32[]{:S(2)}, u32[]{:S(2)}) collective-permute-start(f32[8,4,8,256]{3,2,1,0:T(8,128)S(1)} %get-tuple-element.33), channel_id=1, source_target_pairs={{16,32},{48,64},{80,96},{112,128},{144,160},{176,192},{208,224},{3... | collective-permute-start | bytes 786440 | tf_op jit(solution)/shard_map/ppermute | solution.py:555
  18.0 4.0 %collective-permute-start.5 = (f32[8,4,8,256]{3,2,1,0:T(8,128)S(1)}, f32[8,4,8,256]{3,2,1,0:T(8,128)S(1)}, u32[]{:S(2)}, u32[]{:S(2)}) collective-permute-start(f32[8,4,8,256]{3,2,1,0:T(8,128)S(1)} %get-tuple-element.34), channel_id=1, source_target_pairs={{0,16},{32,48},{64,80},{96,112},{128,144},{160,176},{192,208},{224... | collective-permute-start | bytes 786440 | tf_op jit(solution)/shard_map/ppermute | solution.py:555
  57.0 1.3 %collective-permute-start.6 = (f32[1,32]{1,0:T(1,128)S(1)}, f32[1,32]{1,0:T(1,128)S(1)}, u32[]{:S(2)}, u32[]{:S(2)}) collective-permute-start(f32[1,32]{1,0:T(1,128)S(1)} %get-tuple-element.43), channel_id=1, source_target_pairs={{0,16},{32,48},{64,80},{96,112},{128,144},{160,176},{192,208},{224... | collective-permute-start | bytes 392 | tf_op jit(solution)/shard_map/ppermute | solution.py:555

commit v10 on v9

--- a/solution.py
+++ b/solution.py
@@ -353,7 +353,7 @@
             store(step, table_row(step, m, muscles), jnp.sum(total[step], axis=0, keepdims=True))
         return carry
 
-    lax.fori_loop(0, muscles, muscle, 0, unroll=16)
+    lax.fori_loop(0, muscles, muscle, 0, unroll=32)
 
 
 def inner_kernel(
@@ -367,7 +367,7 @@
             ext[c, LOW + y, pl.ds(SUB, SUB), :] = around_ref[c, y]
         return carry
 
-    lax.fori_loop(0, CHANNELS, assemble, 0, unroll=4)
+    lax.fori_loop(0, CHANNELS, assemble, 0, unroll=8)
     sweep = Sweep(axes, rows, ext, fields, terms, works)
     for step in range(NB - 1):
         first, final = LOW + step, LOW + rows - 2 - step
@@ -417,7 +417,7 @@
                     ext[c, y - HIGH + LOW, pl.ds(SUB * zt, SUB), :] = jnp.where(even_y, far, pair)
         return carry
 
-    lax.fori_loop(0, CHANNELS, assemble, 0, unroll=4)
+    lax.fori_loop(0, CHANNELS, assemble, 0, unroll=8)
     sweep = Sweep(axes, rows, ext, fields, terms, works)
     for step in range(NB - 1):
         low = sweep.rows(step, step + 1, LOW + step, sweep.rate(step, step))

time: 59 us -> 58.6 us (level)
  no operation moved by 1% of the time
where the time goes in v10:
time: 58.6 us; the launch traced here: 58.4 us
  blocking collectives  29.2 us (50%)
  starting transfers between devices  15.6 us (27%)
  Pallas kernels  10.6 us (18%)
  waiting for transfers between devices  1.73 us (3%)
  between operations  0.74 us (1%)
    all_to_all x1, blocking collectives, per_device(): every = lax.all_to_all(sums, ('gy', 'gz'), 0, 0, tiled=True)  29.2 us
    ppermute x7, starting transfers between devices, swap(): return lax.ppermute(shard, axis, pairs + [(j, i) for i, j in pairs])  15.6 us
    pallas_call x1, Pallas kernels, per_device(): pl.pallas_call(functools.partial(outer_kernel, axes, muscles, lax.axis_si...  4.9 us
    pallas_call x1, Pallas kernels, per_device(): pl.pallas_call(functools.partial(inner_kernel, axes, muscles), out_shape=...  3.23 us
    ppermute x7, waiting for transfers between devices, swap(): return lax.ppermute(shard, axis, pairs + [(j, i) for i, j in pairs])  1.73 us
    pallas_call x1, Pallas kernels, per_device(): pl.pallas_call(functools.partial(pack_kernel, axes), out_shape=(arr(CHANN...  1.26 us
  transfers between devices with their start and end apart: 7, of which 3 were waited for; matrix products, arithmetic and copies ran while one was open for 0% of the time, Pallas kernels for 7%

profile of v10, /device:TPU:1, one launch (start us, length us, event | category | flops | bytes accessed | tf_op | source)
XLA Modules:
  0.0 58.4 jit_solution(17999163640758795049)
XLA Ops:
  0.6 1.3 %pack.1 = (f32[8,8,8,256]{3,2,1,0:T(8,128)S(1)}, f32[8,8,4,256]{3,2,1,0:T(4,128)S(1)}, f32[8,8,4,256]{3,2,1,0:T(4,128)S(1)}, f32[8,4,8,256]{3,2,1,0:T(8,128)S(1)...) custom-call(f32[3,8,8,256]{3,2,1,0:T(8,128)} %disp_hbm.1, f32[3,8,8,256]{3,2,1,0:T(8,128)} %load_hbm.1, ...), custom_call_target="tpu_custom_call" | custom-call | tf_op jit(solution)/shard_map/pack/pallas_call | solution.py:570
  1.9 0.7 %collective-permute-start = (f32[8,8,4,256]{3,2,1,0:T(4,128)S(1)}, f32[8,8,4,256]{3,2,1,0:T(4,128)S(1)}, u32[]{:S(2)}, u32[]{:S(2)}) collective-permute-start(f32[8,8,4,256]{3,2,1,0:T(4,128)S(1)} %get-tuple-element.25), channel_id=1, source_target_pairs={{1,2},{3,4},{5,6},{7,8},{9,10},{11,12},{13,14},{2,1},{4,3},{6,5},{... | collective-permute-start | bytes 786440 | tf_op jit(solution)/shard_map/ppermute | solution.py:555
  2.6 4.6 %collective-permute-start.1 = (f32[8,8,4,256]{3,2,1,0:T(4,128)S(1)}, f32[8,8,4,256]{3,2,1,0:T(4,128)S(1)}, u32[]{:S(2)}, u32[]{:S(2)}) collective-permute-start(f32[8,8,4,256]{3,2,1,0:T(4,128)S(1)} %get-tuple-element.26), channel_id=1, source_target_pairs={{0,1},{2,3},{4,5},{6,7},{8,9},{10,11},{12,13},{14,15},{1,0},{3,2},... | collective-permute-start | bytes 786440 | tf_op jit(solution)/shard_map/ppermute | solution.py:555
  7.2 4.7 %collective-permute-start.2 = (f32[8,4,8,256]{3,2,1,0:T(8,128)S(1)}, f32[8,4,8,256]{3,2,1,0:T(8,128)S(1)}, u32[]{:S(2)}, u32[]{:S(2)}) collective-permute-start(f32[8,4,8,256]{3,2,1,0:T(8,128)S(1)} %get-tuple-element.31), channel_id=1, source_target_pairs={{16,32},{48,64},{80,96},{112,128},{144,160},{176,192},{208,224},{3... | collective-permute-start | bytes 786440 | tf_op jit(solution)/shard_map/ppermute | solution.py:555
  11.8 0.1 collective-permute-start.3
  11.9 0.0 collective-permute-done.znext_ref
  11.9 0.9 %collective-permute-done.1.zpair_ref = f32[8,8,4,256]{3,2,1,0:T(4,128)S(1)} collective-permute-done((f32[8,8,4,256]{3,2,1,0:T(4,128)S(1)}, f32[8,8,4,256]{3,2,1,0:T(4,128)S(1)}, u32[]{:S(2)}, u32[]{:S(2)}) %collective-permute-start.1) | collective-permute-done | bytes 262176 | tf_op jit(solution)/shard_map/ppermute | solution.py:555
  12.9 0.1 corner.1
  13.0 5.0 %collective-permute-start.4 = (f32[8,4,8,256]{3,2,1,0:T(8,128)S(1)}, f32[8,4,8,256]{3,2,1,0:T(8,128)S(1)}, u32[]{:S(2)}, u32[]{:S(2)}) collective-permute-start(f32[8,4,8,256]{3,2,1,0:T(8,128)S(1)} %get-tuple-element.33), channel_id=1, source_target_pairs={{16,32},{48,64},{80,96},{112,128},{144,160},{176,192},{208,224},{3... | collective-permute-start | bytes 786440 | tf_op jit(solution)/shard_map/ppermute | solution.py:555
  18.0 0.1 collective-permute-start.5
  18.1 3.2 %inner.1 = (f32[8,15,16,256]{3,2,1,0:T(8,128)S(1)}, f32[3,3,15,16,256]{4,3,2,1,0:T(8,128)S(1)}, f32[15,14,16,256]{3,2,1,0:T(8,128)S(1)}, f32[4,14,8,256]{3,2,1,0...) custom-call(f32[8,8,8,256]{3,2,1,0:T(8,128)S(1)} %get-tuple-element.24.block_ref, ...), custom_call_target="tpu_custom_call" | custom-call | tf_op jit(solution)/shard_map/inner/pallas_call | solution.py:621
  21.3 0.0 collective-permute-done.2.ynext_ref
  21.3 0.0 collective-permute-done.3.ypair_ref
  21.3 0.7 %collective-permute-done.4.cnext_ref = f32[8,4,8,256]{3,2,1,0:T(8,128)S(1)} collective-permute-done((f32[8,4,8,256]{3,2,1,0:T(8,128)S(1)}, f32[8,4,8,256]{3,2,1,0:T(8,128)S(1)}, u32[]{:S(2)}, u32[]{:S(2)}) %collective-permute-start.4) | collective-permute-done | bytes 262176 | tf_op jit(solution)/shard_map/ppermute | solution.py:555
  22.0 0.0 collective-permute-done.5.cpair_ref
  22.0 4.9 %outer.1 = (f32[256,128]{1,0:T(8,128)S(1)}, f32[8,15,16,256]{3,2,1,0:T(8,128)S(1)}, f32[3,3,15,16,256]{4,3,2,1,0:T(8,128)S(1)}, f32[15,14,16,256]{3,2,1,0:T(8,128)S(1)}, f32[4,14,8,256]{3,2,1,0:T(8,128)S(1)}) custom-call(s32[8,8,256]{2,1,0:T(8,128)S(1)} %get-tuple-element.23.group_ref, ...), custom_call_target="tpu_custom_call", output_to_operand_aliasing={{1}: (6, {}), {2}: (7, {}), {3}: (8, {}), {4}: (9, {})} | custom-call | tf_op jit(solution)/shard_map/outer/pallas_call | solution.py:631
  26.9 29.2 %all_to_all.11 = f32[256,1,128]{2,1,0:T(1,128)S(1)} all-to-all(f32[256,1,128]{2,1,0:T(1,128)S(1)} %bitcast.7), channel_id=1, replica_groups=mesh['gy'=16,'gz'=16] {'gy','gz'}, dimensions={0} | all-to-all | bytes 262144 | tf_op jit(solution)/shard_map/all_to_all | solution.py:642
  56.2 0.3 solve.1
  56.5 0.5 collective-permute-start.6
  57.0 0.7 %update.1 = f32[3,8,8,256]{3,2,1,0:T(8,128)} custom-call(f32[4,8,128]{2,1,0:T(8,128)S(1)} %get-tuple-element.41.coef_ref, f32[8,8,8,256]{3,2,1,0:T(8,128)S(1)} %get-tuple-element.24.block_ref, f32[3,3,15,16,256]{4,3,2,1,0:T(8,128)S(1)} %get-tuple-element.42.fields), custom_call_target="tpu_custom_call" | custom-call | tf_op jit(solution)/shard_map/update/pallas_call | solution.py:655
  57.7 0.1 collective-permute-done.6
  57.8 0.5 add_bitcast_fusion
Async XLA Ops:
  1.9 10.0 %collective-permute-start = (f32[8,8,4,256]{3,2,1,0:T(4,128)S(1)}, f32[8,8,4,256]{3,2,1,0:T(4,128)S(1)}, u32[]{:S(2)}, u32[]{:S(2)}) collective-permute-start(f32[8,8,4,256]{3,2,1,0:T(4,128)S(1)} %get-tuple-element.25), channel_id=1, source_target_pairs={{1,2},{3,4},{5,6},{7,8},{9,10},{11,12},{13,14},{2,1},{4,3},{6,5},{... | collective-permute-start | bytes 786440 | tf_op jit(solution)/shard_map/ppermute | solution.py:555
  2.6 10.3 %collective-permute-start.1 = (f32[8,8,4,256]{3,2,1,0:T(4,128)S(1)}, f32[8,8,4,256]{3,2,1,0:T(4,128)S(1)}, u32[]{:S(2)}, u32[]{:S(2)}) collective-permute-start(f32[8,8,4,256]{3,2,1,0:T(4,128)S(1)} %get-tuple-element.26), channel_id=1, source_target_pairs={{0,1},{2,3},{4,5},{6,7},{8,9},{10,11},{12,13},{14,15},{1,0},{3,2},... | collective-permute-start | bytes 786440 | tf_op jit(solution)/shard_map/ppermute | solution.py:555
  7.2 14.2 %collective-permute-start.2 = (f32[8,4,8,256]{3,2,1,0:T(8,128)S(1)}, f32[8,4,8,256]{3,2,1,0:T(8,128)S(1)}, u32[]{:S(2)}, u32[]{:S(2)}) collective-permute-start(f32[8,4,8,256]{3,2,1,0:T(8,128)S(1)} %get-tuple-element.31), channel_id=1, source_target_pairs={{16,32},{48,64},{80,96},{112,128},{144,160},{176,192},{208,224},{3... | collective-permute-start | bytes 786440 | tf_op jit(solution)/shard_map/ppermute | solution.py:555
  11.8 9.5 %collective-permute-start.3 = (f32[8,4,8,256]{3,2,1,0:T(8,128)S(1)}, f32[8,4,8,256]{3,2,1,0:T(8,128)S(1)}, u32[]{:S(2)}, u32[]{:S(2)}) collective-permute-start(f32[8,4,8,256]{3,2,1,0:T(8,128)S(1)} %get-tuple-element.32), channel_id=1, source_target_pairs={{0,16},{32,48},{64,80},{96,112},{128,144},{160,176},{192,208},{224... | collective-permute-start | bytes 786440 | tf_op jit(solution)/shard_map/ppermute | solution.py:555
  13.0 9.0 %collective-permute-start.4 = (f32[8,4,8,256]{3,2,1,0:T(8,128)S(1)}, f32[8,4,8,256]{3,2,1,0:T(8,128)S(1)}, u32[]{:S(2)}, u32[]{:S(2)}) collective-permute-start(f32[8,4,8,256]{3,2,1,0:T(8,128)S(1)} %get-tuple-element.33), channel_id=1, source_target_pairs={{16,32},{48,64},{80,96},{112,128},{144,160},{176,192},{208,224},{3... | collective-permute-start | bytes 786440 | tf_op jit(solution)/shard_map/ppermute | solution.py:555
  18.0 4.0 %collective-permute-start.5 = (f32[8,4,8,256]{3,2,1,0:T(8,128)S(1)}, f32[8,4,8,256]{3,2,1,0:T(8,128)S(1)}, u32[]{:S(2)}, u32[]{:S(2)}) collective-permute-start(f32[8,4,8,256]{3,2,1,0:T(8,128)S(1)} %get-tuple-element.34), channel_id=1, source_target_pairs={{0,16},{32,48},{64,80},{96,112},{128,144},{160,176},{192,208},{224... | collective-permute-start | bytes 786440 | tf_op jit(solution)/shard_map/ppermute | solution.py:555
  56.5 1.3 %collective-permute-start.6 = (f32[1,32]{1,0:T(1,128)S(1)}, f32[1,32]{1,0:T(1,128)S(1)}, u32[]{:S(2)}, u32[]{:S(2)}) collective-permute-start(f32[1,32]{1,0:T(1,128)S(1)} %get-tuple-element.43), channel_id=1, source_target_pairs={{0,16},{32,48},{64,80},{96,112},{128,144},{160,176},{192,208},{224... | collective-permute-start | bytes 392 | tf_op jit(solution)/shard_map/ppermute | solution.py:555
